TPU v7x, 256 devices: a whole 4x4x8 slice. The times are simulated.
256 devices in a mesh: lat: 8 (over y_hi, x), lon: 32 (over z, y_lo, core).
Axes of the slice: x: 4, y: 4 (y_hi: 2, y_lo: 2; y = y_hi * 2 + y_lo), z: 8, core: 2. Of those that a mesh axis runs over, the one named last changes fastest.
Arguments:
- target: float32 [3, 512, 16384], P(None, 'lat', 'lon'), may hold values from -8 to 8
- latent_0: float32 [512, 16384], P('lat', 'lon'), may hold values from -10 to 10
- latent_1: float32 [256, 8192], P('lat', 'lon'), may hold values from -10 to 10
- latent_2: float32 [128, 4096], P('lat', 'lon'), may hold values from -10 to 10
- latent_3: float32 [64, 2048], P('lat', 'lon'), may hold values from -10 to 10
- latent_4: float32 [32, 1024], P('lat', 'lon'), may hold values from -10 to 10
- latent_5: float32 [16, 512], P('lat', 'lon'), may hold values from -10 to 10
- tile_seeds: int32 [8, 32], P('lat', 'lon'), may hold values from 0 to 1073741823
- anchor_parity: int32 [6], replicated, may hold values from 0 to 1
- anchor_scale: float32 [6], replicated, may hold values from 0.5 to 4
- mix_levels: bfloat16 [24, 6], replicated, may hold values from -2.5 to 2.5
- mix_hidden: bfloat16 [24, 24], replicated, may hold values from -1.25 to 1.25
- conv_first: bfloat16 [24, 24, 3, 3], replicated, may hold values from -0.4375 to 0.4375
- conv_second: bfloat16 [24, 24, 3, 3], replicated, may hold values from -0.4375 to 0.4375
- conv_output: bfloat16 [3, 24, 3, 3], replicated, may hold values from -0.4375 to 0.4375
- context_in: float32 [24, 12], replicated, may hold values from -1.75 to 1.75
- context_mid: float32 [24, 24], replicated, may hold values from -1.25 to 1.25
- context_out: float32 [2, 24], replicated, may hold values from -1.25 to 1.25
Outputs:
- reconstruction: float32 [3, 512, 16384], P(None, 'lat', 'lon')
- bits_finest: float32 [512, 16384], P('lat', 'lon')
- loss_terms: float32 [7], replicated
- output_grad: float32 [3, 24, 3, 3], replicated
All inputs are finite; a program needn't handle non-finite values.
Results may differ from a plain program's by a relative error of at most 0.00035.
The roundings to bfloat16 on the way count: a program that leaves them out, or rounds other values in their place, can miss the bound.
Values may be sent and summed in bfloat16 or wider, within the bound.
No kernel may reach another device: no remote copies, remote signals or barrier semaphores. Data moves between devices by JAX's collectives and lax.ppermute only.
A program may use at most 128 MiB of HBM per device.

v0:
```python
import jax
import jax.numpy as jnp
from jax import lax
from jax.sharding import PartitionSpec as P

mix_level = 668265263
mix_row = 374761393
mix_col = 1103515245
mix_mult = 73244475
log_two = 0.6931471805599453
context_steps = (
    (-1, 0),
    (1, 0),
    (0, -1),
    (0, 1),
    (-2, -1),
    (-2, 1),
    (2, -1),
    (2, 1),
    (-1, -2),
    (-1, 2),
    (1, -2),
    (1, 2),
)


def padded_2(shard, sides, width, wrap):
    for axis, dim in sides:
        size, length = (lax.axis_size(axis), shard.shape[dim])
        up = [(i, (i + 1) % size) for i in range(size if wrap else size - 1)]
        down = [(j, i) for i, j in up]
        last = lax.slice_in_dim(shard, length - width, length, axis=dim)
        first = lax.slice_in_dim(shard, 0, width, axis=dim)
        before = lax.ppermute(last, axis, up)
        after = lax.ppermute(first, axis, down)
        shard = jnp.concatenate([before, shard, after], axis=dim)
    return shard


def logical_shift(value, places):
    return jnp.bitwise_and(
        jnp.right_shift(value, jnp.int32(places)), jnp.int32((1 << 32 - places) - 1)
    )


def hashed_noise(seed_value, level_index, local_rows, local_cols):
    value = seed_value + jnp.int32(level_index) * jnp.int32(mix_level)
    value = (
        value + local_rows[:, None] * jnp.int32(mix_row) + local_cols[None, :] * jnp.int32(mix_col)
    )
    value = jnp.bitwise_xor(value, logical_shift(value, 15))
    value = value * jnp.int32(mix_mult)
    value = jnp.bitwise_xor(value, logical_shift(value, 13))
    value = value * jnp.int32(mix_mult)
    value = jnp.bitwise_xor(value, logical_shift(value, 16))
    return jnp.bitwise_and(value, jnp.int32(16777215)).astype(jnp.float32) / 16777216.0 - 0.5


def upsample_axis(extended, factor, along):
    cells_in = extended.shape[along] - 2
    earlier = lax.slice_in_dim(extended, 0, cells_in, axis=along)
    current = lax.slice_in_dim(extended, 1, cells_in + 1, axis=along)
    following = lax.slice_in_dim(extended, 2, cells_in + 2, axis=along)
    position = (jnp.arange(factor, dtype=jnp.float32) + 0.5) / factor - 0.5
    weight_low = jnp.maximum(-position, 0.0)
    weight_high = jnp.maximum(position, 0.0)
    weight_mid = 1.0 - weight_low - weight_high
    view_shape = [1] * (extended.ndim + 1)
    view_shape[along + 1] = factor
    result = jnp.expand_dims(earlier, along + 1) * weight_low.reshape(view_shape)
    result = result + jnp.expand_dims(current, along + 1) * weight_mid.reshape(view_shape)
    result = result + jnp.expand_dims(following, along + 1) * weight_high.reshape(view_shape)
    new_shape = list(extended.shape)
    new_shape[along] = cells_in * factor
    return result.reshape(new_shape)


def laplace_bits(offset, spread):
    magnitude = jnp.abs(offset)
    outer = (
        jnp.log(0.5)
        - (jnp.maximum(magnitude, 0.5) - 0.5) / spread
        + jnp.log(-jnp.expm1(-1.0 / spread))
    )
    inner_offset = jnp.clip(offset, -0.5, 0.5)
    inner = jnp.log(
        1.0
        - 0.5 * (jnp.exp(-(0.5 - inner_offset) / spread) + jnp.exp(-(0.5 + inner_offset) / spread))
    )
    return -jnp.where(magnitude >= 0.5, outer, inner) / log_two


def level_bits(
    extended, context_in, context_mid, context_out, anchor_value, parity_bit, row_start, col_start
):
    rows_in = extended.shape[0] - 4
    cols_in = extended.shape[1] - 4
    context = jnp.stack(
        [
            extended[2 + row_step : 2 + row_step + rows_in, 2 + col_step : 2 + col_step + cols_in]
            for row_step, col_step in context_steps
        ]
    )
    quantized = extended[2 : 2 + rows_in, 2 : 2 + cols_in]
    highest = lax.Precision.HIGHEST
    inner = jax.nn.relu(jnp.einsum("hk,kyx->hyx", context_in, context, precision=highest))
    outer = jax.nn.relu(jnp.einsum("hg,gyx->hyx", context_mid, inner, precision=highest))
    raw_out = jnp.einsum("oh,hyx->oyx", context_out, outer, precision=highest)
    row_ids = row_start + jnp.arange(rows_in, dtype=jnp.int32)
    col_ids = col_start + jnp.arange(cols_in, dtype=jnp.int32)
    anchor = (row_ids[:, None] + col_ids[None, :] + parity_bit) % 2 == 0
    centre = jnp.where(anchor, 0.0, raw_out[0])
    spread = jnp.where(anchor, anchor_value, 0.1 + jax.nn.softplus(raw_out[1]))
    return laplace_bits(quantized - centre, spread)


def conv_valid(field, kernel):
    return lax.conv_general_dilated(
        field[None],
        kernel,
        (1, 1),
        ((0, 0), (0, 0)),
        dimension_numbers=("NCHW", "OIHW", "NCHW"),
        preferred_element_type=jnp.float32,
    )[0]


def local(
    target,
    latent_0,
    latent_1,
    latent_2,
    latent_3,
    latent_4,
    latent_5,
    tile_seeds,
    anchor_parity,
    anchor_scale,
    mix_levels,
    mix_hidden,
    conv_first,
    conv_second,
    conv_output,
    context_in,
    context_mid,
    context_out,
):
    lat_count = lax.axis_size("lat")
    lon_count = lax.axis_size("lon")
    lat_index = lax.axis_index("lat")
    lon_index = lax.axis_index("lon")
    rows_dev = target.shape[1]
    cols_dev = target.shape[2]
    latents = (latent_0, latent_1, latent_2, latent_3, latent_4, latent_5)
    seed_value = tile_seeds[0, 0]
    noisy = []
    for level_index, latent in enumerate(latents):
        rows_here, cols_here = latent.shape
        noise = hashed_noise(
            seed_value,
            level_index,
            jnp.arange(rows_here, dtype=jnp.int32),
            jnp.arange(cols_here, dtype=jnp.int32),
        )
        noisy.append(latent + noise)
    level_count = len(noisy)
    halo_widths = [2] * level_count
    extended = []
    for field, width in zip(noisy, halo_widths):
        sideways = padded_2(field, (("lon", 1),), width, True)
        extended.append(padded_2(sideways, (("lat", 0),), width, False))
    bit_sums = []
    cell_counts = []
    bits_finest = None
    for level_index, field in enumerate(extended):
        rows_here, cols_here = noisy[level_index].shape
        bits = level_bits(
            field,
            context_in,
            context_mid,
            context_out,
            anchor_scale[level_index],
            anchor_parity[level_index],
            lat_index * rows_here,
            lon_index * cols_here,
        )
        if level_index == 0:
            bits_finest = bits
        bit_sums.append(jnp.sum(bits))
        cell_counts.append(float(rows_here * cols_here * lat_count * lon_count))
    rate_local = jnp.stack(bit_sums)
    up_layers = []
    for level_index, field in enumerate(extended):
        factor = 2**level_index
        up_layers.append(upsample_axis(upsample_axis(field[1:-1, 1:-1], factor, 0), factor, 1))
    upsampled = jnp.stack(up_layers).astype(jnp.bfloat16)
    first = jax.nn.relu(
        jnp.einsum("cl,lhw->chw", mix_levels, upsampled, preferred_element_type=jnp.float32)
    ).astype(jnp.bfloat16)
    second = jax.nn.relu(
        jnp.einsum("cd,dhw->chw", mix_hidden, first, preferred_element_type=jnp.float32)
    ).astype(jnp.bfloat16)

    def widen(field):
        sideways = padded_2(field, (("lon", 2),), 1, True)
        return padded_2(sideways, (("lat", 1),), 1, False)

    third = (second + jax.nn.relu(conv_valid(widen(second), conv_first))).astype(jnp.bfloat16)
    fourth = (third + jax.nn.relu(conv_valid(widen(third), conv_second))).astype(jnp.bfloat16)
    padded = widen(fourth)
    reconstruction = conv_valid(padded, conv_output)
    pixel_count = float(target.shape[0] * rows_dev * cols_dev * lat_count * lon_count)
    error = reconstruction - target
    squared_local = jnp.sum(error * error)
    slope = (2.0 * error / pixel_count).astype(jnp.bfloat16)
    taps = []
    for row_tap in range(3):
        for col_tap in range(3):
            window = padded[:, row_tap : row_tap + rows_dev, col_tap : col_tap + cols_dev]
            taps.append(
                jnp.einsum("ohw,chw->oc", slope, window, preferred_element_type=jnp.float32)
            )
    grad_local = jnp.stack(taps, axis=-1).reshape(target.shape[0], second.shape[0], 3, 3)
    rate_total, squared_total, grad_total = lax.psum(
        (rate_local, squared_local, grad_local), ("lat", "lon")
    )
    cells = jnp.array(cell_counts, dtype=jnp.float32)
    loss_terms = jnp.concatenate([squared_total[None] / pixel_count, rate_total / cells])
    return (reconstruction, bits_finest, loss_terms, grad_total)


def solution(mesh):
    return jax.shard_map(
        local,
        mesh=mesh,
        in_specs=(
            P(None, "lat", "lon"),
            P("lat", "lon"),
            P("lat", "lon"),
            P("lat", "lon"),
            P("lat", "lon"),
            P("lat", "lon"),
            P("lat", "lon"),
            P("lat", "lon"),
            P(),
            P(),
            P(),
            P(),
            P(),
            P(),
            P(),
            P(),
            P(),
            P(),
        ),
        out_specs=(P(None, "lat", "lon"), P("lat", "lon"), P(), P()),
        check_vma=False,
    )
```

profile of v0, /device:TPU:6, one launch (start us, length us, event | category | flops | bytes accessed | tf_op | source)
XLA Modules:
  0.0 673.7 jit_solution(6100900240050051850)
XLA Ops:
  2.3 6.4 collective-permute-start.21
  55.1 6.7 collective-permute-start.22
  78.1 7.5 %collective-permute-start.14 = (f32[2,68]{1,0:T(2,128)S(1)}, f32[2,68]{1,0:T(2,128)S(1)}, u32[]{:S(2)}, u32[]{:S(2)}) collective-permute-start(f32[2,68]{1,0:T(2,128)S(1)} %get-tuple-element.122), channel_id=1, source_target_pairs={{0,32},{32,64},{64,96},{96,128},{128,160},{160,192},{192,224},{1,3... | collective-permute-start | bytes 1640 | tf_op jit(solution)/shard_map/ppermute | solution.py:34
  89.9 7.5 %collective-permute-start.10 = (f32[2,132]{1,0:T(2,128)}, f32[2,132]{1,0:T(2,128)S(1)}, u32[]{:S(2)}, u32[]{:S(2)}) collective-permute-start(f32[2,132]{1,0:T(2,128)} %get-tuple-element.85), channel_id=1, source_target_pairs={{0,32},{32,64},{64,96},{96,128},{128,160},{160,192},{192,224},{1,3... | collective-permute-start | bytes 3176 | tf_op jit(solution)/shard_map/ppermute | solution.py:34
  103.3 7.5 %collective-permute-start.6 = (f32[2,260]{1,0:T(2,128)}, f32[2,260]{1,0:T(2,128)}, u32[]{:S(2)}, u32[]{:S(2)}) collective-permute-start(f32[2,260]{1,0:T(2,128)} %get-tuple-element.51), channel_id=1, source_target_pairs={{0,32},{32,64},{64,96},{96,128},{128,160},{160,192},{192,224},{1,3... | collective-permute-start | bytes 6248 | tf_op jit(solution)/shard_map/ppermute | solution.py:34
  114.1 7.5 %collective-permute-start.2 = (f32[2,516]{1,0:T(2,128)}, f32[2,516]{1,0:T(2,128)}, u32[]{:S(2)}, u32[]{:S(2)}) collective-permute-start(f32[2,516]{1,0:T(2,128)} %get-tuple-element.27), channel_id=1, source_target_pairs={{0,32},{32,64},{64,96},{96,128},{128,160},{160,192},{192,224},{1,3... | collective-permute-start | bytes 12392 | tf_op jit(solution)/shard_map/ppermute | solution.py:34
  158.0 7.5 %collective-permute-start.26 = (bf16[24,1,514]{2,0,1:T(8,128)(2,1)S(1)}, bf16[24,1,514]{2,0,1:T(8,128)(2,1)S(1)}, u32[]{:S(2)}, u32[]{:S(2)}) collective-permute-start(bf16[24,1,514]{2,0,1:T(8,128)(2,1)S(1)} %get-tuple-element.17), channel_id=1, source_target_pairs={{0,32},{32,64},{64,96},{96,128},{128,160},{160,192},{192,224},{1,3... | collective-permute-start | bytes 74024 | tf_op jit(solution)/shard_map/ppermute | solution.py:34
  165.6 12.6 %collective-permute-start.27 = (bf16[24,1,514]{2,0,1:T(8,128)(2,1)S(1)}, bf16[24,1,514]{2,0,1:T(8,128)(2,1)S(1)}, u32[]{:S(2)}, u32[]{:S(2)}) collective-permute-start(bf16[24,1,514]{2,0,1:T(8,128)(2,1)S(1)} %get-tuple-element.18), channel_id=1, source_target_pairs={{32,0},{64,32},{96,64},{128,96},{160,128},{192,160},{224,192},{33,... | collective-permute-start | bytes 74024 | tf_op jit(solution)/shard_map/ppermute | solution.py:35
  183.0 7.2 %stack.302 = f32[12,64,512]{2,0,1:T(8,128)} concatenate(f32[1,64,512]{2,0,1:T(1,128)S(1)} %copy.625, f32[1,64,512]{2,0,1:T(1,128)} %copy.626, f32[1,64,512]{2,0,1:T(1,128)S(1)} %copy.627, f32[1,64,512]{2,0,1:T(1,128)S(1)} %copy.628, f32[1,64,512]{2,0,1:T(1,128)} %copy.629, f32[1,64,512]{2,0,1:T(1,128)S(1)} %copy.630, f32[1,64,512]{2,0,1:T(1,128)} %copy.631, ...), dimensions={0} | concatenate | bytes 3145728 | tf_op jit(solution)/shard_map/stack | solution.py:98
  192.9 6.5 reshape.891
  199.3 10.8 %copy.616 = bf16[24,66,1,8,65]{0,3,4,1,2:T(8,128)(2,1)} copy(bf16[24,66,1,8,65]{4,3,0,1,2:T(8,128)(2,1)} %reshape.891) | data formatting | bytes 3294720 | tf_op jit(solution)/shard_map/conv_general_dilated | solution.py:118
  211.2 15.9 %select_maximum_fusion.1 = f32[64,8,65,24]{3,1,2,0:T(8,128)} fusion(bf16[24,24,3,3]{1,0,3,2:T(8,128)(2,1)S(1)} %copy-done, bf16[24,66,1,7,2]{0,3,4,1,2:T(8,128)(2,1)S(1)} %slice.857, bf16[24,66,1,8,65]{0,3,4,1,2:T(8,128)(2,1)} %copy.616, pred[8,65]{0,1:T(8,128)(4,1)S(1)} %copy-done.60), kind=kOutput, calls=%fused_computation.5 | convolution fusion | flops 351738624 | bytes 4897480 | tf_op jit(solution)/shard_map/conv_general_dilated | solution.py:118
  227.1 12.7 %copy.617 = f32[64,8,65,24]{2,1,3,0:T(8,128)} copy(f32[64,8,65,24]{3,1,2,0:T(8,128)} %select_maximum_fusion.1) | data formatting | bytes 6389760 | tf_op jit(solution)/shard_map/jit(relu)/max | solution.py:208
  239.8 7.1 %reshape.895 = f32[64,1,520,24]{2,3,0,1:T(8,128)} reshape(f32[64,8,65,24]{2,1,3,0:T(8,128)} %copy.617) | data formatting | bytes 6389760 | tf_op jit(solution)/shard_map/jit(relu)/max | solution.py:208
  259.2 7.5 %collective-permute-start.30 = (bf16[24,1,514]{2,0,1:T(8,128)(2,1)S(1)}, bf16[24,1,514]{2,0,1:T(8,128)(2,1)S(1)}, u32[]{:S(2)}, u32[]{:S(2)}) collective-permute-start(bf16[24,1,514]{2,0,1:T(8,128)(2,1)S(1)} %get-tuple-element.15), channel_id=1, source_target_pairs={{0,32},{32,64},{64,96},{96,128},{128,160},{160,192},{192,224},{1,3... | collective-permute-start | bytes 74024 | tf_op jit(solution)/shard_map/ppermute | solution.py:34
  278.8 6.5 reshape.898
  285.3 10.8 %copy.619 = bf16[24,66,1,8,65]{0,3,4,1,2:T(8,128)(2,1)} copy(bf16[24,66,1,8,65]{4,3,0,1,2:T(8,128)(2,1)} %reshape.898) | data formatting | bytes 3294720 | tf_op jit(solution)/shard_map/conv_general_dilated | solution.py:118
  297.2 15.9 %select_maximum_fusion = f32[64,8,65,24]{3,1,2,0:T(8,128)} fusion(bf16[24,24,3,3]{1,0,3,2:T(8,128)(2,1)S(1)} %copy-done.54, bf16[24,66,1,7,2]{0,3,4,1,2:T(8,128)(2,1)S(1)} %slice.861, bf16[24,66,1,8,65]{0,3,4,1,2:T(8,128)(2,1)} %copy.619, pred[8,65]{0,1:T(8,128)(4,1)S(1)} %copy-done.60), kind=kOutput, calls=%fused_computation.4 | convolution fusion | flops 351738624 | bytes 4897480 | tf_op jit(solution)/shard_map/conv_general_dilated | solution.py:118
  313.1 12.7 %copy.620 = f32[64,8,65,24]{2,1,3,0:T(8,128)} copy(f32[64,8,65,24]{3,1,2,0:T(8,128)} %select_maximum_fusion) | data formatting | bytes 6389760 | tf_op jit(solution)/shard_map/jit(relu)/max | solution.py:209
  325.7 7.1 %reshape.902 = f32[64,1,520,24]{2,3,0,1:T(8,128)} reshape(f32[64,8,65,24]{2,1,3,0:T(8,128)} %copy.620) | data formatting | bytes 6389760 | tf_op jit(solution)/shard_map/jit(relu)/max | solution.py:209
  363.0 6.4 reshape.905
  369.4 10.8 %copy.622 = bf16[24,66,1,8,65]{0,3,4,1,2:T(8,128)(2,1)} copy(bf16[24,66,1,8,65]{4,3,0,1,2:T(8,128)(2,1)} %reshape.905) | data formatting | bytes 3294720 | tf_op jit(solution)/shard_map/conv_general_dilated | solution.py:118
  381.3 190.5 %fusion.25 = f32[64,8,65,3]{1,3,2,0:T(4,128)} fusion(bf16[24,66,1,7,2]{0,3,4,1,2:T(8,128)(2,1)S(1)} %slice.865, bf16[24,66,1,8,65]{0,3,4,1,2:T(8,128)(2,1)} %copy.622, pred[8,65]{0,1:T(8,128)(4,1)S(1)} %copy-done.60, bf16[3,24,3,3]{1,3,2,0:T(4,128)(2,1)S(1)} %copy-done.55), kind=kOutput, calls=%fused_computation.25 | convolution fusion | flops 48324864 | bytes 2092888 | tf_op jit(solution)/shard_map/conv_general_dilated | solution.py:118
  593.4 78.7 %all-reduce = (f32[6]{0:T(128)S(1)}, f32[]{:T(128)}, f32[3,24,3,3]{1,3,2,0:T(4,128)}) all-reduce(f32[6]{0:T(128)S(1)} %stack.374, f32[]{:T(128)} %multiply_reduce_fusion, f32[3,24,3,3]{1,3,2,0:T(4,128)S(1)} %copy.706), channel_id=1, replica_groups=mesh['lat'=8,'lon'=32] {'lat','lon'}, use_global_device_ids=true, to_apply=%region_8.9 | all-reduce | flops 655 | bytes 5240 | tf_op jit(solution)/shard_map/psum | solution.py:224
  (540 shorter events, 198.7 us)
Async XLA Ops:
  2.2 37.0 %collective-permute-start.20 = (f32[2,2]{1,0:T(2,128)S(1)}, f32[2,2]{1,0:T(2,128)S(1)}, u32[]{:S(2)}, u32[]{:S(2)}) collective-permute-start(f32[2,2]{1,0:T(2,128)S(1)} %get-tuple-element.148), channel_id=1, source_target_pairs={{0,1},{1,2},{2,3},{3,4},{4,5},{5,6},{6,7},{7,8},{8,9},{9,10},{10,1... | collective-permute-start | bytes 56 | tf_op jit(solution)/shard_map/ppermute | solution.py:34
  2.3 40.8 %collective-permute-start.21 = (f32[2,2]{1,0:T(2,128)S(1)}, f32[2,2]{1,0:T(2,128)S(1)}, u32[]{:S(2)}, u32[]{:S(2)}) collective-permute-start(f32[2,2]{1,0:T(2,128)S(1)} %get-tuple-element.149), channel_id=1, source_target_pairs={{1,0},{2,1},{3,2},{4,3},{5,4},{6,5},{7,6},{8,7},{9,8},{10,9},{11,1... | collective-permute-start | bytes 56 | tf_op jit(solution)/shard_map/ppermute | solution.py:35
  9.5 34.4 %collective-permute-start.16 = (f32[4,2]{1,0:T(4,128)S(1)}, f32[4,2]{1,0:T(4,128)S(1)}, u32[]{:S(2)}, u32[]{:S(2)}) collective-permute-start(f32[4,2]{1,0:T(4,128)S(1)} %get-tuple-element.140), channel_id=1, source_target_pairs={{0,1},{1,2},{2,3},{3,4},{4,5},{5,6},{6,7},{7,8},{8,9},{9,10},{10,1... | collective-permute-start | bytes 104 | tf_op jit(solution)/shard_map/ppermute | solution.py:34
  9.5 38.2 %collective-permute-start.17 = (f32[4,2]{1,0:T(4,128)S(1)}, f32[4,2]{1,0:T(4,128)S(1)}, u32[]{:S(2)}, u32[]{:S(2)}) collective-permute-start(f32[4,2]{1,0:T(4,128)S(1)} %get-tuple-element.141), channel_id=1, source_target_pairs={{1,0},{2,1},{3,2},{4,3},{5,4},{6,5},{7,6},{8,7},{9,8},{10,9},{11,1... | collective-permute-start | bytes 104 | tf_op jit(solution)/shard_map/ppermute | solution.py:35
  14.2 33.9 %collective-permute-start.12 = (f32[8,2]{1,0:T(8,128)S(1)}, f32[8,2]{1,0:T(8,128)S(1)}, u32[]{:S(2)}, u32[]{:S(2)}) collective-permute-start(f32[8,2]{1,0:T(8,128)S(1)} %get-tuple-element.124), channel_id=1, source_target_pairs={{0,1},{1,2},{2,3},{3,4},{4,5},{5,6},{6,7},{7,8},{8,9},{9,10},{10,1... | collective-permute-start | bytes 200 | tf_op jit(solution)/shard_map/ppermute | solution.py:34
  39.2 12.7 %collective-permute-start.13 = (f32[8,2]{1,0:T(8,128)S(1)}, f32[8,2]{1,0:T(8,128)S(1)}, u32[]{:S(2)}, u32[]{:S(2)}) collective-permute-start(f32[8,2]{1,0:T(8,128)S(1)} %get-tuple-element.125), channel_id=1, source_target_pairs={{1,0},{2,1},{3,2},{4,3},{5,4},{6,5},{7,6},{8,7},{9,8},{10,9},{11,1... | collective-permute-start | bytes 200 | tf_op jit(solution)/shard_map/ppermute | solution.py:35
  47.7 28.4 %collective-permute-start.4 = (f32[32,2]{1,0:T(8,128)S(1)}, f32[32,2]{1,0:T(8,128)S(1)}, u32[]{:S(2)}, u32[]{:S(2)}) collective-permute-start(f32[32,2]{1,0:T(8,128)S(1)} %get-tuple-element.71), channel_id=1, source_target_pairs={{0,1},{1,2},{2,3},{3,4},{4,5},{5,6},{6,7},{7,8},{8,9},{9,10},{10,1... | collective-permute-start | bytes 776 | tf_op jit(solution)/shard_map/ppermute | solution.py:34
  48.1 30.0 %collective-permute-start.5 = (f32[32,2]{1,0:T(8,128)S(1)}, f32[32,2]{1,0:T(8,128)S(1)}, u32[]{:S(2)}, u32[]{:S(2)}) collective-permute-start(f32[32,2]{1,0:T(8,128)S(1)} %get-tuple-element.72), channel_id=1, source_target_pairs={{1,0},{2,1},{3,2},{4,3},{5,4},{6,5},{7,6},{8,7},{9,8},{10,9},{11,1... | collective-permute-start | bytes 776 | tf_op jit(solution)/shard_map/ppermute | solution.py:35
  52.0 49.4 %collective-permute-start = (f32[64,2]{1,0:T(8,128)S(1)}, f32[64,2]{1,0:T(8,128)S(1)}, u32[]{:S(2)}, u32[]{:S(2)}) collective-permute-start(f32[64,2]{1,0:T(8,128)S(1)} %get-tuple-element.41), channel_id=1, source_target_pairs={{0,1},{1,2},{2,3},{3,4},{4,5},{5,6},{6,7},{7,8},{8,9},{9,10},{10,1... | collective-permute-start | bytes 1544 | tf_op jit(solution)/shard_map/ppermute | solution.py:34
  63.4 40.0 %collective-permute-start.1 = (f32[64,2]{1,0:T(8,128)S(1)}, f32[64,2]{1,0:T(8,128)S(1)}, u32[]{:S(2)}, u32[]{:S(2)}) collective-permute-start(f32[64,2]{1,0:T(8,128)S(1)} %get-tuple-element.42), channel_id=1, source_target_pairs={{1,0},{2,1},{3,2},{4,3},{5,4},{6,5},{7,6},{8,7},{9,8},{10,9},{11,1... | collective-permute-start | bytes 1544 | tf_op jit(solution)/shard_map/ppermute | solution.py:35
  66.7 21.2 %collective-permute-start.18 = (f32[2,36]{1,0:T(2,128)S(1)}, f32[2,36]{1,0:T(2,128)S(1)}, u32[]{:S(2)}, u32[]{:S(2)}) collective-permute-start(f32[2,36]{1,0:T(2,128)S(1)} %get-tuple-element.138), channel_id=1, source_target_pairs={{0,32},{32,64},{64,96},{96,128},{128,160},{160,192},{192,224},{1,3... | collective-permute-start | bytes 872 | tf_op jit(solution)/shard_map/ppermute | solution.py:34
  76.1 13.8 %collective-permute-start.19 = (f32[2,36]{1,0:T(2,128)S(1)}, f32[2,36]{1,0:T(2,128)S(1)}, u32[]{:S(2)}, u32[]{:S(2)}) collective-permute-start(f32[2,36]{1,0:T(2,128)S(1)} %get-tuple-element.139), channel_id=1, source_target_pairs={{32,0},{64,32},{96,64},{128,96},{160,128},{192,160},{224,192},{33,... | collective-permute-start | bytes 872 | tf_op jit(solution)/shard_map/ppermute | solution.py:35
  78.1 34.1 %collective-permute-start.14 = (f32[2,68]{1,0:T(2,128)S(1)}, f32[2,68]{1,0:T(2,128)S(1)}, u32[]{:S(2)}, u32[]{:S(2)}) collective-permute-start(f32[2,68]{1,0:T(2,128)S(1)} %get-tuple-element.122), channel_id=1, source_target_pairs={{0,32},{32,64},{64,96},{96,128},{128,160},{160,192},{192,224},{1,3... | collective-permute-start | bytes 1640 | tf_op jit(solution)/shard_map/ppermute | solution.py:34
  88.0 26.1 %collective-permute-start.15 = (f32[2,68]{1,0:T(2,128)S(1)}, f32[2,68]{1,0:T(2,128)S(1)}, u32[]{:S(2)}, u32[]{:S(2)}) collective-permute-start(f32[2,68]{1,0:T(2,128)S(1)} %get-tuple-element.123), channel_id=1, source_target_pairs={{32,0},{64,32},{96,64},{128,96},{160,128},{192,160},{224,192},{33,... | collective-permute-start | bytes 1640 | tf_op jit(solution)/shard_map/ppermute | solution.py:35
  89.9 35.8 %collective-permute-start.10 = (f32[2,132]{1,0:T(2,128)}, f32[2,132]{1,0:T(2,128)S(1)}, u32[]{:S(2)}, u32[]{:S(2)}) collective-permute-start(f32[2,132]{1,0:T(2,128)} %get-tuple-element.85), channel_id=1, source_target_pairs={{0,32},{32,64},{64,96},{96,128},{128,160},{160,192},{192,224},{1,3... | collective-permute-start | bytes 3176 | tf_op jit(solution)/shard_map/ppermute | solution.py:34
  101.4 26.3 %collective-permute-start.11 = (f32[2,132]{1,0:T(2,128)}, f32[2,132]{1,0:T(2,128)S(1)}, u32[]{:S(2)}, u32[]{:S(2)}) collective-permute-start(f32[2,132]{1,0:T(2,128)} %get-tuple-element.86), channel_id=1, source_target_pairs={{32,0},{64,32},{96,64},{128,96},{160,128},{192,160},{224,192},{33,... | collective-permute-start | bytes 3176 | tf_op jit(solution)/shard_map/ppermute | solution.py:35
  103.3 29.7 %collective-permute-start.6 = (f32[2,260]{1,0:T(2,128)}, f32[2,260]{1,0:T(2,128)}, u32[]{:S(2)}, u32[]{:S(2)}) collective-permute-start(f32[2,260]{1,0:T(2,128)} %get-tuple-element.51), channel_id=1, source_target_pairs={{0,32},{32,64},{64,96},{96,128},{128,160},{160,192},{192,224},{1,3... | collective-permute-start | bytes 6248 | tf_op jit(solution)/shard_map/ppermute | solution.py:34
  112.2 20.9 %collective-permute-start.7 = (f32[2,260]{1,0:T(2,128)}, f32[2,260]{1,0:T(2,128)S(1)}, u32[]{:S(2)}, u32[]{:S(2)}) collective-permute-start(f32[2,260]{1,0:T(2,128)} %get-tuple-element.52), channel_id=1, source_target_pairs={{32,0},{64,32},{96,64},{128,96},{160,128},{192,160},{224,192},{33,... | collective-permute-start | bytes 6248 | tf_op jit(solution)/shard_map/ppermute | solution.py:35
  114.1 26.9 %collective-permute-start.2 = (f32[2,516]{1,0:T(2,128)}, f32[2,516]{1,0:T(2,128)}, u32[]{:S(2)}, u32[]{:S(2)}) collective-permute-start(f32[2,516]{1,0:T(2,128)} %get-tuple-element.27), channel_id=1, source_target_pairs={{0,32},{32,64},{64,96},{96,128},{128,160},{160,192},{192,224},{1,3... | collective-permute-start | bytes 12392 | tf_op jit(solution)/shard_map/ppermute | solution.py:34
  125.8 15.3 %collective-permute-start.3 = (f32[2,516]{1,0:T(2,128)}, f32[2,516]{1,0:T(2,128)}, u32[]{:S(2)}, u32[]{:S(2)}) collective-permute-start(f32[2,516]{1,0:T(2,128)} %get-tuple-element.28), channel_id=1, source_target_pairs={{32,0},{64,32},{96,64},{128,96},{160,128},{192,160},{224,192},{33,... | collective-permute-start | bytes 12392 | tf_op jit(solution)/shard_map/ppermute | solution.py:35
  158.0 32.1 %collective-permute-start.26 = (bf16[24,1,514]{2,0,1:T(8,128)(2,1)S(1)}, bf16[24,1,514]{2,0,1:T(8,128)(2,1)S(1)}, u32[]{:S(2)}, u32[]{:S(2)}) collective-permute-start(bf16[24,1,514]{2,0,1:T(8,128)(2,1)S(1)} %get-tuple-element.17), channel_id=1, source_target_pairs={{0,32},{32,64},{64,96},{96,128},{128,160},{160,192},{192,224},{1,3... | collective-permute-start | bytes 74024 | tf_op jit(solution)/shard_map/ppermute | solution.py:34
  165.6 24.6 %collective-permute-start.27 = (bf16[24,1,514]{2,0,1:T(8,128)(2,1)S(1)}, bf16[24,1,514]{2,0,1:T(8,128)(2,1)S(1)}, u32[]{:S(2)}, u32[]{:S(2)}) collective-permute-start(bf16[24,1,514]{2,0,1:T(8,128)(2,1)S(1)} %get-tuple-element.18), channel_id=1, source_target_pairs={{32,0},{64,32},{96,64},{128,96},{160,128},{192,160},{224,192},{33,... | collective-permute-start | bytes 74024 | tf_op jit(solution)/shard_map/ppermute | solution.py:35
  259.2 14.7 %collective-permute-start.30 = (bf16[24,1,514]{2,0,1:T(8,128)(2,1)S(1)}, bf16[24,1,514]{2,0,1:T(8,128)(2,1)S(1)}, u32[]{:S(2)}, u32[]{:S(2)}) collective-permute-start(bf16[24,1,514]{2,0,1:T(8,128)(2,1)S(1)} %get-tuple-element.15), channel_id=1, source_target_pairs={{0,32},{32,64},{64,96},{96,128},{128,160},{160,192},{192,224},{1,3... | collective-permute-start | bytes 74024 | tf_op jit(solution)/shard_map/ppermute | solution.py:34
  345.5 14.2 %collective-permute-start.34 = (bf16[24,1,514]{2,0,1:T(8,128)(2,1)S(1)}, bf16[24,1,514]{2,0,1:T(8,128)(2,1)S(1)}, u32[]{:S(2)}, u32[]{:S(2)}) collective-permute-start(bf16[24,1,514]{2,0,1:T(8,128)(2,1)S(1)} %get-tuple-element.13), channel_id=1, source_target_pairs={{0,32},{32,64},{64,96},{96,128},{128,160},{160,192},{192,224},{1,3... | collective-permute-start | bytes 74024 | tf_op jit(solution)/shard_map/ppermute | solution.py:34
  (74 other events, 1520.6 us)
where the time goes:
time: 686 us; the launch traced here: 674 us
  matrix products  247 us (36%)
  local copies, waits for them, and re-layouts  153 us (22%)
  starting transfers between devices  128 us (19%)
  blocking collectives  78.7 us (11%)
  other arithmetic  48.3 us (7%)
  waiting for transfers between devices  14 us (2%)
    conv_general_dilated x3, matrix products, conv_valid(): lax.conv_general_dilated(field[None], kernel, (1, 1), ((0, 0), (0, 0)), d...  222 us
    psum x1, blocking collectives, local(): lax.psum((rate_local, squared_local, grad_local), ('lat', 'lon'))  78.7 us
    ppermute x18, starting transfers between devices, padded_2(): after = lax.ppermute(first, axis, down)  65.7 us
    ppermute x18, starting transfers between devices, padded_2(): before = lax.ppermute(last, axis, up)  62.4 us
    conv_general_dilated x11, local copies, waits for them, and re-layouts, conv_valid(): lax.conv_general_dilated(field[None], kernel, (1, 1), ((0, 0), (0, 0)), d...  62 us
    max x2, local copies, waits for them, and re-layouts, local(): jax.nn.relu(conv_valid(widen(second), conv_first))  19.8 us
    max x2, local copies, waits for them, and re-layouts, local(): jax.nn.relu(conv_valid(widen(third), conv_second))  19.8 us
    another operation x48, local copies, waits for them, and re-layouts, level_bits(): jnp.stack([extended[2 + row_step:2 + row_step + rows_in, 2 + col_step:2 +...  17.1 us
  transfers between devices with their start and end apart: 36, of which 5 were waited for; matrix products, arithmetic and copies ran while one was open for 13% of the time, Pallas kernels for 0%

commit v1 on v0

v1 whole, which is shorter than its diff:
```python
import functools

import jax
import jax.numpy as jnp
import numpy as np
from jax import lax
from jax.experimental import pallas as pl
from jax.experimental.pallas import tpu as pltpu
from jax.sharding import PartitionSpec as P

F32, BF16, I32 = jnp.float32, jnp.bfloat16, jnp.int32
STEPS = (
    (-1, 0), (1, 0), (0, -1), (0, 1), (-2, -1), (-2, 1),
    (2, -1), (2, 1), (-1, -2), (-1, 2), (1, -2), (1, 2),
)
LEVELS, CH, H, W = 6, 24, 64, 512
ROWS = [H >> l for l in range(LEVELS)]
COLS = [W >> l for l in range(LEVELS)]
HALO = [3, 2, 2, 2, 2, 2]
OFFS = [0, 3, 5, 7, 9, 11]
PACK = 13
WIDE = [640, 384, 256, 128, 128, 128]
TALL = [80, 48, 32, 32, 32, 32]
TOP = 12
LANES = 640
BLOCKS = 9
BLOCK = 8 * CH
SLAB = 256
EDGE = 32
PLACE = [(0, 0), (3, 0), (3, 384), (5, 0), (5, 128), (5, 256)]
VMEM = pl.BlockSpec(memory_space=pltpu.VMEM)
SMEM = pl.BlockSpec(memory_space=pltpu.SMEM)


def dot(a, b):
    return lax.dot_general(a, b, (((1,), (0,)), ((), ())), preferred_element_type=F32)


def wrap32(v):
    return int(np.int64(v).astype(np.int32))


def quantize(lat_ref, seed, level):
    shape = lat_ref.shape
    rows = lax.broadcasted_iota(I32, shape, 0)
    cols = lax.broadcasted_iota(I32, shape, 1)
    h = (seed + wrap32(level * 668265263)) + rows * 374761393 + cols * 1103515245
    h = h ^ lax.shift_right_logical(h, jnp.full(shape, 15, I32))
    h = h * 73244475
    h = h ^ lax.shift_right_logical(h, jnp.full(shape, 13, I32))
    h = h * 73244475
    h = h ^ lax.shift_right_logical(h, jnp.full(shape, 16, I32))
    noise = (h & 16777215).astype(F32) * (1.0 / 16777216.0) - 0.5
    return lat_ref[...] + noise


def place_own(lats, seed, fields):
    for level in range(LEVELS):
        fields[level][...] = jnp.zeros(fields[level].shape, F32)
        fields[level][TOP : TOP + ROWS[level], 0 : COLS[level]] = quantize(
            lats[level], seed, level
        )


def place_sides(left, right, fields):
    lane = lax.broadcasted_iota(I32, (8, 128), 1)
    for level in range(LEVELS):
        h, c = HALO[level], COLS[level]
        start = c % 128
        base = (c // 128) * 128
        for g in range(max(1, ROWS[level] // 8)):
            at = PACK * g + OFFS[level]
            a = pltpu.roll(right, (start - at) % 128, 1)
            b = pltpu.roll(left, (128 - h - at) % 128, 1)
            tile = jnp.where((lane >= start) & (lane < start + h), a, 0.0)
            tile = jnp.where(lane >= 128 - h, b, tile)
            rows = pl.ds(TOP + 8 * g, 8)
            if level < 3:
                fields[level][rows, base : base + 128] = tile
            else:
                fields[level][rows, 0:128] = fields[level][rows, 0:128] + tile


def place_ends(above, below, fields):
    for level in range(LEVELS):
        h, (r, c), w = HALO[level], PLACE[level], WIDE[level]
        fields[level][TOP - h : TOP, :] = above[r : r + h, c : c + w]
        end = TOP + ROWS[level]
        fields[level][end : end + h, :] = below[r : r + h, c : c + w]


def sides_kernel(seed, *refs):
    lats, (to_right, to_left), fields = refs[:6], refs[6:8], refs[8:]
    place_own(lats, seed[0, 0], fields)
    lane = lax.broadcasted_iota(I32, (8, 128), 1)
    right = jnp.zeros((8, 128), F32)
    left = jnp.zeros((8, 128), F32)
    for level in range(LEVELS):
        h, c = HALO[level], COLS[level]
        base = max(c - 128, 0)
        for g in range(max(1, ROWS[level] // 8)):
            at = PACK * g + OFFS[level]
            here = (lane >= at) & (lane < at + h)
            rows = pl.ds(TOP + 8 * g, 8)
            last = fields[level][rows, base : base + 128]
            first = fields[level][rows, 0:128]
            right = jnp.where(here, pltpu.roll(last, (at - (c - h - base)) % 128, 1), right)
            left = jnp.where(here, pltpu.roll(first, at % 128, 1), left)
    to_right[...] = right
    to_left[...] = left


def ends_kernel(seed, *refs):
    lats, (left, right), (up, down), fields = refs[:6], refs[6:8], refs[8:10], refs[10:]
    place_own(lats, seed[0, 0], fields)
    place_sides(left[...], right[...], fields)
    up[...] = jnp.zeros(up.shape, F32)
    down[...] = jnp.zeros(down.shape, F32)
    for level in range(LEVELS):
        h, (r, c), w = HALO[level], PLACE[level], WIDE[level]
        end = TOP + ROWS[level]
        up[r : r + h, c : c + w] = fields[level][TOP : TOP + h, :]
        down[r : r + h, c : c + w] = fields[level][end - h : end, :]


def slab_row(d, c):
    return CH * d + EDGE + c


@functools.lru_cache(None)
def tables():
    t = {}
    spread = np.zeros((BLOCK, CH), np.float32)
    for r in range(8):
        for c in range(CH):
            spread[CH * r + c, c] = 1
    t["spread"] = spread
    t["gather"] = np.ascontiguousarray(spread.T)
    place = np.zeros((CH, SLAB), np.float32)
    tap = np.full((BLOCK, SLAB), 9, np.float32)
    for d in range(-1, 9):
        for c in range(CH):
            place[c, slab_row(d, c)] = 1
            for r in range(8):
                tap[CH * r : CH * r + CH, slab_row(d, c)] = d - r + 1
    t["place"], t["tap"] = place, tap
    t["tap_out"] = np.tile(tap[::CH], (3, 1))
    same = np.zeros((BLOCK, BLOCK), np.float32)
    for r in range(8):
        same[CH * r : CH * r + CH, CH * r : CH * r + CH] = 1
    t["same"] = same
    t["same_out"] = np.tile(same[::CH], (2, 1))
    levels = np.zeros((LEVELS, 8 * LEVELS), np.float32)
    rowof = np.zeros((BLOCK, 8 * LEVELS), np.float32)
    for l in range(LEVELS):
        for r in range(8):
            levels[l, 8 * l + r] = 1
            rowof[CH * r : CH * r + CH, 8 * l + r] = 1
    t["levels"], t["rowof"] = levels, rowof
    ctx = np.zeros((8, len(STEPS), 80), np.float32)
    for r in range(8):
        for k, (i, j) in enumerate(STEPS):
            ctx[r, k, (j + 2) * 16 + (r + i + 4)] = 1
    t["ctx"] = ctx
    for l in range(1, LEVELS):
        s = 1 << l
        up_r = np.zeros((80, TALL[l]), np.float32)
        for n in range(72):
            y = n - 4
            m, p = y >> l, ((y & (s - 1)) + 0.5) / s - 0.5
            for e, wgt in ((-1, max(-p, 0)), (0, 1 - abs(p)), (1, max(p, 0))):
                at = TOP + m + e
                if 0 <= at < TALL[l]:
                    up_r[n, at] += wgt
        up_c = np.zeros((WIDE[l], LANES), np.float32)
        for n in range(LANES):
            x = n if n < W + 4 else n - LANES
            if x < -4:
                continue
            m, p = x >> l, ((x & (s - 1)) + 0.5) / s - 0.5
            for e, wgt in ((-1, max(-p, 0)), (0, 1 - abs(p)), (1, max(p, 0))):
                q = m + e
                if -HALO[l] <= q < COLS[l] + HALO[l]:
                    up_c[q % WIDE[l], n] += wgt
        t[f"rows{l}"] = np.concatenate([up_r] * 3, axis=1)
        t[f"cols{l}"] = up_c
    return t


def table(name, dtype=BF16):
    return jnp.asarray(tables()[name], dtype)


def split2(x):
    hi = x.astype(BF16)
    return hi, (x - hi.astype(F32)).astype(BF16)


def split3(x):
    hi = x.astype(BF16)
    rest = x - hi.astype(F32)
    mid = rest.astype(BF16)
    return hi, mid, (rest - mid.astype(F32)).astype(BF16)


def weights_kernel(
    ml, mh, cf, cs, co, w1, w2, w3, spread, gather, place, tap, tap_out, same, same_out,
    levels, rowof, ctx, wm1, wm2, wc1, wc2, wout, a1, a2, a3,
):
    grow = spread[...]
    wide = gather[...]

    def diag(w):
        return dot(dot(grow, w).astype(BF16), wide) * same[...].astype(F32)

    wm1[...] = (
        dot(dot(grow, ml[...]).astype(BF16), levels[...]) * rowof[...].astype(F32)
    ).astype(BF16)
    wm2[...] = diag(mh[...]).astype(BF16)
    taps = tap[...].astype(F32)
    for src, dst in ((cf, wc1), (cs, wc2)):
        for b in range(3):
            total = jnp.zeros((BLOCK, SLAB), F32)
            for a in range(3):
                full = dot(dot(grow, src[a, b]).astype(BF16), place[...])
                total = jnp.where(taps == float(a), full, total)
            dst[BLOCK * b : BLOCK * b + BLOCK, :] = total.astype(BF16)
    rows = dot(co[...], place[...])
    taps3 = tap_out[...].astype(F32)[0:8]
    for b in range(3):
        for o in range(3):
            total = jnp.zeros((8, SLAB), F32)
            for a in range(3):
                k = 9 * o + 3 * a + b
                total = jnp.where(
                    taps3 == float(a), jnp.broadcast_to(rows[k : k + 1], (8, SLAB)), total
                )
            at = 24 * b + 8 * o
            wout[at : at + 8, :] = total
    hi, lo = split2(w1[...])
    for r in range(8):
        sel = ctx[r]
        h, l = dot(hi, sel).astype(BF16), dot(lo, sel).astype(BF16)
        a1[CH * r : CH * r + CH, :] = jnp.concatenate([h, h, l], axis=1)
    hi, lo = split2(w2[...])
    h, l = diag(hi).astype(BF16), diag(lo).astype(BF16)
    a2[...] = jnp.concatenate([h, h, l], axis=1)
    hi, lo = split2(w3[...])
    keep = same_out[...].astype(F32)

    def out(w):
        v = dot(w, wide)
        v = jnp.concatenate(
            [jnp.broadcast_to(v[0:1], (8, BLOCK)), jnp.broadcast_to(v[1:2], (8, BLOCK))], axis=0
        )
        return (v * keep).astype(BF16)

    h, l = out(hi), out(lo)
    a3[...] = jnp.concatenate([h, h, l], axis=1)


def laplace(x, centre, spread):
    y = 1.0 / spread
    off = x - centre
    mag = jnp.abs(off)
    inside = jnp.clip(off, -0.5, 0.5)
    e1 = jnp.exp((inside - 0.5) * y)
    e2 = jnp.exp((-0.5 - inside) * y)
    poly = y * (1 - y * (1 / 2 - y * (1 / 6 - y * (1 / 24 - y * (1 / 120)))))
    tail = jnp.where(y < 0.05, poly, 1.0 - e1 * e2)
    beyond = mag >= 0.5
    arg = jnp.where(beyond, 0.5 * tail, 1.0 - 0.5 * (e1 + e2))
    extra = jnp.where(beyond, (mag - 0.5) * y, 0.0)
    return (extra - jnp.log(arg)) * (1.0 / 0.6931471805599453)


def main_kernel(
    seed, parity, scale, ends, l0, l1, l2, l3, l4, l5, left, right, above, below, target,
    wm1, wm2, wc1, wc2, wout, a1, a2, a3, r1, r2, r3, r4, r5, u1, u2, u3, u4, u5,
    recon, bits, part,
    f0, f1, f2, f3, f4, f5, up, second, third, fourth, grad, sq, rate,
    *, pixels,
):
    fields = (f0, f1, f2, f3, f4, f5)
    place_own((l0, l1, l2, l3, l4, l5), seed[0, 0], fields)
    place_sides(left[...], right[...], fields)
    place_ends(above, below, fields)

    for n in range(BLOCKS):
        up[48 * n : 48 * n + 8, :] = f0[8 + 8 * n : 16 + 8 * n, :]
    for level, ru, cu in ((1, r1, u1), (2, r2, u2), (3, r3, u3), (4, r4, u4), (5, r5, u5)):
        grown = dot(ru[...], jnp.concatenate(split3(fields[level][...]), axis=0))
        full = dot(jnp.concatenate(split3(grown), axis=0), cu[...])
        full = (full[0:80] + full[80:160]) + full[160:240]
        for n in range(BLOCKS):
            up[48 * n + 8 * level : 48 * n + 8 * level + 8, :] = full[8 * n : 8 * n + 8]

    end = EDGE + BLOCK * BLOCKS
    for buf in (second, third, fourth):
        buf[0:EDGE, :] = jnp.zeros((EDGE, LANES), BF16)
        buf[end : end + EDGE, :] = jnp.zeros((EDGE, LANES), BF16)

    def clear(buf):
        @pl.when(ends[0] == 1)
        def _():
            buf[EDGE : EDGE + 96, :] = jnp.zeros((96, LANES), BF16)

        @pl.when(ends[1] == 1)
        def _():
            buf[end - 96 : end, :] = jnp.zeros((96, LANES), BF16)

    def mix(n, _):
        u = up[pl.ds(pl.multiple_of(48 * n, 16), 48), :].astype(BF16)
        first = jnp.maximum(dot(wm1[...], u), 0.0).astype(BF16)
        out = jnp.maximum(dot(wm2[...], first), 0.0).astype(BF16)
        second[pl.ds(pl.multiple_of(EDGE + BLOCK * n, 32), BLOCK), :] = out
        return 0

    lax.fori_loop(0, BLOCKS, mix, 0)
    clear(second)

    def conv(src, dst, w):
        def body(n, _):
            slab = src[pl.ds(pl.multiple_of(BLOCK * n, 64), SLAB), :]
            y = dot(w[...], slab)
            c = y[BLOCK : 2 * BLOCK] + pltpu.roll(y[0:BLOCK], 1, 1)
            c = c + pltpu.roll(y[2 * BLOCK :], LANES - 1, 1)
            rows = pl.ds(pl.multiple_of(EDGE + BLOCK * n, 32), BLOCK)
            dst[rows, :] = (src[rows, :].astype(F32) + jnp.maximum(c, 0.0)).astype(BF16)
            return 0

        lax.fori_loop(0, BLOCKS, body, 0)
        clear(dst)

    conv(second, third, wc1)
    conv(third, fourth, wc2)

    grad[...] = jnp.zeros(grad.shape, F32)
    sq[...] = jnp.zeros(sq.shape, F32)

    def output(n, _):
        slab = fourth[pl.ds(pl.multiple_of(BLOCK * n + 96, 32), SLAB), :]
        y = dot(wout[...].astype(BF16), slab)
        c = y[24:48] + pltpu.roll(y[0:24], 1, 1) + pltpu.roll(y[48:72], LANES - 1, 1)
        rows = pl.ds(pl.multiple_of(8 * n, 8), 8)
        slopes = []
        for o in range(3):
            value = c[8 * o : 8 * o + 8, 0:W]
            recon[o, rows, :] = value
            error = value - target[o, rows, :]
            sq[...] += error * error
            slopes.append((2.0 * error / pixels).astype(BF16).astype(F32))
        slope = jnp.concatenate(slopes, axis=0)
        slope = jnp.concatenate([slope, jnp.zeros((24, LANES - W), F32)], axis=1)
        moved = jnp.concatenate(
            [pltpu.roll(slope, LANES - 1, 1), slope, pltpu.roll(slope, 1, 1)], axis=0
        ).astype(BF16)
        grad[...] += lax.dot_general(
            moved, slab, (((1,), (1,)), ((), ())), preferred_element_type=F32
        )
        return 0

    lax.fori_loop(0, H // 8, output, 0)

    rates = []
    for level in range(LEVELS):
        field = fields[level]
        cols = max(COLS[level], 128)
        wide = WIDE[level]
        rate[...] = jnp.zeros(rate.shape, F32)

        def cells(n, _, level=level, field=field, cols=cols, wide=wide):
            slab = field[pl.ds(pl.multiple_of(8 * n + 8, 8), 16), :]
            moved = [
                slab[:, 0:cols] if j == 0 else pltpu.roll(slab, (-j) % wide, 1)[:, 0:cols]
                for j in range(-2, 3)
            ]
            hi, lo = split2(jnp.concatenate(moved, axis=0))
            inner = jnp.maximum(dot(a1[...], jnp.concatenate([hi, lo, hi], axis=0)), 0.0)
            hi, lo = split2(inner)
            outer = jnp.maximum(dot(a2[...], jnp.concatenate([hi, lo, hi], axis=0)), 0.0)
            hi, lo = split2(outer)
            raw = dot(a3[...], jnp.concatenate([hi, lo, hi], axis=0))
            sigma = raw[8:16]
            soft = jnp.maximum(sigma, 0.0) + jnp.log(1.0 + jnp.exp(-jnp.abs(sigma)))
            row = lax.broadcasted_iota(I32, (8, cols), 0)
            col = lax.broadcasted_iota(I32, (8, cols), 1)
            anchor = ((row + col + parity[level]) & 1) == 0
            centre = jnp.where(anchor, 0.0, raw[0:8])
            spread = jnp.where(anchor, scale[level], 0.1 + soft)
            own = slab[4:12, 0:cols]
            value = laplace(own, centre, spread)
            if level == 0:
                bits[pl.ds(pl.multiple_of(8 * n, 8), 8), :] = value
            if level > 2:
                value = jnp.where((row < ROWS[level]) & (col < COLS[level]), value, 0.0)
            rate[:, 0:cols] += value
            return 0

        count = max(1, ROWS[level] // 8)
        if count == 1:
            cells(0, 0)
        else:
            lax.fori_loop(0, count, cells, 0)
        rates.append(jnp.sum(rate[...]))

    row = lax.broadcasted_iota(I32, (72, SLAB), 0) & 7
    g = grad[...]
    total = jnp.zeros((72, SLAB), F32)
    for r in range(8):
        total = total + jnp.where(row == r, pltpu.roll(g, (-CH * r) % SLAB, 1), 0.0)
    part[...] = jnp.zeros(part.shape, F32)
    for k in range(9):
        part[k : k + 1, :] = jnp.sum(total[8 * k : 8 * k + 8, 0:128], axis=0, keepdims=True)
    lane = lax.broadcasted_iota(I32, (1, 128), 1)
    line = jnp.where(lane == 0, jnp.sum(sq[...]), 0.0)
    for level in range(LEVELS):
        line = jnp.where(lane == 1 + level, rates[level], line)
    part[9:10, :] = line


def pair_steps(lat, lon):
    def flat(f):
        return [(a * lon + b, f(a, b)[0] * lon + f(a, b)[1]) for a in range(lat) for b in range(lon)]

    steps = []
    if (lat, lon) == (8, 32):
        def ring4(v, odd):
            return v ^ 1 if not odd else ((v + 1) % 4 if v & 1 else (v - 1) % 4)

        def far8(z):
            return {1: 6, 6: 1, 2: 5, 5: 2, 3: 0, 0: 3, 4: 7, 7: 4}[z]

        def y_move(a, b, odd):
            y = ring4((a // 4) * 2 + ((b // 2) & 1), odd)
            return (y // 2) * 4 + a % 4, (b & ~2) | ((y & 1) << 1)

        def z_move(a, b, f):
            return a, f(b // 4) * 4 + b % 4

        steps.append(flat(lambda a, b: (a, b ^ 1)))
        for odd in (False, True):
            steps.append(flat(lambda a, b, odd=odd: ((a & ~3) | ring4(a & 3, odd), b)))
        for odd in (False, True):
            steps.append(flat(lambda a, b, odd=odd: y_move(a, b, odd)))
        steps.append(flat(lambda a, b: z_move(a, b, lambda z: z ^ 1)))
        steps.append(flat(lambda a, b: z_move(a, b, lambda z: (z + 1) % 8 if z & 1 else (z - 1) % 8)))
        steps.append(flat(lambda a, b: z_move(a, b, far8)))
        return steps
    k = 1
    while k < lon:
        steps.append(flat(lambda a, b, k=k: (a, b ^ k)))
        k *= 2
    k = 1
    while k < lat:
        steps.append(flat(lambda a, b, k=k: (a ^ k, b)))
        k *= 2
    return steps


def call(kernel, outs, scratch, specs, *args):
    return pl.pallas_call(
        kernel,
        out_shape=outs,
        in_specs=specs,
        out_specs=jax.tree.map(lambda _: VMEM, outs),
        scratch_shapes=scratch,
        compiler_params=pltpu.CompilerParams(vmem_limit_bytes=60 * 1024 * 1024),
    )(*args)


def local(
    target, latent_0, latent_1, latent_2, latent_3, latent_4, latent_5, tile_seeds,
    anchor_parity, anchor_scale, mix_levels, mix_hidden, conv_first, conv_second,
    conv_output, context_in, context_mid, context_out,
):
    lat, lon = lax.axis_size("lat"), lax.axis_size("lon")
    lats = (latent_0, latent_1, latent_2, latent_3, latent_4, latent_5)
    fields = [pltpu.VMEM((TALL[l], WIDE[l]), F32) for l in range(LEVELS)]
    sds = jax.ShapeDtypeStruct
    to_right, to_left = call(
        sides_kernel, (sds((8, 128), F32),) * 2, fields, [SMEM] + [VMEM] * 6, tile_seeds, *lats
    )
    east = [(i, (i + 1) % lon) for i in range(lon)]
    left = lax.ppermute(to_right, "lon", east)
    right = lax.ppermute(to_left, "lon", [(j, i) for i, j in east])
    up, down = call(
        ends_kernel, (sds((8, LANES), F32),) * 2, fields, [SMEM] + [VMEM] * 8,
        tile_seeds, *lats, left, right,
    )
    south = [(i, i + 1) for i in range(lat - 1)]
    above = lax.ppermute(down, "lat", south)
    below = lax.ppermute(up, "lat", [(j, i) for i, j in south])

    names = ("spread", "gather", "place", "tap", "tap_out", "same", "same_out", "levels", "rowof", "ctx")
    prepared = call(
        weights_kernel,
        (
            sds((BLOCK, 48), BF16), sds((BLOCK, BLOCK), BF16), sds((3 * BLOCK, SLAB), BF16),
            sds((3 * BLOCK, SLAB), BF16), sds((72, SLAB), F32), sds((BLOCK, 240), BF16),
            sds((BLOCK, 3 * BLOCK), BF16), sds((16, 3 * BLOCK), BF16),
        ),
        [],
        [VMEM] * (8 + len(names)),
        mix_levels, mix_hidden, conv_first.transpose(2, 3, 0, 1), conv_second.transpose(2, 3, 0, 1),
        conv_output.transpose(0, 2, 3, 1).reshape(27, CH), context_in, context_mid, context_out,
        *[table(n) for n in names],
    )

    index = lax.axis_index("lat")
    ends = jnp.stack([index == 0, index == lat - 1]).astype(I32)
    pixels = float(3 * H * W * lat * lon)
    feature = pltpu.VMEM((2 * EDGE + BLOCK * BLOCKS, LANES), BF16)
    recon, bits, part = call(
        functools.partial(main_kernel, pixels=pixels),
        (sds((3, H, W), F32), sds((H, W), F32), sds((16, 128), F32)),
        fields
        + [pltpu.VMEM((48 * BLOCKS, LANES), F32), feature, feature, feature]
        + [pltpu.VMEM((72, SLAB), F32), pltpu.VMEM((8, W), F32), pltpu.VMEM((8, W), F32)],
        [SMEM] * 4 + [VMEM] * 29,
        tile_seeds, anchor_parity, anchor_scale, ends, *lats, left, right, above, below, target,
        *prepared, *[table(f"rows{l}") for l in range(1, LEVELS)],
        *[table(f"cols{l}") for l in range(1, LEVELS)],
    )
    for step in pair_steps(lat, lon):
        part = part + lax.ppermute(part, ("lat", "lon"), step)
    sizes = [pixels] + [float(ROWS[l] * COLS[l] * lat * lon) for l in range(LEVELS)]
    loss = part[9, 0:7] / jnp.array(sizes, F32)
    grad = part[0:9, 8:80].reshape(3, 3, 3, CH).transpose(1, 3, 2, 0)
    return recon, bits, loss, grad


def solution(mesh):
    tile = P("lat", "lon")
    return jax.shard_map(
        local,
        mesh=mesh,
        in_specs=(P(None, "lat", "lon"),) + (tile,) * 7 + (P(),) * 10,
        out_specs=(P(None, "lat", "lon"), tile, P(), P()),
        check_vma=False,
    )
```

time: 686 us -> 101 us (0.15)
  the two profiles are of different devices: /device:TPU:6 before, /device:TPU:24 now
where the time goes in v1:
time: 101 us
  Pallas kernels  42 us (42%)
  starting transfers between devices  26.2 us (26%)
  waiting for transfers between devices  23.9 us (24%)
  local copies, waits for them, and re-layouts  5.14 us (5%)
  other arithmetic  1.89 us (2%)
  between operations  1.36 us (1%)
    pallas_call x4, Pallas kernels, call(): pl.pallas_call(kernel, out_shape=outs, in_specs=specs, out_specs=jax.tree...  42 us
    ppermute x8, waiting for transfers between devices, local(): part = part + lax.ppermute(part, ('lat', 'lon'), step)  22.4 us
    ppermute x8, starting transfers between devices, local(): part = part + lax.ppermute(part, ('lat', 'lon'), step)  14.9 us
    ppermute x1, starting transfers between devices, local(): below = lax.ppermute(up, 'lat', [(j, i) for i, j in south])  6.06 us
    unnamed x18, local copies, waits for them, and re-layouts  3.77 us
    ppermute x1, starting transfers between devices, local(): above = lax.ppermute(down, 'lat', south)  3.52 us
  transfers between devices with their start and end apart: 12, of which 9 were waited for; matrix products, arithmetic and copies ran while one was open for 3% of the time, Pallas kernels for 4%

profile of v1, /device:TPU:24, one launch (start us, length us, event | category | flops | bytes accessed | tf_op | source)
XLA Modules:
  0.0 100.6 jit_solution(11967982341429302342)
XLA Ops:
  1.3 1.7 %shard_map.390 = (f32[8,128]{1,0:T(8,128)}, f32[8,128]{1,0:T(8,128)}) custom-call(s32[1,1]{1,0:T(1,128)S(6)} %copy.51.seed, f32[64,512]{1,0:T(8,128)} %l0.1, f32[32,256]{1,0:T(8,128)} %l1.1, f32[16,128]{1,0:T(8,128)} %l2.1, f32[8,64]{1,0:T(8,128)} %l3.1, f32[4,32]{1,0:T(4,128)} %l4.1, f32[2,16]{1,0:T(2,128)} %l5.1), custom_call_target="tpu_custom_call" | custom-call | tf_op jit(solution)/shard_map/pallas_call | solution.py:462
  3.0 1.7 %collective-permute-start.1 = (f32[8,128]{1,0:T(8,128)}, f32[8,128]{1,0:T(8,128)S(1)}, u32[]{:S(2)}, u32[]{:S(2)}) collective-permute-start(f32[8,128]{1,0:T(8,128)} %get-tuple-element.20), channel_id=1, source_target_pairs={{1,0},{2,1},{3,2},{4,3},{5,4},{6,5},{7,6},{8,7},{9,8},{10,9},{11,1... | collective-permute-start | bytes 12296 | tf_op jit(solution)/shard_map/ppermute | solution.py:486
  4.8 1.5 %collective-permute-done.refs_6_.left = f32[8,128]{1,0:T(8,128)S(1)} collective-permute-done((f32[8,128]{1,0:T(8,128)}, f32[8,128]{1,0:T(8,128)S(1)}, u32[]{:S(2)}, u32[]{:S(2)}) %collective-permute-start) | collective-permute-done | bytes 4128 | tf_op jit(solution)/shard_map/ppermute | solution.py:485
  7.4 1.7 %shard_map.391 = (f32[8,640]{1,0:T(8,128)}, f32[8,640]{1,0:T(8,128)}) custom-call(s32[1,1]{1,0:T(1,128)S(6)} %copy.51.seed, f32[64,512]{1,0:T(8,128)} %l0.1, f32[32,256]{1,0:T(8,128)} %l1.1, f32[16,128]{1,0:T(8,128)} %l2.1, f32[8,64]{1,0:T(8,128)} %l3.1, f32[4,32]{1,0:T(4,128)} %l4.1, f32[2,16]{1,0:T(2,128)} %l5.1, f32[8,128]{1,0:T(8,128)} %copy-done.2, ...), custom_call_target="tpu_custom_call" | custom-call | tf_op jit(solution)/shard_map/pallas_call | solution.py:462
  9.2 3.5 %collective-permute-start.2 = (f32[8,640]{1,0:T(8,128)}, f32[8,640]{1,0:T(8,128)S(1)}, u32[]{:S(2)}, u32[]{:S(2)}) collective-permute-start(f32[8,640]{1,0:T(8,128)} %get-tuple-element.21), channel_id=1, source_target_pairs={{0,32},{32,64},{64,96},{96,128},{128,160},{160,192},{192,224},{1,3... | collective-permute-start | bytes 61448 | tf_op jit(solution)/shard_map/ppermute | solution.py:492
  12.7 6.1 %collective-permute-start.3 = (f32[8,640]{1,0:T(8,128)}, f32[8,640]{1,0:T(8,128)S(1)}, u32[]{:S(2)}, u32[]{:S(2)}) collective-permute-start(f32[8,640]{1,0:T(8,128)} %get-tuple-element.22), channel_id=1, source_target_pairs={{32,0},{64,32},{96,64},{128,96},{160,128},{192,160},{224,192},{33,... | collective-permute-start | bytes 61448 | tf_op jit(solution)/shard_map/ppermute | solution.py:493
  18.8 0.7 add_convert_fusion.ends
  19.4 0.7 copy.46.ml
  20.8 0.7 copy.47.w1
  21.5 4.0 %shard_map.392 = (bf16[192,48]{1,0:T(8,128)(2,1)}, bf16[192,192]{1,0:T(8,128)(2,1)}, bf16[576,256]{1,0:T(8,128)(2,1)}, bf16[576,256]{1,0:T(8,128)(2,1)}, f32[72,...) custom-call(bf16[24,6]{1,0:T(8,128)(2,1)} %copy.46.ml, ...), custom_call_target="tpu_custom_call" | custom-call | tf_op jit(solution)/shard_map/pallas_call | solution.py:462
  26.1 34.5 %shard_map.393 = (f32[3,64,512]{2,1,0:T(8,128)}, f32[64,512]{1,0:T(8,128)}, f32[16,128]{1,0:T(8,128)}) custom-call(s32[1,1]{1,0:T(1,128)S(6)} %copy.51.seed, s32[6]{0:T(128)} %parity.1, f32[6]{0:T(128)} %scale.1, s32[2]{0:T(128)} %add_convert_fusion.ends, f32[64,512]{1,0:T(8,128)} %l0.1, f32[32,256]{1,0:T(8,128)} %l1.1, f32[16,128]{1,0:T(8,128)} %l2.1, ...), custom_call_target="tpu_custom_call" | custom-call | tf_op jit(solution)/shard_map/pallas_call | solution.py:462
  60.7 2.1 %collective-permute-start.4 = (f32[16,128]{1,0:T(8,128)}, f32[16,128]{1,0:T(8,128)S(1)}, u32[]{:S(2)}, u32[]{:S(2)}) collective-permute-start(f32[16,128]{1,0:T(8,128)} %get-tuple-element.33), channel_id=1, source_target_pairs={{0,1},{1,0},{2,3},{3,2},{4,5},{5,4},{6,7},{7,6},{8,9},{9,8},{10,11... | collective-permute-start | bytes 24584 | tf_op jit(solution)/shard_map/ppermute | solution.py:526
  62.7 1.0 %collective-permute-done.4 = f32[16,128]{1,0:T(8,128)S(1)} collective-permute-done((f32[16,128]{1,0:T(8,128)}, f32[16,128]{1,0:T(8,128)S(1)}, u32[]{:S(2)}, u32[]{:S(2)}) %collective-permute-start.4) | collective-permute-done | bytes 8224 | tf_op jit(solution)/shard_map/ppermute | solution.py:526
  63.8 0.7 add.24
  64.5 3.6 %collective-permute-done.5 = f32[16,128]{1,0:T(8,128)S(1)} collective-permute-done((f32[16,128]{1,0:T(8,128)S(1)}, f32[16,128]{1,0:T(8,128)S(1)}, u32[]{:S(2)}, u32[]{:S(2)}) %collective-permute-start.5) | collective-permute-done | bytes 8224 | tf_op jit(solution)/shard_map/ppermute | solution.py:526
  68.1 4.9 %collective-permute-done.6 = f32[16,128]{1,0:T(8,128)S(1)} collective-permute-done((f32[16,128]{1,0:T(8,128)S(1)}, f32[16,128]{1,0:T(8,128)S(1)}, u32[]{:S(2)}, u32[]{:S(2)}) %collective-permute-start.6) | collective-permute-done | bytes 8224 | tf_op jit(solution)/shard_map/ppermute | solution.py:526
  73.0 3.4 %collective-permute-start.7 = (f32[16,128]{1,0:T(8,128)S(1)}, f32[16,128]{1,0:T(8,128)S(1)}, u32[]{:S(2)}, u32[]{:S(2)}) collective-permute-start(f32[16,128]{1,0:T(8,128)S(1)} %add.26), channel_id=1, source_target_pairs={{0,2},{1,3},{2,0},{3,1},{4,6},{5,7},{6,4},{7,5},{8,10},{9,11},{10,... | collective-permute-start | bytes 24584 | tf_op jit(solution)/shard_map/ppermute | solution.py:526
  76.4 1.6 %collective-permute-done.7 = f32[16,128]{1,0:T(8,128)S(1)} collective-permute-done((f32[16,128]{1,0:T(8,128)S(1)}, f32[16,128]{1,0:T(8,128)S(1)}, u32[]{:S(2)}, u32[]{:S(2)}) %collective-permute-start.7) | collective-permute-done | bytes 8224 | tf_op jit(solution)/shard_map/ppermute | solution.py:526
  78.0 4.9 %collective-permute-done.8 = f32[16,128]{1,0:T(8,128)S(1)} collective-permute-done((f32[16,128]{1,0:T(8,128)S(1)}, f32[16,128]{1,0:T(8,128)S(1)}, u32[]{:S(2)}, u32[]{:S(2)}) %collective-permute-start.8) | collective-permute-done | bytes 8224 | tf_op jit(solution)/shard_map/ppermute | solution.py:526
  83.4 3.1 %collective-permute-done.9 = f32[16,128]{1,0:T(8,128)S(1)} collective-permute-done((f32[16,128]{1,0:T(8,128)S(1)}, f32[16,128]{1,0:T(8,128)S(1)}, u32[]{:S(2)}, u32[]{:S(2)}) %collective-permute-start.9) | collective-permute-done | bytes 8224 | tf_op jit(solution)/shard_map/ppermute | solution.py:526
  86.5 3.3 %collective-permute-start.10 = (f32[16,128]{1,0:T(8,128)S(1)}, f32[16,128]{1,0:T(8,128)S(1)}, u32[]{:S(2)}, u32[]{:S(2)}) collective-permute-start(f32[16,128]{1,0:T(8,128)S(1)} %add.29), channel_id=1, source_target_pairs={{0,28},{1,29},{2,30},{3,31},{4,8},{5,9},{6,10},{7,11},{8,4},{9,5},... | collective-permute-start | bytes 24584 | tf_op jit(solution)/shard_map/ppermute | solution.py:526
  89.9 1.7 %collective-permute-done.10 = f32[16,128]{1,0:T(8,128)S(1)} collective-permute-done((f32[16,128]{1,0:T(8,128)S(1)}, f32[16,128]{1,0:T(8,128)S(1)}, u32[]{:S(2)}, u32[]{:S(2)}) %collective-permute-start.10) | collective-permute-done | bytes 8224 | tf_op jit(solution)/shard_map/ppermute | solution.py:526
  91.5 5.5 %collective-permute-start.11 = (f32[16,128]{1,0:T(8,128)S(1)}, f32[16,128]{1,0:T(8,128)S(1)}, u32[]{:S(2)}, u32[]{:S(2)}) collective-permute-start(f32[16,128]{1,0:T(8,128)S(1)} %add.30), channel_id=1, source_target_pairs={{0,12},{1,13},{2,14},{3,15},{4,24},{5,25},{6,26},{7,27},{8,20},{9,... | collective-permute-start | bytes 24584 | tf_op jit(solution)/shard_map/ppermute | solution.py:526
  97.1 1.6 %collective-permute-done.11 = f32[16,128]{1,0:T(8,128)S(1)} collective-permute-done((f32[16,128]{1,0:T(8,128)S(1)}, f32[16,128]{1,0:T(8,128)S(1)}, u32[]{:S(2)}, u32[]{:S(2)}) %collective-permute-start.11) | collective-permute-done | bytes 8224 | tf_op jit(solution)/shard_map/ppermute | solution.py:526
  (36 shorter events, 4.9 us)
Async XLA Ops:
  3.0 3.2 %collective-permute-start = (f32[8,128]{1,0:T(8,128)}, f32[8,128]{1,0:T(8,128)S(1)}, u32[]{:S(2)}, u32[]{:S(2)}) collective-permute-start(f32[8,128]{1,0:T(8,128)} %get-tuple-element.19), channel_id=1, source_target_pairs={{0,1},{1,2},{2,3},{3,4},{4,5},{5,6},{6,7},{7,8},{8,9},{9,10},{10,1... | collective-permute-start | bytes 12296 | tf_op jit(solution)/shard_map/ppermute | solution.py:485
  3.0 3.3 %collective-permute-start.1 = (f32[8,128]{1,0:T(8,128)}, f32[8,128]{1,0:T(8,128)S(1)}, u32[]{:S(2)}, u32[]{:S(2)}) collective-permute-start(f32[8,128]{1,0:T(8,128)} %get-tuple-element.20), channel_id=1, source_target_pairs={{1,0},{2,1},{3,2},{4,3},{5,4},{6,5},{7,6},{8,7},{9,8},{10,9},{11,1... | collective-permute-start | bytes 12296 | tf_op jit(solution)/shard_map/ppermute | solution.py:486
  6.3 0.6 copy-start.2
  6.9 0.6 copy-start.3
  7.4 12.0 %copy-start.6 = (bf16[24,6]{0,1:T(8,128)(2,1)S(1)}, bf16[24,6]{0,1:T(8,128)(2,1)}, u32[]{:S(2)}) copy-start(bf16[24,6]{0,1:T(8,128)(2,1)} %param.49) | copy-start | bytes 868
  9.2 10.9 %copy-start.4 = (bf16[3,24,3,3]{1,3,2,0:T(4,128)(2,1)S(1)}, bf16[3,24,3,3]{1,3,2,0:T(4,128)(2,1)}, u32[]{:S(2)}) copy-start(bf16[3,24,3,3]{1,3,2,0:T(4,128)(2,1)} %param.53) | copy-start | bytes 3892
  9.2 16.3 %collective-permute-start.2 = (f32[8,640]{1,0:T(8,128)}, f32[8,640]{1,0:T(8,128)S(1)}, u32[]{:S(2)}, u32[]{:S(2)}) collective-permute-start(f32[8,640]{1,0:T(8,128)} %get-tuple-element.21), channel_id=1, source_target_pairs={{0,32},{32,64},{64,96},{96,128},{128,160},{160,192},{192,224},{1,3... | collective-permute-start | bytes 61448 | tf_op jit(solution)/shard_map/ppermute | solution.py:492
  12.7 12.8 %collective-permute-start.3 = (f32[8,640]{1,0:T(8,128)}, f32[8,640]{1,0:T(8,128)S(1)}, u32[]{:S(2)}, u32[]{:S(2)}) collective-permute-start(f32[8,640]{1,0:T(8,128)} %get-tuple-element.22), channel_id=1, source_target_pairs={{32,0},{64,32},{96,64},{128,96},{160,128},{192,160},{224,192},{33,... | collective-permute-start | bytes 61448 | tf_op jit(solution)/shard_map/ppermute | solution.py:493
  20.1 0.7 copy-start.5
  25.5 0.6 copy-start
  25.5 0.6 copy-start.1
  60.7 3.1 %collective-permute-start.4 = (f32[16,128]{1,0:T(8,128)}, f32[16,128]{1,0:T(8,128)S(1)}, u32[]{:S(2)}, u32[]{:S(2)}) collective-permute-start(f32[16,128]{1,0:T(8,128)} %get-tuple-element.33), channel_id=1, source_target_pairs={{0,1},{1,0},{2,3},{3,2},{4,5},{5,4},{6,7},{7,6},{8,9},{9,8},{10,11... | collective-permute-start | bytes 24584 | tf_op jit(solution)/shard_map/ppermute | solution.py:526
  64.5 3.7 %collective-permute-start.5 = (f32[16,128]{1,0:T(8,128)S(1)}, f32[16,128]{1,0:T(8,128)S(1)}, u32[]{:S(2)}, u32[]{:S(2)}) collective-permute-start(f32[16,128]{1,0:T(8,128)S(1)} %add.24), channel_id=1, source_target_pairs={{0,32},{1,33},{2,34},{3,35},{4,36},{5,37},{6,38},{7,39},{8,40},{9,... | collective-permute-start | bytes 24584 | tf_op jit(solution)/shard_map/ppermute | solution.py:526
  68.1 4.9 %collective-permute-start.6 = (f32[16,128]{1,0:T(8,128)S(1)}, f32[16,128]{1,0:T(8,128)S(1)}, u32[]{:S(2)}, u32[]{:S(2)}) collective-permute-start(f32[16,128]{1,0:T(8,128)S(1)} %add.25), channel_id=1, source_target_pairs={{0,96},{1,97},{2,98},{3,99},{4,100},{5,101},{6,102},{7,103},{8,104... | collective-permute-start | bytes 24584 | tf_op jit(solution)/shard_map/ppermute | solution.py:526
  73.0 5.0 %collective-permute-start.7 = (f32[16,128]{1,0:T(8,128)S(1)}, f32[16,128]{1,0:T(8,128)S(1)}, u32[]{:S(2)}, u32[]{:S(2)}) collective-permute-start(f32[16,128]{1,0:T(8,128)S(1)} %add.26), channel_id=1, source_target_pairs={{0,2},{1,3},{2,0},{3,1},{4,6},{5,7},{6,4},{7,5},{8,10},{9,11},{10,... | collective-permute-start | bytes 24584 | tf_op jit(solution)/shard_map/ppermute | solution.py:526
  78.0 4.9 %collective-permute-start.8 = (f32[16,128]{1,0:T(8,128)S(1)}, f32[16,128]{1,0:T(8,128)S(1)}, u32[]{:S(2)}, u32[]{:S(2)}) collective-permute-start(f32[16,128]{1,0:T(8,128)S(1)} %add.27), channel_id=1, source_target_pairs={{0,130},{1,131},{2,128},{3,129},{4,134},{5,135},{6,132},{7,133},{8... | collective-permute-start | bytes 24584 | tf_op jit(solution)/shard_map/ppermute | solution.py:526
  82.9 3.7 %collective-permute-start.9 = (f32[16,128]{1,0:T(8,128)S(1)}, f32[16,128]{1,0:T(8,128)S(1)}, u32[]{:S(2)}, u32[]{:S(2)}) collective-permute-start(f32[16,128]{1,0:T(8,128)S(1)} %add.28), channel_id=1, source_target_pairs={{0,4},{1,5},{2,6},{3,7},{4,0},{5,1},{6,2},{7,3},{8,12},{9,13},{10,... | collective-permute-start | bytes 24584 | tf_op jit(solution)/shard_map/ppermute | solution.py:526
  86.5 5.0 %collective-permute-start.10 = (f32[16,128]{1,0:T(8,128)S(1)}, f32[16,128]{1,0:T(8,128)S(1)}, u32[]{:S(2)}, u32[]{:S(2)}) collective-permute-start(f32[16,128]{1,0:T(8,128)S(1)} %add.29), channel_id=1, source_target_pairs={{0,28},{1,29},{2,30},{3,31},{4,8},{5,9},{6,10},{7,11},{8,4},{9,5},... | collective-permute-start | bytes 24584 | tf_op jit(solution)/shard_map/ppermute | solution.py:526
  91.5 7.2 %collective-permute-start.11 = (f32[16,128]{1,0:T(8,128)S(1)}, f32[16,128]{1,0:T(8,128)S(1)}, u32[]{:S(2)}, u32[]{:S(2)}) collective-permute-start(f32[16,128]{1,0:T(8,128)S(1)} %add.30), channel_id=1, source_target_pairs={{0,12},{1,13},{2,14},{3,15},{4,24},{5,25},{6,26},{7,27},{8,20},{9,... | collective-permute-start | bytes 24584 | tf_op jit(solution)/shard_map/ppermute | solution.py:526
  98.7 0.7 copy-start.7

commit v2 on v1

v2 whole, which is shorter than its diff:
```python
import functools

import jax
import jax.numpy as jnp
import numpy as np
from jax import lax
from jax.experimental import pallas as pl
from jax.experimental.pallas import tpu as pltpu
from jax.sharding import PartitionSpec as P

F32, BF16, I32 = jnp.float32, jnp.bfloat16, jnp.int32
STEPS = (
    (-1, 0), (1, 0), (0, -1), (0, 1), (-2, -1), (-2, 1),
    (2, -1), (2, 1), (-1, -2), (-1, 2), (1, -2), (1, 2),
)
LEVELS, CH, H, W = 6, 24, 64, 512
ROWS = [H >> l for l in range(LEVELS)]
COLS = [W >> l for l in range(LEVELS)]
HALO = [3, 2, 2, 2, 2, 2]
OFFS = [0, 3, 5, 7, 9, 11]
PACK = 13
WIDE = [640, 384, 256, 128, 128, 128]
TALL = [80, 56, 40, 32, 32, 32]
TOP = 12
UPROWS = [0, 48, 32, 16, 16, 16]
LANES = 640
BLOCKS = 9
BLOCK = 8 * CH
SLAB = 256
GROUPS = BLOCK // 16
UNITS = 11
LAST = [(3, 0), (4, 64), (5, 96)]
EDGE = 32
PLACE = [(0, 0), (3, 0), (3, 384), (5, 0), (5, 128), (5, 256)]
VMEM = pl.BlockSpec(memory_space=pltpu.VMEM)
SMEM = pl.BlockSpec(memory_space=pltpu.SMEM)
HBM = pl.BlockSpec(memory_space=pltpu.HBM)
SCALARS = pl.BlockSpec(memory_space=pltpu.HBM)


def dot(a, b):
    return lax.dot_general(a, b, (((1,), (0,)), ((), ())), preferred_element_type=F32)


def dot_t(a, b):
    return lax.dot_general(a, b, (((1,), (1,)), ((), ())), preferred_element_type=F32)


def wrap32(v):
    return int(np.int64(v).astype(np.int32))


def quantize(lat_ref, seed, level):
    shape = lat_ref.shape
    rows = lax.broadcasted_iota(I32, shape, 0)
    cols = lax.broadcasted_iota(I32, shape, 1)
    h = (seed + wrap32(level * 668265263)) + rows * 374761393 + cols * 1103515245
    h = h ^ lax.shift_right_logical(h, jnp.full(shape, 15, I32))
    h = h * 73244475
    h = h ^ lax.shift_right_logical(h, jnp.full(shape, 13, I32))
    h = h * 73244475
    h = h ^ lax.shift_right_logical(h, jnp.full(shape, 16, I32))
    noise = (h & 16777215).astype(F32) * (1.0 / 16777216.0) - 0.5
    return lat_ref[...] + noise


def place_own(lats, seed, fields):
    for level in range(LEVELS):
        fields[level][...] = jnp.zeros(fields[level].shape, F32)
        fields[level][TOP : TOP + ROWS[level], 0 : COLS[level]] = quantize(
            lats[level], seed, level
        )


def place_sides(left, right, fields):
    for level in range(LEVELS):
        base = (COLS[level] // 128) * 128
        for g in range(max(1, ROWS[level] // 8)):
            tile = side_tile(left, right, level, g)
            rows = pl.ds(TOP + 8 * g, 8)
            if base:
                fields[level][rows, base : base + 128] = tile
            else:
                fields[level][rows, 0:128] = fields[level][rows, 0:128] + tile


def place_ends(above, below, fields):
    for level in range(LEVELS):
        h, (r, c), w = HALO[level], PLACE[level], WIDE[level]
        fields[level][TOP - h : TOP, :] = above[r : r + h, c : c + w]
        end = TOP + ROWS[level]
        fields[level][end : end + h, :] = below[r : r + h, c : c + w]


def settle(copies):
    for copy in copies:
        copy.wait()


def side_tile(left, right, level, g):
    h, c = HALO[level], COLS[level]
    lane = lax.broadcasted_iota(I32, (8, 128), 1)
    start = c % 128
    at = PACK * g + OFFS[level]
    tile = jnp.where(
        (lane >= start) & (lane < start + h), pltpu.roll(right, (start - at) % 128, 1), 0.0
    )
    return jnp.where(lane >= 128 - h, pltpu.roll(left, (128 - h - at) % 128, 1), tile)


def sides_kernel(copies, seed, *refs):
    lats, (to_right, to_left), fields = refs[:6], refs[6:8], refs[8:]
    settle(copies)
    place_own(lats, seed[0, 0], fields)
    lane = lax.broadcasted_iota(I32, (8, 128), 1)
    right = jnp.zeros((8, 128), F32)
    left = jnp.zeros((8, 128), F32)
    for level in range(LEVELS):
        h, c = HALO[level], COLS[level]
        base = max(c - 128, 0)
        for g in range(max(1, ROWS[level] // 8)):
            at = PACK * g + OFFS[level]
            here = (lane >= at) & (lane < at + h)
            rows = pl.ds(TOP + 8 * g, 8)
            last = fields[level][rows, base : base + 128]
            first = fields[level][rows, 0:128]
            right = jnp.where(here, pltpu.roll(last, (at - (c - h - base)) % 128, 1), right)
            left = jnp.where(here, pltpu.roll(first, at % 128, 1), left)
    to_right[...] = right
    to_left[...] = left


def ends_kernel(copies, *refs):
    fields, (left, right), (_, up, down) = refs[:6], refs[6:8], refs[8:]
    up[...] = jnp.zeros(up.shape, F32)
    down[...] = jnp.zeros(down.shape, F32)
    for level in range(LEVELS):
        h, (r, c), own = HALO[level], PLACE[level], COLS[level]
        count = max(1, ROWS[level] // 8)
        base = (own // 128) * 128
        for dst, g, skip in ((up, 0, 0), (down, count - 1, min(8, ROWS[level]) - h)):
            tile = side_tile(left[...], right[...], level, g)
            at = TOP + 8 * g + skip
            if base:
                dst[r : r + h, c : c + base] = fields[level][at : at + h, 0:base]
                dst[r : r + h, c + base : c + base + 128] = tile[skip : skip + h]
            else:
                dst[r : r + h, c : c + 128] = (
                    fields[level][at : at + h, :] + tile[skip : skip + h]
                )


def slab_row(d, c):
    return CH * d + EDGE + c


@functools.lru_cache(None)
def tables():
    t = {}
    spread = np.zeros((BLOCK, CH), np.float32)
    for r in range(8):
        for c in range(CH):
            spread[CH * r + c, c] = 1
    t["spread"] = spread
    t["gather"] = np.ascontiguousarray(spread.T)
    place = np.zeros((CH, SLAB), np.float32)
    tap = np.full((BLOCK, SLAB), 9, np.float32)
    for d in range(-1, 9):
        for c in range(CH):
            place[c, slab_row(d, c)] = 1
            for r in range(8):
                tap[CH * r : CH * r + CH, slab_row(d, c)] = d - r + 1
    t["place"], t["tap"] = place, tap
    t["tap_out"] = np.tile(tap[::CH], (3, 1))
    same = np.zeros((BLOCK, BLOCK), np.float32)
    for r in range(8):
        same[CH * r : CH * r + CH, CH * r : CH * r + CH] = 1
    t["same"] = same
    t["same_out"] = np.tile(same[::CH], (2, 1))
    levels = np.zeros((LEVELS, 8 * LEVELS), np.float32)
    rowof = np.zeros((BLOCK, 8 * LEVELS), np.float32)
    for l in range(LEVELS):
        for r in range(8):
            levels[l, 8 * l + r] = 1
            rowof[CH * r : CH * r + CH, 8 * l + r] = 1
    t["levels"], t["rowof"] = levels, rowof
    ctx = np.zeros((8, len(STEPS), 80), np.float32)
    for r in range(8):
        for k, (i, j) in enumerate(STEPS):
            ctx[r, k, (j + 2) * 16 + (r + i + 4)] = 1
    t["ctx"] = ctx
    for l in range(1, LEVELS):
        s = 1 << l
        up_r = np.zeros((72, UPROWS[l]), np.float32)
        for n in range(72):
            y = n - 4
            m, p = y >> l, ((y & (s - 1)) + 0.5) / s - 0.5
            for e, wgt in ((-1, max(-p, 0)), (0, 1 - abs(p)), (1, max(p, 0))):
                at = TOP - 8 + m + e
                if 0 <= at < UPROWS[l]:
                    up_r[n, at] += wgt
        up_c = np.zeros((WIDE[l], LANES), np.float32)
        for n in range(LANES):
            x = n if n < W + 4 else n - LANES
            if x < -4:
                continue
            m, p = x >> l, ((x & (s - 1)) + 0.5) / s - 0.5
            for e, wgt in ((-1, max(-p, 0)), (0, 1 - abs(p)), (1, max(p, 0))):
                q = m + e
                if -HALO[l] <= q < COLS[l] + HALO[l]:
                    up_c[q % WIDE[l], n] += wgt
        t[f"rows{l}"] = np.concatenate([up_r] * 3, axis=1)
        t[f"cols{l}"] = up_c
    return t


def table(name, dtype=BF16):
    return jnp.asarray(tables()[name], dtype)


def split2(x):
    hi = x.astype(BF16)
    return hi, (x - hi.astype(F32)).astype(BF16)


def split3(x):
    hi = x.astype(BF16)
    rest = x - hi.astype(F32)
    mid = rest.astype(BF16)
    return hi, mid, (rest - mid.astype(F32)).astype(BF16)


def conv_weights_kernel(copies, cf, cs, co, spread, place, tap, tap_out, wc1, wc2, wout):
    settle(copies)
    grow = spread[...]
    taps = tap[...].astype(F32)
    for src, dst in ((cf, wc1), (cs, wc2)):
        for b in range(3):
            total = jnp.zeros((BLOCK, SLAB), F32)
            for a in range(3):
                full = dot(dot(grow, src[a, b]).astype(BF16), place[...])
                total = jnp.where(taps == float(a), full, total)
            total = total.astype(BF16)
            for g in range(GROUPS):
                at = 48 * g + 16 * b
                dst[at : at + 16, :] = total[16 * g : 16 * g + 16]
    taps3 = tap_out[...].astype(F32)[0:8]
    for o in range(3):
        rows = [dot(co[o, a], place[...]) for a in range(3)]
        for b in range(3):
            total = jnp.zeros((8, SLAB), F32)
            for a in range(3):
                line = jnp.broadcast_to(rows[a][b : b + 1], (8, SLAB))
                total = jnp.where(taps3 == float(a), line, total)
            at = 24 * b + 8 * o
            wout[at : at + 8, :] = total


def mix_weights_kernel(
    copies, ml, mh, w1, w2, w3, spread, gather, same, same_out, levels, rowof, ctx,
    token, wm1, wm2, a1, a2, a3,
):
    settle(copies)
    token[...] = jnp.zeros(token.shape, F32)
    grow = spread[...]
    wide = gather[...]

    def diag(w):
        return dot(dot(grow, w).astype(BF16), wide) * same[...].astype(F32)

    wm1[...] = (
        dot(dot_t(grow, ml[...]).astype(BF16), levels[...]) * rowof[...].astype(F32)
    ).astype(BF16)
    wm2[...] = diag(mh[...]).astype(BF16)
    hi, lo = split2(w1[...])
    hi, lo = dot_t(grow, hi).astype(BF16), dot_t(grow, lo).astype(BF16)
    for r in range(8):
        rows = slice(CH * r, CH * r + CH)
        sel = ctx[r]
        h, l = dot(hi[rows], sel).astype(BF16), dot(lo[rows], sel).astype(BF16)
        a1[rows, :] = jnp.concatenate([h, h, l], axis=1)
    hi, lo = split2(w2[...])
    h, l = diag(hi).astype(BF16), diag(lo).astype(BF16)
    a2[...] = jnp.concatenate([h, h, l], axis=1)
    hi, lo = split2(w3[...])
    keep = same_out[...].astype(F32)

    def out(w):
        v = dot(w, wide)
        v = jnp.concatenate(
            [jnp.broadcast_to(v[0:1], (8, BLOCK)), jnp.broadcast_to(v[1:2], (8, BLOCK))], axis=0
        )
        return (v * keep).astype(BF16)

    h, l = out(hi), out(lo)
    a3[...] = jnp.concatenate([h, h, l], axis=1)


def laplace(x, centre, spread):
    y = 1.0 / spread
    off = x - centre
    mag = jnp.abs(off)
    inside = jnp.clip(off, -0.5, 0.5)
    e1 = jnp.exp((inside - 0.5) * y)
    e2 = jnp.exp((-0.5 - inside) * y)
    poly = y * (1 - y * (1 / 2 - y * (1 / 6 - y * (1 / 24 - y * (1 / 120)))))
    tail = jnp.where(y < 0.05, poly, 1.0 - e1 * e2)
    beyond = mag >= 0.5
    arg = jnp.where(beyond, 0.5 * tail, 1.0 - 0.5 * (e1 + e2))
    extra = jnp.where(beyond, (mag - 0.5) * y, 0.0)
    return (extra - jnp.log(arg)) * (1.0 / 0.6931471805599453)


def main_kernel(
    copies, parity, scale, q0, q1, q2, q3, q4, q5, left, right, above, below, target,
    wm1, wm2, wc1, wc2, wout, a1, a2, a3, r1, r2, r3, r4, r5, u1, u2, u3, u4, u5,
    recon_out, bits_out, part,
    recon, bits, sems, f0, f1, f2, f3, f4, f5, up, second, third, taps, hidden1, hidden2, own, anchors, moved, sq,
    *, pixels, lat,
):
    fields = (f0, f1, f2, f3, f4, f5)
    settle(copies[:2])
    for src, dst in zip((q0, q1, q2, q3, q4, q5), fields):
        dst[...] = src[...]
    place_sides(left[...], right[...], fields)
    place_ends(above, below, fields)

    lane = lax.broadcasted_iota(I32, (8, 128), 1)
    row = lax.broadcasted_iota(I32, (8, 128), 0)

    def turn(level, n, j):
        slab = fields[level][8 * n + 8 : 8 * n + 24, :]
        cols, wide = max(COLS[level], 128), WIDE[level]
        return (slab if j == 0 else pltpu.roll(slab, (-j) % wide, 1))[:, 0:cols]

    def small(j):
        deep = lax.broadcasted_iota(I32, (16, 128), 1)
        out = jnp.zeros((16, 128), F32)
        for level, at in LAST:
            turned = fields[level][8:24, :]
            if (at - j) % 128:
                turned = pltpu.roll(turned, (at - j) % 128, 1)
            out = jnp.where((deep >= at) & (deep < at + COLS[level]), turned, out)
        return out

    def unit(u, shifted):
        hi, lo = split2(jnp.concatenate(shifted, axis=0))
        taps[u, 0:80, :] = hi
        taps[u, 80:160, :] = lo
        own[u] = shifted[2][4:12]

    for n in range(8):
        unit(n, [turn(0, n, j) for j in range(-2, 3)])
    for n in range(2):
        unit(8 + n, [
            jnp.concatenate([turn(1, 2 * n, j), turn(1, 2 * n + 1, j)], axis=1)
            for j in range(-2, 3)
        ])
    unit(10, [
        jnp.concatenate([turn(2, 0, j), turn(2, 1, j), small(j), jnp.zeros((16, 128), F32)], axis=1)
        for j in range(-2, 3)
    ])

    def cover(level):
        odd = (row + lane + parity[level]) & 1
        plain = jnp.full((8, 128), scale[level], F32)
        return jnp.where(odd == 0, plain, 0.0)

    mixed = jnp.zeros((8, 128), F32)
    for level, at in LAST:
        mixed = jnp.where((lane >= at) & (lane < at + COLS[level]), cover(level), mixed)
    for u in range(UNITS):
        tiles = [cover(0 if u < 8 else 1)] * 4
        if u == 10:
            tiles = [cover(2), cover(2), mixed, mixed]
        anchors[u] = jnp.concatenate(tiles, axis=1)

    taps[UNITS] = jnp.zeros((160, W), BF16)
    own[UNITS] = jnp.zeros((8, W), F32)
    anchors[UNITS] = jnp.ones((8, W), F32)

    settle(copies[3:])
    for n in range(BLOCKS):
        up[48 * n : 48 * n + 8, :] = f0[8 + 8 * n : 16 + 8 * n, :]
    for level, ru, cu in ((1, r1, u1), (2, r2, u2), (3, r3, u3), (4, r4, u4), (5, r5, u5)):
        count = UPROWS[level]
        grown = dot(jnp.concatenate(split3(fields[level][8 : 8 + count, :]), axis=0), cu[...])
        grown = (grown[0:count] + grown[count : 2 * count]) + grown[2 * count :]
        full = dot(ru[...], jnp.concatenate(split3(grown), axis=0))
        for n in range(BLOCKS):
            up[48 * n + 8 * level : 48 * n + 8 * level + 8, :] = full[8 * n : 8 * n + 8]

    end = EDGE + BLOCK * BLOCKS
    for buf in (second, third):
        buf[0:EDGE, :] = jnp.zeros((EDGE, LANES), BF16)
        buf[end : end + EDGE, :] = jnp.zeros((EDGE, LANES), BF16)
    index = lax.axis_index("lat")

    def clear(buf):
        @pl.when(index == 0)
        def _():
            buf[EDGE : EDGE + 96, :] = jnp.zeros((96, LANES), BF16)

        @pl.when(index == lat - 1)
        def _():
            buf[end - 96 : end, :] = jnp.zeros((96, LANES), BF16)

    def block_rows(n):
        return pl.ds(pl.multiple_of(EDGE + BLOCK * n, 32), BLOCK)

    def mix(n):
        u = up[pl.ds(pl.multiple_of(48 * n, 16), 48), :].astype(BF16)
        first = jnp.maximum(dot(wm1[...], u), 0.0).astype(BF16)
        second[block_rows(n), :] = jnp.maximum(dot(wm2[...], first), 0.0).astype(BF16)

    def conv(src, dst, w, n):
        slab = src[pl.ds(pl.multiple_of(BLOCK * n, 64), SLAB), :]
        y = dot(w[...], slab)
        before = src[block_rows(n), :]
        out = []
        for g in range(GROUPS):
            at = 48 * g
            c = y[at + 16 : at + 32] + pltpu.roll(y[at : at + 16], 1, 1)
            c = c + pltpu.roll(y[at + 32 : at + 48], LANES - 1, 1)
            kept = before[16 * g : 16 * g + 16].astype(F32)
            out.append((kept + jnp.maximum(c, 0.0)).astype(BF16))
        dst[block_rows(n), :] = jnp.concatenate(out, axis=0)

    def layer(src, dst, w, u, k):
        hi, lo = src[u, 0:k, :], src[u, k : 2 * k, :]
        hi, lo = split2(jnp.maximum(dot(w[...], jnp.concatenate([hi, lo, hi], axis=0)), 0.0))
        dst[u, 0:BLOCK, :] = hi
        dst[u, BLOCK : 2 * BLOCK, :] = lo

    def cost(u):
        hi, lo = hidden2[u, 0:BLOCK, :], hidden2[u, BLOCK : 2 * BLOCK, :]
        raw = dot(a3[...], jnp.concatenate([hi, lo, hi], axis=0))
        sigma = raw[8:16]
        soft = jnp.maximum(sigma, 0.0) + jnp.log(1.0 + jnp.exp(-jnp.abs(sigma)))
        plain = anchors[u]
        anchor = plain > 0.0
        centre = jnp.where(anchor, 0.0, raw[0:8])
        own[u] = laplace(own[u], centre, jnp.where(anchor, plain, 0.1 + soft))

    def run(synth, entropy):
        def body(t, _):
            for k in range(4):
                if k < 3:
                    synth(3 * t + k)
                entropy(4 * t + k)
            return 0

        lax.fori_loop(0, 3, body, 0)

    run(mix, lambda u: layer(taps, hidden1, a1, u, 80))
    clear(second)
    run(lambda n: conv(second, third, wc1, n), lambda u: layer(hidden1, hidden2, a2, u, BLOCK))
    clear(third)
    run(lambda n: conv(third, second, wc2, n), cost)
    clear(second)

    for n in range(8):
        bits[8 * n : 8 * n + 8, :] = own[n]
    sq[...] = jnp.zeros(sq.shape, F32)

    def output(n):
        slab = second[pl.ds(pl.multiple_of(BLOCK * n + 96, 32), SLAB), :]
        y = dot(wout[...].astype(BF16), slab)
        c = y[24:48] + pltpu.roll(y[0:24], 1, 1) + pltpu.roll(y[48:72], LANES - 1, 1)
        rows = pl.ds(pl.multiple_of(8 * n, 8), 8)
        slopes = []
        total = jnp.zeros((8, W), F32)
        for o in range(3):
            value = c[8 * o : 8 * o + 8, 0:W]
            recon[o, rows, :] = value
            error = value - target[o, rows, :]
            total = total + error * error
            slopes.append((2.0 * error / pixels).astype(BF16).astype(F32))
        slope = jnp.concatenate(slopes, axis=0)
        slope = jnp.concatenate([slope, jnp.zeros((24, LANES - W), F32)], axis=1)
        moved[n, 0:72, :] = jnp.concatenate(
            [pltpu.roll(slope, LANES - 1, 1), slope, pltpu.roll(slope, 1, 1)], axis=0
        ).astype(BF16)
        return total

    def outputs(t, _):
        total = output(4 * t)
        for k in range(1, 4):
            total = total + output(4 * t + k)
        sq[...] += total
        return 0

    settle(copies[2:3])
    send_bits = pltpu.make_async_copy(bits, bits_out, sems.at[0])
    send_bits.start()
    lax.fori_loop(0, 2, outputs, 0)
    send_recon = pltpu.make_async_copy(recon, recon_out, sems.at[1])
    send_recon.start()
    g = jnp.zeros((72, SLAB), F32)
    for n in range(8):
        g = g + dot_t(moved[n, 0:72, :], second[BLOCK * n + 96 : BLOCK * n + 96 + SLAB, :])

    sums = [jnp.zeros((8, W), F32)] * 2
    for n in range(8):
        sums[0] = sums[0] + own[n]
    sums[1] = own[8] + own[9]
    sums.append(own[10, :, 0:128] + own[10, :, 128:256])
    for level, at in LAST:
        keep = (lane >= at) & (lane < at + COLS[level]) & (row < ROWS[level])
        sums.append(jnp.where(keep, own[10, :, 256:384], 0.0))
    row = lax.broadcasted_iota(I32, (72, SLAB), 0) & 7
    total = jnp.zeros((72, SLAB), F32)
    for r in range(8):
        total = total + jnp.where(row == r, pltpu.roll(g, (-CH * r) % SLAB, 1), 0.0)
    part[...] = jnp.zeros(part.shape, F32)
    for k in range(9):
        part[k : k + 1, :] = jnp.sum(total[8 * k : 8 * k + 8, 0:128], axis=0, keepdims=True)
    lane = lax.broadcasted_iota(I32, (1, 128), 1)
    line = jnp.where(lane == 0, jnp.sum(sq[...]), 0.0)
    for level in range(LEVELS):
        line = jnp.where(lane == 1 + level, jnp.sum(sums[level]), line)
    part[9:10, :] = line
    send_bits.wait()
    send_recon.wait()


def final_kernel(copies, mine, other, loss, grad, *, sizes):
    total = mine[...] + other[...]
    lane = lax.broadcasted_iota(I32, (1, 7), 1)
    size = jnp.full((1, 7), sizes[0], F32)
    for k in range(1, 7):
        size = jnp.where(lane == k, sizes[k], size)
    loss[...] = total[9:10, 0:7] / size
    for a in range(3):
        turned = pltpu.roll(total, 128 - 8 - CH * a, 1)
        for b in range(3):
            for o in range(3):
                k = 3 * b + o
                grad[o, a, b : b + 1, :] = turned[k : k + 1, 0:CH]


def pair_steps(lat, lon):
    def flat(f):
        return [(a * lon + b, f(a, b)[0] * lon + f(a, b)[1]) for a in range(lat) for b in range(lon)]

    steps = []
    if (lat, lon) == (8, 32):
        def ring4(v, odd):
            return v ^ 1 if not odd else ((v + 1) % 4 if v & 1 else (v - 1) % 4)

        def far8(z):
            return {1: 6, 6: 1, 2: 5, 5: 2, 3: 0, 0: 3, 4: 7, 7: 4}[z]

        def y_move(a, b, odd):
            y = ring4((a // 4) * 2 + ((b // 2) & 1), odd)
            return (y // 2) * 4 + a % 4, (b & ~2) | ((y & 1) << 1)

        def z_move(a, b, f):
            return a, f(b // 4) * 4 + b % 4

        steps.append(flat(lambda a, b: (a, b ^ 1)))
        for odd in (False, True):
            steps.append(flat(lambda a, b, odd=odd: ((a & ~3) | ring4(a & 3, odd), b)))
        for odd in (False, True):
            steps.append(flat(lambda a, b, odd=odd: y_move(a, b, odd)))
        steps.append(flat(lambda a, b: z_move(a, b, lambda z: z ^ 1)))
        steps.append(flat(lambda a, b: z_move(a, b, lambda z: (z + 1) % 8 if z & 1 else (z - 1) % 8)))
        steps.append(flat(lambda a, b: z_move(a, b, far8)))
        return steps
    k = 1
    while k < lon:
        steps.append(flat(lambda a, b, k=k: (a, b ^ k)))
        k *= 2
    k = 1
    while k < lat:
        steps.append(flat(lambda a, b, k=k: (a ^ k, b)))
        k *= 2
    return steps


def call(kernel, outs, scratch, specs, mib, *args, out_specs=None):
    held = [i for i, spec in enumerate(specs) if spec is HBM or spec is SCALARS]
    many = len(jax.tree.leaves(outs))

    def body(*refs):
        args_in, rest = list(refs[: len(specs)]), refs[len(specs) :]
        outs_in, work = rest[:many], rest[many:]
        bufs, sems, work = work[: len(held)], work[len(held)], work[len(held) + 1 :]
        copies = []
        for k, i in enumerate(held):
            copy = pltpu.make_async_copy(args_in[i], bufs[k], sems.at[k])
            copy.start()
            copies.append(copy)
            args_in[i] = bufs[k]
        kernel(copies, *args_in, *outs_in, *work)

    args = [
        pltpu.with_memory_space_constraint(a, pltpu.HBM) if spec is HBM or spec is SCALARS else a
        for a, spec in zip(args, specs)
    ]
    space = {i: pltpu.SMEM if specs[i] is SCALARS else pltpu.VMEM for i in held}
    buffers = [space[i](args[i].shape, args[i].dtype) for i in held]
    return pl.pallas_call(
        body,
        out_shape=outs,
        in_specs=specs,
        out_specs=out_specs or jax.tree.map(lambda _: VMEM, outs),
        scratch_shapes=buffers + [pltpu.SemaphoreType.DMA((max(1, len(held)),))] + list(scratch),
        compiler_params=pltpu.CompilerParams(vmem_limit_bytes=mib * 1024 * 1024),
        name=getattr(kernel, "func", kernel).__name__,
    )(*args)


def local(
    target, latent_0, latent_1, latent_2, latent_3, latent_4, latent_5, tile_seeds,
    anchor_parity, anchor_scale, mix_levels, mix_hidden, conv_first, conv_second,
    conv_output, context_in, context_mid, context_out,
):
    lat, lon = lax.axis_size("lat"), lax.axis_size("lon")
    lats = (latent_0, latent_1, latent_2, latent_3, latent_4, latent_5)
    fields = [pltpu.VMEM((TALL[l], WIDE[l]), F32) for l in range(LEVELS)]
    sds = jax.ShapeDtypeStruct
    packs = (sds((8, LANES), F32),) * 2
    whole = tuple(sds((TALL[l], WIDE[l]), F32) for l in range(LEVELS))
    to_right, to_left, *quantized = call(
        sides_kernel, (sds((8, 128), F32),) * 2 + whole, [], [SMEM] + [HBM] * 6, 4,
        tile_seeds, *lats,
    )
    east = [(i, (i + 1) % lon) for i in range(lon)]
    left = lax.ppermute(to_right, "lon", east)
    right = lax.ppermute(to_left, "lon", [(j, i) for i, j in east])
    names = ("spread", "gather", "same", "same_out", "levels", "rowof", "ctx")
    token, wm1, wm2, a1, a2, a3 = call(
        mix_weights_kernel,
        (
            sds((8, 128), F32), sds((BLOCK, 48), BF16), sds((BLOCK, BLOCK), BF16),
            sds((BLOCK, 240), BF16), sds((BLOCK, 3 * BLOCK), BF16), sds((16, 3 * BLOCK), BF16),
        ),
        [], [HBM] * (5 + len(names)), 8,
        mix_levels.T, mix_hidden, context_in.T, context_mid, context_out, *[table(n) for n in names],
    )
    up, down = call(
        ends_kernel, packs, [], [VMEM] * 9, 4, *quantized, left, right, token,
    )
    south = [(i, i + 1) for i in range(lat - 1)]
    above = lax.ppermute(down, "lat", south)
    below = lax.ppermute(up, "lat", [(j, i) for i, j in south])
    names = ("spread", "place", "tap", "tap_out")
    wc1, wc2, wout = call(
        conv_weights_kernel,
        (sds((3 * BLOCK, SLAB), BF16), sds((3 * BLOCK, SLAB), BF16), sds((72, SLAB), F32)),
        [], [HBM] * (3 + len(names)), 8,
        conv_first.transpose(2, 3, 0, 1), conv_second.transpose(2, 3, 0, 1),
        conv_output.transpose(0, 2, 3, 1), *[table(n) for n in names],
    )

    pixels = float(3 * H * W * lat * lon)
    feature = pltpu.VMEM((2 * EDGE + BLOCK * BLOCKS, LANES), BF16)
    hidden = pltpu.VMEM((UNITS + 1, 2 * BLOCK, W), BF16)
    plain = pltpu.VMEM((UNITS + 1, 8, W), F32)
    fields = [pltpu.VMEM((TALL[l], WIDE[l]), F32) for l in range(LEVELS)]
    recon, bits, part = call(
        functools.partial(main_kernel, pixels=pixels, lat=lat),
        (sds((3, H, W), F32), sds((H, W), F32), sds((16, 128), F32)),
        [pltpu.VMEM((3, H, W), F32), pltpu.VMEM((H, W), F32), pltpu.SemaphoreType.DMA((2,))]
        + fields
        + [pltpu.VMEM((48 * BLOCKS, LANES), F32), feature, feature]
        + [pltpu.VMEM((UNITS + 1, 160, W), BF16), hidden, hidden, plain, plain]
        + [pltpu.VMEM((8, 80, LANES), BF16), pltpu.VMEM((8, W), F32)],
        [SCALARS] * 2 + [VMEM] * 10 + [HBM] + [VMEM] * 8 + [HBM] * 10,
        32,
        anchor_parity, anchor_scale, *quantized, left, right, above, below, target,
        wm1, wm2, wc1, wc2, wout, a1, a2, a3,
        *[table(f"rows{l}") for l in range(1, LEVELS)],
        *[table(f"cols{l}") for l in range(1, LEVELS)],
        out_specs=(HBM, HBM, VMEM),
    )
    steps = pair_steps(lat, lon)
    for step in steps[:-1]:
        part = part + lax.ppermute(part, ("lat", "lon"), step)
    other = lax.ppermute(part, ("lat", "lon"), steps[-1])
    sizes = [pixels] + [float(ROWS[l] * COLS[l] * lat * lon) for l in range(LEVELS)]
    loss, grad = call(
        functools.partial(final_kernel, sizes=sizes),
        (sds((1, 7), F32), sds((3, 3, 3, CH), F32)), [], [VMEM] * 2, 1, part, other,
    )
    return recon, bits, loss.reshape(7), grad.transpose(0, 3, 1, 2)


def solution(mesh):
    tile = P("lat", "lon")
    return jax.shard_map(
        local,
        mesh=mesh,
        in_specs=(P(None, "lat", "lon"),) + (tile,) * 7 + (P(),) * 10,
        out_specs=(P(None, "lat", "lon"), tile, P(), P()),
        check_vma=False,
    )
```

time: 101 us -> 75.7 us (0.75)
  the two profiles are of different devices: /device:TPU:24 before, /device:TPU:6 now
where the time goes in v2:
time: 75.7 us; the launch traced here: 75.5 us
  waiting for transfers between devices  32 us (42%)
  Pallas kernels  24.2 us (32%)
  starting transfers between devices  17.9 us (24%)
  between operations  1.39 us (2%)
    ppermute x7, waiting for transfers between devices, local(): part = part + lax.ppermute(part, ('lat', 'lon'), step)  24.3 us
    pallas_call x6, Pallas kernels, call(): pl.pallas_call(body, out_shape=outs, in_specs=specs, out_specs=out_specs...  24.2 us
    ppermute x1, starting transfers between devices, local(): right = lax.ppermute(to_left, 'lon', [(j, i) for i, j in east])  6.38 us
    ppermute x1, starting transfers between devices, local(): above = lax.ppermute(down, 'lat', south)  4.72 us
    ppermute x1, waiting for transfers between devices, local(): below = lax.ppermute(up, 'lat', [(j, i) for i, j in south])  4.49 us
    ppermute x1, waiting for transfers between devices, local(): other = lax.ppermute(part, ('lat', 'lon'), steps[-1])  3.18 us
    ppermute x7, starting transfers between devices, local(): part = part + lax.ppermute(part, ('lat', 'lon'), step)  2.5 us
    ppermute x1, starting transfers between devices, local(): other = lax.ppermute(part, ('lat', 'lon'), steps[-1])  2.27 us
  transfers between devices with their start and end apart: 12, of which 9 were waited for; matrix products, arithmetic and copies ran while one was open for 0% of the time, Pallas kernels for 6%

profile of v2, /device:TPU:6, one launch (start us, length us, event | category | flops | bytes accessed | tf_op | source)
XLA Modules:
  0.0 75.5 jit_solution(17455038218915354541)
XLA Ops:
  1.3 1.2 %sides_kernel.1 = (f32[8,128]{1,0:T(8,128)S(1)}, f32[8,128]{1,0:T(8,128)S(1)}, f32[80,640]{1,0:T(8,128)S(1)}, f32[56,384]{1,0:T(8,128)S(1)}, f32[40,256]{1,0:T(8...) custom-call(s32[1,1]{1,0:T(1,128)S(6)} %copy.43.refs_0_, f32[64,512]{1,0:T(8,128)} %refs_1_.3, ...), custom_call_target="tpu_custom_call" | custom-call | tf_op jit(solution)/shard_map/sides_kernel/pallas_call | solution.py:603
  2.5 0.1 collective-permute-start
  2.6 6.4 %collective-permute-start.1 = (f32[8,128]{1,0:T(8,128)S(1)}, f32[8,128]{1,0:T(8,128)S(1)}, u32[]{:S(2)}, u32[]{:S(2)}) collective-permute-start(f32[8,128]{1,0:T(8,128)S(1)} %get-tuple-element.35), channel_id=1, source_target_pairs={{1,0},{2,1},{3,2},{4,3},{5,4},{6,5},{7,6},{8,7},{9,8},{10,9},{11,1... | collective-permute-start | bytes 12296 | tf_op jit(solution)/shard_map/ppermute | solution.py:631
  9.0 1.8 %mix_weights_kernel.1 = (f32[8,128]{1,0:T(8,128)S(1)}, bf16[192,48]{1,0:T(8,128)(2,1)S(1)}, bf16[192,192]{1,0:T(8,128)(2,1)S(1)}, bf16[192,240]{1,0:T(8,128)(2,1...) custom-call(bf16[6,24]{1,0:T(8,128)(2,1)} %bitcast.11, bf16[24,24]{1,0:T(8,128)(2,1)} %refs_1_.4, ...), custom_call_target="tpu_custom_call" | custom-call | tf_op jit(solution)/shard_map/mix_weights_kernel/pallas_call | solution.py:603
  10.8 0.0 collective-permute-done.1.refs_7_.refs_9_
  10.8 0.1 ends_kernel.1
  10.9 4.7 %collective-permute-start.2 = (f32[8,640]{1,0:T(8,128)S(1)}, f32[8,640]{1,0:T(8,128)S(1)}, u32[]{:S(2)}, u32[]{:S(2)}) collective-permute-start(f32[8,640]{1,0:T(8,128)S(1)} %get-tuple-element.37), channel_id=1, source_target_pairs={{0,32},{32,64},{64,96},{96,128},{128,160},{160,192},{192,224},{1,3... | collective-permute-start | bytes 61448 | tf_op jit(solution)/shard_map/ppermute | solution.py:646
  15.7 1.9 %collective-permute-start.3 = (f32[8,640]{1,0:T(8,128)S(1)}, f32[8,640]{1,0:T(8,128)S(1)}, u32[]{:S(2)}, u32[]{:S(2)}) collective-permute-start(f32[8,640]{1,0:T(8,128)S(1)} %get-tuple-element.38), channel_id=1, source_target_pairs={{32,0},{64,32},{96,64},{128,96},{160,128},{192,160},{224,192},{33,... | collective-permute-start | bytes 61448 | tf_op jit(solution)/shard_map/ppermute | solution.py:647
  17.6 2.9 %conv_weights_kernel.1 = (bf16[576,256]{1,0:T(8,128)(2,1)S(1)}, bf16[576,256]{1,0:T(8,128)(2,1)S(1)}, f32[72,256]{1,0:T(8,128)S(1)}) custom-call(bf16[3,3,24,24]{3,2,1,0:T(8,128)(2,1)} %bitcast.7, bf16[3,3,24,24]{3,2,1,0:T(8,128)(2,1)} %bitcast.8, bf16[3,3,3,24]{3,2,1,0:T(4,128)(2,1)} %bitcast.9, bf16[192,24]{1,0:T(8,128)(2,1)} %constant.40.clone.refs_5_.refs_3_, ...), custom_call_target="tpu_custom_call" | custom-call | tf_op jit(solution)/shard_map/conv_weights_kernel/pallas_call | solution.py:603
  20.4 0.0 collective-permute-done.2.refs_10_
  20.5 4.5 %collective-permute-done.3.refs_11_ = f32[8,640]{1,0:T(8,128)S(1)} collective-permute-done((f32[8,640]{1,0:T(8,128)S(1)}, f32[8,640]{1,0:T(8,128)S(1)}, u32[]{:S(2)}, u32[]{:S(2)}) %collective-permute-start.3) | collective-permute-done | bytes 20512 | tf_op jit(solution)/shard_map/ppermute | solution.py:647
  24.9 17.6 %main_kernel.1 = (f32[3,64,512]{2,1,0:T(8,128)}, f32[64,512]{1,0:T(8,128)}, f32[16,128]{1,0:T(8,128)S(1)}) custom-call(s32[6]{0:T(128)} %refs_0_.2, f32[6]{0:T(128)} %refs_1_.5, f32[80,640]{1,0:T(8,128)S(1)} %get-tuple-element.28.refs_0_.refs_2_, f32[56,384]{1,0:T(8,128)S(1)} %get-tuple-element.29.refs_1_.refs_3_, ...), custom_call_target="tpu_custom_call" | custom-call | tf_op jit(solution)/shard_map/main_kernel/pallas_call | solution.py:603
  42.5 0.1 collective-permute-start.4
  42.6 1.2 %collective-permute-done.4 = f32[16,128]{1,0:T(8,128)S(1)} collective-permute-done((f32[16,128]{1,0:T(8,128)S(1)}, f32[16,128]{1,0:T(8,128)S(1)}, u32[]{:S(2)}, u32[]{:S(2)}) %collective-permute-start.4) | collective-permute-done | bytes 8224 | tf_op jit(solution)/shard_map/ppermute | solution.py:680
  43.8 3.6 %collective-permute-done.5 = f32[16,128]{1,0:T(8,128)S(1)} collective-permute-done((f32[16,128]{1,0:T(8,128)S(1)}, f32[16,128]{1,0:T(8,128)S(1)}, u32[]{:S(2)}, u32[]{:S(2)}) %collective-permute-start.5) | collective-permute-done | bytes 8224 | tf_op jit(solution)/shard_map/ppermute | solution.py:680
  47.4 4.9 %collective-permute-done.6 = f32[16,128]{1,0:T(8,128)S(1)} collective-permute-done((f32[16,128]{1,0:T(8,128)S(1)}, f32[16,128]{1,0:T(8,128)S(1)}, u32[]{:S(2)}, u32[]{:S(2)}) %collective-permute-start.6) | collective-permute-done | bytes 8224 | tf_op jit(solution)/shard_map/ppermute | solution.py:680
  52.3 3.6 %collective-permute-done.7 = f32[16,128]{1,0:T(8,128)S(1)} collective-permute-done((f32[16,128]{1,0:T(8,128)S(1)}, f32[16,128]{1,0:T(8,128)S(1)}, u32[]{:S(2)}, u32[]{:S(2)}) %collective-permute-start.7) | collective-permute-done | bytes 8224 | tf_op jit(solution)/shard_map/ppermute | solution.py:680
  56.0 4.9 %collective-permute-done.8 = f32[16,128]{1,0:T(8,128)S(1)} collective-permute-done((f32[16,128]{1,0:T(8,128)S(1)}, f32[16,128]{1,0:T(8,128)S(1)}, u32[]{:S(2)}, u32[]{:S(2)}) %collective-permute-start.8) | collective-permute-done | bytes 8224 | tf_op jit(solution)/shard_map/ppermute | solution.py:680
  60.8 3.6 %collective-permute-done.9 = f32[16,128]{1,0:T(8,128)S(1)} collective-permute-done((f32[16,128]{1,0:T(8,128)S(1)}, f32[16,128]{1,0:T(8,128)S(1)}, u32[]{:S(2)}, u32[]{:S(2)}) %collective-permute-start.9) | collective-permute-done | bytes 8224 | tf_op jit(solution)/shard_map/ppermute | solution.py:680
  64.5 2.4 %collective-permute-start.10 = (f32[16,128]{1,0:T(8,128)S(1)}, f32[16,128]{1,0:T(8,128)S(1)}, u32[]{:S(2)}, u32[]{:S(2)}) collective-permute-start(f32[16,128]{1,0:T(8,128)S(1)} %add.26), channel_id=1, source_target_pairs={{0,28},{1,29},{2,30},{3,31},{4,8},{5,9},{6,10},{7,11},{8,4},{9,5},... | collective-permute-start | bytes 24584 | tf_op jit(solution)/shard_map/ppermute | solution.py:680
  66.9 2.5 %collective-permute-done.10 = f32[16,128]{1,0:T(8,128)S(1)} collective-permute-done((f32[16,128]{1,0:T(8,128)S(1)}, f32[16,128]{1,0:T(8,128)S(1)}, u32[]{:S(2)}, u32[]{:S(2)}) %collective-permute-start.10) | collective-permute-done | bytes 8224 | tf_op jit(solution)/shard_map/ppermute | solution.py:680
  69.3 2.3 %collective-permute-start.11 = (f32[16,128]{1,0:T(8,128)S(1)}, f32[16,128]{1,0:T(8,128)S(1)}, u32[]{:S(2)}, u32[]{:S(2)}) collective-permute-start(f32[16,128]{1,0:T(8,128)S(1)} %add.27.refs_0_), channel_id=1, source_target_pairs={{0,12},{1,13},{2,14},{3,15},{4,24},{5,25},{6,26},{7,27},{8,20},{9,... | collective-permute-start | bytes 24584 | tf_op jit(solution)/shard_map/ppermute | solution.py:681
  71.6 3.2 %collective-permute-done.11.refs_1_ = f32[16,128]{1,0:T(8,128)S(1)} collective-permute-done((f32[16,128]{1,0:T(8,128)S(1)}, f32[16,128]{1,0:T(8,128)S(1)}, u32[]{:S(2)}, u32[]{:S(2)}) %collective-permute-start.11) | collective-permute-done | bytes 8224 | tf_op jit(solution)/shard_map/ppermute | solution.py:681
  74.8 0.7 final_kernel.1
  (13 shorter events, 0.0 us)
Async XLA Ops:
  2.5 8.3 %collective-permute-start = (f32[8,128]{1,0:T(8,128)S(1)}, f32[8,128]{1,0:T(8,128)S(1)}, u32[]{:S(2)}, u32[]{:S(2)}) collective-permute-start(f32[8,128]{1,0:T(8,128)S(1)} %get-tuple-element.34), channel_id=1, source_target_pairs={{0,1},{1,2},{2,3},{3,4},{4,5},{5,6},{6,7},{7,8},{8,9},{9,10},{10,1... | collective-permute-start | bytes 12296 | tf_op jit(solution)/shard_map/ppermute | solution.py:630
  2.6 8.2 %collective-permute-start.1 = (f32[8,128]{1,0:T(8,128)S(1)}, f32[8,128]{1,0:T(8,128)S(1)}, u32[]{:S(2)}, u32[]{:S(2)}) collective-permute-start(f32[8,128]{1,0:T(8,128)S(1)} %get-tuple-element.35), channel_id=1, source_target_pairs={{1,0},{2,1},{3,2},{4,3},{5,4},{6,5},{7,6},{8,7},{9,8},{10,9},{11,1... | collective-permute-start | bytes 12296 | tf_op jit(solution)/shard_map/ppermute | solution.py:631
  10.9 9.5 %collective-permute-start.2 = (f32[8,640]{1,0:T(8,128)S(1)}, f32[8,640]{1,0:T(8,128)S(1)}, u32[]{:S(2)}, u32[]{:S(2)}) collective-permute-start(f32[8,640]{1,0:T(8,128)S(1)} %get-tuple-element.37), channel_id=1, source_target_pairs={{0,32},{32,64},{64,96},{96,128},{128,160},{160,192},{192,224},{1,3... | collective-permute-start | bytes 61448 | tf_op jit(solution)/shard_map/ppermute | solution.py:646
  15.7 9.3 %collective-permute-start.3 = (f32[8,640]{1,0:T(8,128)S(1)}, f32[8,640]{1,0:T(8,128)S(1)}, u32[]{:S(2)}, u32[]{:S(2)}) collective-permute-start(f32[8,640]{1,0:T(8,128)S(1)} %get-tuple-element.38), channel_id=1, source_target_pairs={{32,0},{64,32},{96,64},{128,96},{160,128},{192,160},{224,192},{33,... | collective-permute-start | bytes 61448 | tf_op jit(solution)/shard_map/ppermute | solution.py:647
  42.5 1.3 %collective-permute-start.4 = (f32[16,128]{1,0:T(8,128)S(1)}, f32[16,128]{1,0:T(8,128)S(1)}, u32[]{:S(2)}, u32[]{:S(2)}) collective-permute-start(f32[16,128]{1,0:T(8,128)S(1)} %get-tuple-element.49), channel_id=1, source_target_pairs={{0,1},{1,0},{2,3},{3,2},{4,5},{5,4},{6,7},{7,6},{8,9},{9,8},{10,11... | collective-permute-start | bytes 24584 | tf_op jit(solution)/shard_map/ppermute | solution.py:680
  43.8 3.7 %collective-permute-start.5 = (f32[16,128]{1,0:T(8,128)S(1)}, f32[16,128]{1,0:T(8,128)S(1)}, u32[]{:S(2)}, u32[]{:S(2)}) collective-permute-start(f32[16,128]{1,0:T(8,128)S(1)} %add.21), channel_id=1, source_target_pairs={{0,32},{1,33},{2,34},{3,35},{4,36},{5,37},{6,38},{7,39},{8,40},{9,... | collective-permute-start | bytes 24584 | tf_op jit(solution)/shard_map/ppermute | solution.py:680
  47.4 4.9 %collective-permute-start.6 = (f32[16,128]{1,0:T(8,128)S(1)}, f32[16,128]{1,0:T(8,128)S(1)}, u32[]{:S(2)}, u32[]{:S(2)}) collective-permute-start(f32[16,128]{1,0:T(8,128)S(1)} %add.22), channel_id=1, source_target_pairs={{0,96},{1,97},{2,98},{3,99},{4,100},{5,101},{6,102},{7,103},{8,104... | collective-permute-start | bytes 24584 | tf_op jit(solution)/shard_map/ppermute | solution.py:680
  52.3 3.7 %collective-permute-start.7 = (f32[16,128]{1,0:T(8,128)S(1)}, f32[16,128]{1,0:T(8,128)S(1)}, u32[]{:S(2)}, u32[]{:S(2)}) collective-permute-start(f32[16,128]{1,0:T(8,128)S(1)} %add.23), channel_id=1, source_target_pairs={{0,2},{1,3},{2,0},{3,1},{4,6},{5,7},{6,4},{7,5},{8,10},{9,11},{10,... | collective-permute-start | bytes 24584 | tf_op jit(solution)/shard_map/ppermute | solution.py:680
  56.0 4.9 %collective-permute-start.8 = (f32[16,128]{1,0:T(8,128)S(1)}, f32[16,128]{1,0:T(8,128)S(1)}, u32[]{:S(2)}, u32[]{:S(2)}) collective-permute-start(f32[16,128]{1,0:T(8,128)S(1)} %add.24), channel_id=1, source_target_pairs={{0,130},{1,131},{2,128},{3,129},{4,134},{5,135},{6,132},{7,133},{8... | collective-permute-start | bytes 24584 | tf_op jit(solution)/shard_map/ppermute | solution.py:680
  60.8 3.7 %collective-permute-start.9 = (f32[16,128]{1,0:T(8,128)S(1)}, f32[16,128]{1,0:T(8,128)S(1)}, u32[]{:S(2)}, u32[]{:S(2)}) collective-permute-start(f32[16,128]{1,0:T(8,128)S(1)} %add.25), channel_id=1, source_target_pairs={{0,4},{1,5},{2,6},{3,7},{4,0},{5,1},{6,2},{7,3},{8,12},{9,13},{10,... | collective-permute-start | bytes 24584 | tf_op jit(solution)/shard_map/ppermute | solution.py:680
  64.5 4.9 %collective-permute-start.10 = (f32[16,128]{1,0:T(8,128)S(1)}, f32[16,128]{1,0:T(8,128)S(1)}, u32[]{:S(2)}, u32[]{:S(2)}) collective-permute-start(f32[16,128]{1,0:T(8,128)S(1)} %add.26), channel_id=1, source_target_pairs={{0,28},{1,29},{2,30},{3,31},{4,8},{5,9},{6,10},{7,11},{8,4},{9,5},... | collective-permute-start | bytes 24584 | tf_op jit(solution)/shard_map/ppermute | solution.py:680
  69.3 5.4 %collective-permute-start.11 = (f32[16,128]{1,0:T(8,128)S(1)}, f32[16,128]{1,0:T(8,128)S(1)}, u32[]{:S(2)}, u32[]{:S(2)}) collective-permute-start(f32[16,128]{1,0:T(8,128)S(1)} %add.27.refs_0_), channel_id=1, source_target_pairs={{0,12},{1,13},{2,14},{3,15},{4,24},{5,25},{6,26},{7,27},{8,20},{9,... | collective-permute-start | bytes 24584 | tf_op jit(solution)/shard_map/ppermute | solution.py:681

commit v3 on v2

--- a/solution.py
+++ b/solution.py
@@ -27,7 +27,9 @@
 BLOCKS = 9
 BLOCK = 8 * CH
 SLAB = 256
-GROUPS = BLOCK // 16
+HALF = 4 * CH
+PAIR = 2 * CH
+SHORT = 160
 UNITS = 11
 LAST = [(3, 0), (4, 64), (5, 96)]
 EDGE = 32
@@ -189,28 +191,6 @@
         for k, (i, j) in enumerate(STEPS):
             ctx[r, k, (j + 2) * 16 + (r + i + 4)] = 1
     t["ctx"] = ctx
-    for l in range(1, LEVELS):
-        s = 1 << l
-        up_r = np.zeros((72, UPROWS[l]), np.float32)
-        for n in range(72):
-            y = n - 4
-            m, p = y >> l, ((y & (s - 1)) + 0.5) / s - 0.5
-            for e, wgt in ((-1, max(-p, 0)), (0, 1 - abs(p)), (1, max(p, 0))):
-                at = TOP - 8 + m + e
-                if 0 <= at < UPROWS[l]:
-                    up_r[n, at] += wgt
-        up_c = np.zeros((WIDE[l], LANES), np.float32)
-        for n in range(LANES):
-            x = n if n < W + 4 else n - LANES
-            if x < -4:
-                continue
-            m, p = x >> l, ((x & (s - 1)) + 0.5) / s - 0.5
-            for e, wgt in ((-1, max(-p, 0)), (0, 1 - abs(p)), (1, max(p, 0))):
-                q = m + e
-                if -HALO[l] <= q < COLS[l] + HALO[l]:
-                    up_c[q % WIDE[l], n] += wgt
-        t[f"rows{l}"] = np.concatenate([up_r] * 3, axis=1)
-        t[f"cols{l}"] = up_c
     return t
 
 
@@ -230,20 +210,45 @@
     return hi, mid, (rest - mid.astype(F32)).astype(BF16)
 
 
-def conv_weights_kernel(copies, cf, cs, co, spread, place, tap, tap_out, wc1, wc2, wout):
+def hat(shape, level, fine, coarse):
+    place = (fine + 0.5) * (1.0 / (1 << level)) - 0.5
+    return jnp.maximum(1.0 - jnp.abs(place - coarse), 0.0).astype(BF16)
+
+
+def conv_weights_kernel(
+    copies, cf, cs, co, spread, place, tap, tap_out, wc1, wc2, wout, *scales
+):
+    row_scales, col_scales = scales[:5], scales[5:]
+    for level in range(1, LEVELS):
+        count = UPROWS[level]
+        shape = (72, 3 * count)
+        fine = lax.broadcasted_iota(I32, shape, 0) - 4
+        at = lax.broadcasted_iota(I32, shape, 1)
+        at = jnp.where(at >= 2 * count, at - 2 * count, jnp.where(at >= count, at - count, at))
+        row_scales[level - 1][...] = hat(
+            shape, level, fine.astype(F32), (at + (8 - TOP)).astype(F32)
+        )
+        own, wide, h = COLS[level], WIDE[level], HALO[level]
+        for first in range(0, wide, 128):
+            shape = (128, LANES)
+            fine = lax.broadcasted_iota(I32, shape, 1)
+            fine = jnp.where(fine < W + 4, fine, jnp.where(fine >= LANES - 4, fine - LANES, -99999))
+            at = lax.broadcasted_iota(I32, shape, 0) + first
+            at = jnp.where(at < own + h, at, jnp.where(at >= wide - h, at - wide, 99999))
+            col_scales[level - 1][first : first + 128, :] = hat(
+                shape, level, fine.astype(F32), at.astype(F32)
+            )
     settle(copies)
-    grow = spread[...]
-    taps = tap[...].astype(F32)
+    grow = spread[0:HALF, :]
+    short = place[:, 0:SHORT]
+    taps = tap[0:HALF, 0:SHORT].astype(F32)
     for src, dst in ((cf, wc1), (cs, wc2)):
         for b in range(3):
-            total = jnp.zeros((BLOCK, SLAB), F32)
+            total = jnp.zeros((HALF, SHORT), F32)
             for a in range(3):
-                full = dot(dot(grow, src[a, b]).astype(BF16), place[...])
+                full = dot(dot(grow, src[a, b]).astype(BF16), short)
                 total = jnp.where(taps == float(a), full, total)
-            total = total.astype(BF16)
-            for g in range(GROUPS):
-                at = 48 * g + 16 * b
-                dst[at : at + 16, :] = total[16 * g : 16 * g + 16]
+            dst[:, SHORT * b : SHORT * b + SHORT] = total.astype(BF16)
     taps3 = tap_out[...].astype(F32)[0:8]
     for o in range(3):
         rows = [dot(co[o, a], place[...]) for a in range(3)]
@@ -280,7 +285,7 @@
         h, l = dot(hi[rows], sel).astype(BF16), dot(lo[rows], sel).astype(BF16)
         a1[rows, :] = jnp.concatenate([h, h, l], axis=1)
     hi, lo = split2(w2[...])
-    h, l = diag(hi).astype(BF16), diag(lo).astype(BF16)
+    h, l = diag(hi).astype(BF16)[0:PAIR, 0:PAIR], diag(lo).astype(BF16)[0:PAIR, 0:PAIR]
     a2[...] = jnp.concatenate([h, h, l], axis=1)
     hi, lo = split2(w3[...])
     keep = same_out[...].astype(F32)
@@ -319,19 +324,32 @@
     *, pixels, lat,
 ):
     fields = (f0, f1, f2, f3, f4, f5)
-    settle(copies[:2])
     for src, dst in zip((q0, q1, q2, q3, q4, q5), fields):
         dst[...] = src[...]
     place_sides(left[...], right[...], fields)
     place_ends(above, below, fields)
 
+    for n in range(BLOCKS):
+        up[48 * n : 48 * n + 8, :] = f0[8 + 8 * n : 16 + 8 * n, :]
+    for level, ru, cu in ((1, r1, u1), (2, r2, u2), (3, r3, u3), (4, r4, u4), (5, r5, u5)):
+        count = UPROWS[level]
+        grown = dot(jnp.concatenate(split3(fields[level][8 : 8 + count, :]), axis=0), cu[...])
+        grown = (grown[0:count] + grown[count : 2 * count]) + grown[2 * count :]
+        full = dot(ru[...], jnp.concatenate(split3(grown), axis=0))
+        for n in range(BLOCKS):
+            up[48 * n + 8 * level : 48 * n + 8 * level + 8, :] = full[8 * n : 8 * n + 8]
+
     lane = lax.broadcasted_iota(I32, (8, 128), 1)
     row = lax.broadcasted_iota(I32, (8, 128), 0)
 
+    turned = {}
+    for level in range(3):
+        for j in range(-2, 3):
+            rows = fields[level][8 : 24 + ROWS[level] - 8, :]
+            turned[level, j] = pltpu.roll(rows, (-j) % WIDE[level], 1) if j else rows
+
     def turn(level, n, j):
-        slab = fields[level][8 * n + 8 : 8 * n + 24, :]
-        cols, wide = max(COLS[level], 128), WIDE[level]
-        return (slab if j == 0 else pltpu.roll(slab, (-j) % wide, 1))[:, 0:cols]
+        return turned[level, j][8 * n : 8 * n + 16, 0 : max(COLS[level], 128)]
 
     def small(j):
         deep = lax.broadcasted_iota(I32, (16, 128), 1)
@@ -361,6 +379,8 @@
         for j in range(-2, 3)
     ])
 
+    settle(copies[:2])
+
     def cover(level):
         odd = (row + lane + parity[level]) & 1
         plain = jnp.full((8, 128), scale[level], F32)
@@ -379,52 +399,59 @@
     own[UNITS] = jnp.zeros((8, W), F32)
     anchors[UNITS] = jnp.ones((8, W), F32)
 
-    settle(copies[3:])
-    for n in range(BLOCKS):
-        up[48 * n : 48 * n + 8, :] = f0[8 + 8 * n : 16 + 8 * n, :]
-    for level, ru, cu in ((1, r1, u1), (2, r2, u2), (3, r3, u3), (4, r4, u4), (5, r5, u5)):
-        count = UPROWS[level]
-        grown = dot(jnp.concatenate(split3(fields[level][8 : 8 + count, :]), axis=0), cu[...])
-        grown = (grown[0:count] + grown[count : 2 * count]) + grown[2 * count :]
-        full = dot(ru[...], jnp.concatenate(split3(grown), axis=0))
-        for n in range(BLOCKS):
-            up[48 * n + 8 * level : 48 * n + 8 * level + 8, :] = full[8 * n : 8 * n + 8]
-
     end = EDGE + BLOCK * BLOCKS
     for buf in (second, third):
-        buf[0:EDGE, :] = jnp.zeros((EDGE, LANES), BF16)
-        buf[end : end + EDGE, :] = jnp.zeros((EDGE, LANES), BF16)
+        buf[:, 0:EDGE, :] = jnp.zeros((3, EDGE, LANES), BF16)
+        buf[:, end : end + EDGE, :] = jnp.zeros((3, EDGE, LANES), BF16)
     index = lax.axis_index("lat")
 
     def clear(buf):
         @pl.when(index == 0)
         def _():
-            buf[EDGE : EDGE + 96, :] = jnp.zeros((96, LANES), BF16)
+            buf[:, EDGE : EDGE + 96, :] = jnp.zeros((3, 96, LANES), BF16)
 
         @pl.when(index == lat - 1)
         def _():
-            buf[end - 96 : end, :] = jnp.zeros((96, LANES), BF16)
+            buf[:, end - 96 : end, :] = jnp.zeros((3, 96, LANES), BF16)
 
     def block_rows(n):
-        return pl.ds(pl.multiple_of(EDGE + BLOCK * n, 32), BLOCK)
+        return pl.ds(EDGE + BLOCK * n, BLOCK)
 
     def mix(n):
-        u = up[pl.ds(pl.multiple_of(48 * n, 16), 48), :].astype(BF16)
+        u = up[pl.ds(48 * n, 48), :].astype(BF16)
         first = jnp.maximum(dot(wm1[...], u), 0.0).astype(BF16)
-        second[block_rows(n), :] = jnp.maximum(dot(wm2[...], first), 0.0).astype(BF16)
-
-    def conv(src, dst, w, n):
-        slab = src[pl.ds(pl.multiple_of(BLOCK * n, 64), SLAB), :]
-        y = dot(w[...], slab)
-        before = src[block_rows(n), :]
-        out = []
-        for g in range(GROUPS):
-            at = 48 * g
-            c = y[at + 16 : at + 32] + pltpu.roll(y[at : at + 16], 1, 1)
-            c = c + pltpu.roll(y[at + 32 : at + 48], LANES - 1, 1)
-            kept = before[16 * g : 16 * g + 16].astype(F32)
-            out.append((kept + jnp.maximum(c, 0.0)).astype(BF16))
-        dst[block_rows(n), :] = jnp.concatenate(out, axis=0)
+        value = jnp.maximum(dot(wm2[...], first), 0.0).astype(BF16)
+        put(second, block_rows(n), value)
+
+    def put(buf, rows, value):
+        buf[1, rows, :] = value
+        buf[0, rows, :] = pltpu.roll(value, 1, 1)
+        buf[2, rows, :] = pltpu.roll(value, LANES - 1, 1)
+
+    def conv(src, w, n, part):
+        slab = pl.ds(BLOCK * n + HALF * part, SHORT)
+        rows = pl.ds(EDGE + BLOCK * n + HALF * part, HALF)
+        c = dot(w[...], jnp.concatenate([src[b, slab, :] for b in range(3)], axis=0))
+        return rows, (src[1, rows, :].astype(F32) + jnp.maximum(c, 0.0)).astype(BF16)
+
+    def conv_one(n):
+        for part in range(2):
+            rows, value = conv(second, wc1, n, part)
+            put(third, rows, value)
+
+    def conv_two(n):
+        for part in range(2):
+            rows, value = conv(third, wc2, n, part)
+            second[1, rows, :] = value
+
+    def middle(u):
+        for k in range(4):
+            hi = hidden1[u, PAIR * k : PAIR * k + PAIR, :]
+            lo = hidden1[u, BLOCK + PAIR * k : BLOCK + PAIR * k + PAIR, :]
+            out = jnp.maximum(dot(a2[...], jnp.concatenate([hi, lo, hi], axis=0)), 0.0)
+            hi, lo = split2(out)
+            hidden2[u, PAIR * k : PAIR * k + PAIR, :] = hi
+            hidden2[u, BLOCK + PAIR * k : BLOCK + PAIR * k + PAIR, :] = lo
 
     def layer(src, dst, w, u, k):
         hi, lo = src[u, 0:k, :], src[u, k : 2 * k, :]
@@ -447,27 +474,28 @@
             for k in range(4):
                 if k < 3:
                     synth(3 * t + k)
-                entropy(4 * t + k)
+                if 4 * t + k < UNITS:
+                    entropy(4 * t + k)
             return 0
 
-        lax.fori_loop(0, 3, body, 0)
+        for t in range(3):
+            body(t, 0)
 
     run(mix, lambda u: layer(taps, hidden1, a1, u, 80))
     clear(second)
-    run(lambda n: conv(second, third, wc1, n), lambda u: layer(hidden1, hidden2, a2, u, BLOCK))
+    run(conv_one, middle)
     clear(third)
-    run(lambda n: conv(third, second, wc2, n), cost)
+    run(conv_two, cost)
     clear(second)
 
     for n in range(8):
         bits[8 * n : 8 * n + 8, :] = own[n]
-    sq[...] = jnp.zeros(sq.shape, F32)
 
     def output(n):
-        slab = second[pl.ds(pl.multiple_of(BLOCK * n + 96, 32), SLAB), :]
+        slab = second[1, BLOCK * n + 96 : BLOCK * n + 96 + SLAB, :]
         y = dot(wout[...].astype(BF16), slab)
         c = y[24:48] + pltpu.roll(y[0:24], 1, 1) + pltpu.roll(y[48:72], LANES - 1, 1)
-        rows = pl.ds(pl.multiple_of(8 * n, 8), 8)
+        rows = slice(8 * n, 8 * n + 8)
         slopes = []
         total = jnp.zeros((8, W), F32)
         for o in range(3):
@@ -483,23 +511,18 @@
         ).astype(BF16)
         return total
 
-    def outputs(t, _):
-        total = output(4 * t)
-        for k in range(1, 4):
-            total = total + output(4 * t + k)
-        sq[...] += total
-        return 0
-
     settle(copies[2:3])
     send_bits = pltpu.make_async_copy(bits, bits_out, sems.at[0])
     send_bits.start()
-    lax.fori_loop(0, 2, outputs, 0)
+    total = jnp.zeros((8, W), F32)
+    g = jnp.zeros((72, SLAB), F32)
+    for n in range(8):
+        total = total + output(n)
+    for n in range(8):
+        g = g + dot_t(moved[n, 0:72, :], second[1, BLOCK * n + 96 : BLOCK * n + 96 + SLAB, :])
+    sq[...] = total
     send_recon = pltpu.make_async_copy(recon, recon_out, sems.at[1])
     send_recon.start()
-    g = jnp.zeros((72, SLAB), F32)
-    for n in range(8):
-        g = g + dot_t(moved[n, 0:72, :], second[BLOCK * n + 96 : BLOCK * n + 96 + SLAB, :])
-
     sums = [jnp.zeros((8, W), F32)] * 2
     for n in range(8):
         sums[0] = sums[0] + own[n]
@@ -634,7 +657,7 @@
         mix_weights_kernel,
         (
             sds((8, 128), F32), sds((BLOCK, 48), BF16), sds((BLOCK, BLOCK), BF16),
-            sds((BLOCK, 240), BF16), sds((BLOCK, 3 * BLOCK), BF16), sds((16, 3 * BLOCK), BF16),
+            sds((BLOCK, 240), BF16), sds((PAIR, 3 * PAIR), BF16), sds((16, 3 * BLOCK), BF16),
         ),
         [], [HBM] * (5 + len(names)), 8,
         mix_levels.T, mix_hidden, context_in.T, context_mid, context_out, *[table(n) for n in names],
@@ -646,16 +669,18 @@
     above = lax.ppermute(down, "lat", south)
     below = lax.ppermute(up, "lat", [(j, i) for i, j in south])
     names = ("spread", "place", "tap", "tap_out")
-    wc1, wc2, wout = call(
+    wc1, wc2, wout, *scales = call(
         conv_weights_kernel,
-        (sds((3 * BLOCK, SLAB), BF16), sds((3 * BLOCK, SLAB), BF16), sds((72, SLAB), F32)),
+        (sds((HALF, 3 * SHORT), BF16), sds((HALF, 3 * SHORT), BF16), sds((72, SLAB), F32))
+        + tuple(sds((72, 3 * UPROWS[l]), BF16) for l in range(1, LEVELS))
+        + tuple(sds((WIDE[l], LANES), BF16) for l in range(1, LEVELS)),
         [], [HBM] * (3 + len(names)), 8,
         conv_first.transpose(2, 3, 0, 1), conv_second.transpose(2, 3, 0, 1),
         conv_output.transpose(0, 2, 3, 1), *[table(n) for n in names],
     )
 
     pixels = float(3 * H * W * lat * lon)
-    feature = pltpu.VMEM((2 * EDGE + BLOCK * BLOCKS, LANES), BF16)
+    feature = pltpu.VMEM((3, 2 * EDGE + BLOCK * BLOCKS, LANES), BF16)
     hidden = pltpu.VMEM((UNITS + 1, 2 * BLOCK, W), BF16)
     plain = pltpu.VMEM((UNITS + 1, 8, W), F32)
     fields = [pltpu.VMEM((TALL[l], WIDE[l]), F32) for l in range(LEVELS)]
@@ -667,12 +692,11 @@
         + [pltpu.VMEM((48 * BLOCKS, LANES), F32), feature, feature]
         + [pltpu.VMEM((UNITS + 1, 160, W), BF16), hidden, hidden, plain, plain]
         + [pltpu.VMEM((8, 80, LANES), BF16), pltpu.VMEM((8, W), F32)],
-        [SCALARS] * 2 + [VMEM] * 10 + [HBM] + [VMEM] * 8 + [HBM] * 10,
-        32,
+        [SCALARS] * 2 + [VMEM] * 10 + [HBM] + [VMEM] * 18,
+        40,
         anchor_parity, anchor_scale, *quantized, left, right, above, below, target,
         wm1, wm2, wc1, wc2, wout, a1, a2, a3,
-        *[table(f"rows{l}") for l in range(1, LEVELS)],
-        *[table(f"cols{l}") for l in range(1, LEVELS)],
+        *scales,
         out_specs=(HBM, HBM, VMEM),
     )
     steps = pair_steps(lat, lon)

time: 75.7 us -> 71.8 us (0.948)
  Pallas kernels: 24.2 us -> 19.9 us
    pallas_call x6, Pallas kernels: 24.2 us -> 19.9 us  [call(): pl.pallas_call(body, out_shape=outs, in_specs=specs, out_specs=out_specs...]
where the time goes in v3:
time: 71.8 us; the launch traced here: 71.5 us
  waiting for transfers between devices  32.2 us (45%)
  Pallas kernels  19.9 us (28%)
  starting transfers between devices  17.9 us (25%)
  between operations  1.55 us (2%)
    ppermute x7, waiting for transfers between devices, local(): part = part + lax.ppermute(part, ('lat', 'lon'), step)  24.3 us
    pallas_call x6, Pallas kernels, call(): pl.pallas_call(body, out_shape=outs, in_specs=specs, out_specs=out_specs...  19.9 us
    ppermute x1, starting transfers between devices, local(): right = lax.ppermute(to_left, 'lon', [(j, i) for i, j in east])  6.38 us
    ppermute x1, waiting for transfers between devices, local(): below = lax.ppermute(up, 'lat', [(j, i) for i, j in south])  4.73 us
    ppermute x1, starting transfers between devices, local(): above = lax.ppermute(down, 'lat', south)  4.72 us
    ppermute x1, waiting for transfers between devices, local(): other = lax.ppermute(part, ('lat', 'lon'), steps[-1])  3.16 us
    ppermute x7, starting transfers between devices, local(): part = part + lax.ppermute(part, ('lat', 'lon'), step)  2.52 us
    ppermute x1, starting transfers between devices, local(): other = lax.ppermute(part, ('lat', 'lon'), steps[-1])  2.29 us
  transfers between devices with their start and end apart: 12, of which 9 were waited for; matrix products, arithmetic and copies ran while one was open for 0% of the time, Pallas kernels for 6%

profile of v3, /device:TPU:6, one launch (start us, length us, event | category | flops | bytes accessed | tf_op | source)
XLA Modules:
  0.0 71.5 jit_solution(13416738749970899421)
XLA Ops:
  1.3 1.2 %sides_kernel.1 = (f32[8,128]{1,0:T(8,128)S(1)}, f32[8,128]{1,0:T(8,128)S(1)}, f32[80,640]{1,0:T(8,128)S(1)}, f32[56,384]{1,0:T(8,128)S(1)}, f32[40,256]{1,0:T(8...) custom-call(s32[1,1]{1,0:T(1,128)S(6)} %copy.33.refs_0_, f32[64,512]{1,0:T(8,128)} %refs_1_.3, ...), custom_call_target="tpu_custom_call" | custom-call | tf_op jit(solution)/shard_map/sides_kernel/pallas_call | solution.py:626
  2.5 0.1 collective-permute-start
  2.6 6.4 %collective-permute-start.1 = (f32[8,128]{1,0:T(8,128)S(1)}, f32[8,128]{1,0:T(8,128)S(1)}, u32[]{:S(2)}, u32[]{:S(2)}) collective-permute-start(f32[8,128]{1,0:T(8,128)S(1)} %get-tuple-element.45), channel_id=1, source_target_pairs={{1,0},{2,1},{3,2},{4,3},{5,4},{6,5},{7,6},{8,7},{9,8},{10,9},{11,1... | collective-permute-start | bytes 12296 | tf_op jit(solution)/shard_map/ppermute | solution.py:654
  9.0 1.8 %mix_weights_kernel.1 = (f32[8,128]{1,0:T(8,128)S(1)}, bf16[192,48]{1,0:T(8,128)(2,1)S(1)}, bf16[192,192]{1,0:T(8,128)(2,1)S(1)}, bf16[192,240]{1,0:T(8,128)(2,1...) custom-call(bf16[6,24]{1,0:T(8,128)(2,1)} %bitcast.11, bf16[24,24]{1,0:T(8,128)(2,1)} %refs_1_.4, ...), custom_call_target="tpu_custom_call" | custom-call | tf_op jit(solution)/shard_map/mix_weights_kernel/pallas_call | solution.py:626
  10.8 0.0 collective-permute-done.1.refs_7_.refs_9_
  10.8 0.1 ends_kernel.1
  10.9 4.7 %collective-permute-start.2 = (f32[8,640]{1,0:T(8,128)S(1)}, f32[8,640]{1,0:T(8,128)S(1)}, u32[]{:S(2)}, u32[]{:S(2)}) collective-permute-start(f32[8,640]{1,0:T(8,128)S(1)} %get-tuple-element.47), channel_id=1, source_target_pairs={{0,32},{32,64},{64,96},{96,128},{128,160},{160,192},{192,224},{1,3... | collective-permute-start | bytes 61448 | tf_op jit(solution)/shard_map/ppermute | solution.py:669
  15.7 1.9 %collective-permute-start.3 = (f32[8,640]{1,0:T(8,128)S(1)}, f32[8,640]{1,0:T(8,128)S(1)}, u32[]{:S(2)}, u32[]{:S(2)}) collective-permute-start(f32[8,640]{1,0:T(8,128)S(1)} %get-tuple-element.48), channel_id=1, source_target_pairs={{32,0},{64,32},{96,64},{128,96},{160,128},{192,160},{224,192},{33,... | collective-permute-start | bytes 61448 | tf_op jit(solution)/shard_map/ppermute | solution.py:670
  17.6 2.6 %conv_weights_kernel.1 = (bf16[96,480]{1,0:T(8,128)(2,1)S(1)}, bf16[96,480]{1,0:T(8,128)(2,1)S(1)}, f32[72,256]{1,0:T(8,128)S(1)}, bf16[72,144]{1,0:T(8,128)(2,1...) custom-call(bf16[3,3,24,24]{3,2,1,0:T(8,128)(2,1)} %bitcast.7, ...), custom_call_target="tpu_custom_call" | custom-call | tf_op jit(solution)/shard_map/conv_weights_kernel/pallas_call | solution.py:626
  20.2 0.0 collective-permute-done.2.refs_10_
  20.2 4.7 %collective-permute-done.3.refs_11_ = f32[8,640]{1,0:T(8,128)S(1)} collective-permute-done((f32[8,640]{1,0:T(8,128)S(1)}, f32[8,640]{1,0:T(8,128)S(1)}, u32[]{:S(2)}, u32[]{:S(2)}) %collective-permute-start.3) | collective-permute-done | bytes 20512 | tf_op jit(solution)/shard_map/ppermute | solution.py:670
  24.9 13.4 %main_kernel.1 = (f32[3,64,512]{2,1,0:T(8,128)}, f32[64,512]{1,0:T(8,128)}, f32[16,128]{1,0:T(8,128)S(1)}) custom-call(s32[6]{0:T(128)} %refs_0_.2, f32[6]{0:T(128)} %refs_1_.5, f32[80,640]{1,0:T(8,128)S(1)} %get-tuple-element.38.refs_0_.refs_2_, f32[56,384]{1,0:T(8,128)S(1)} %get-tuple-element.39.refs_1_.refs_3_, ...), custom_call_target="tpu_custom_call" | custom-call | tf_op jit(solution)/shard_map/main_kernel/pallas_call | solution.py:626
  38.4 0.1 collective-permute-start.4
  38.5 1.2 %collective-permute-done.4 = f32[16,128]{1,0:T(8,128)S(1)} collective-permute-done((f32[16,128]{1,0:T(8,128)S(1)}, f32[16,128]{1,0:T(8,128)S(1)}, u32[]{:S(2)}, u32[]{:S(2)}) %collective-permute-start.4) | collective-permute-done | bytes 8224 | tf_op jit(solution)/shard_map/ppermute | solution.py:704
  39.6 3.6 %collective-permute-done.5 = f32[16,128]{1,0:T(8,128)S(1)} collective-permute-done((f32[16,128]{1,0:T(8,128)S(1)}, f32[16,128]{1,0:T(8,128)S(1)}, u32[]{:S(2)}, u32[]{:S(2)}) %collective-permute-start.5) | collective-permute-done | bytes 8224 | tf_op jit(solution)/shard_map/ppermute | solution.py:704
  43.3 4.9 %collective-permute-done.6 = f32[16,128]{1,0:T(8,128)S(1)} collective-permute-done((f32[16,128]{1,0:T(8,128)S(1)}, f32[16,128]{1,0:T(8,128)S(1)}, u32[]{:S(2)}, u32[]{:S(2)}) %collective-permute-start.6) | collective-permute-done | bytes 8224 | tf_op jit(solution)/shard_map/ppermute | solution.py:704
  48.2 3.6 %collective-permute-done.7 = f32[16,128]{1,0:T(8,128)S(1)} collective-permute-done((f32[16,128]{1,0:T(8,128)S(1)}, f32[16,128]{1,0:T(8,128)S(1)}, u32[]{:S(2)}, u32[]{:S(2)}) %collective-permute-start.7) | collective-permute-done | bytes 8224 | tf_op jit(solution)/shard_map/ppermute | solution.py:704
  51.8 4.9 %collective-permute-done.8 = f32[16,128]{1,0:T(8,128)S(1)} collective-permute-done((f32[16,128]{1,0:T(8,128)S(1)}, f32[16,128]{1,0:T(8,128)S(1)}, u32[]{:S(2)}, u32[]{:S(2)}) %collective-permute-start.8) | collective-permute-done | bytes 8224 | tf_op jit(solution)/shard_map/ppermute | solution.py:704
  56.7 3.6 %collective-permute-done.9 = f32[16,128]{1,0:T(8,128)S(1)} collective-permute-done((f32[16,128]{1,0:T(8,128)S(1)}, f32[16,128]{1,0:T(8,128)S(1)}, u32[]{:S(2)}, u32[]{:S(2)}) %collective-permute-start.9) | collective-permute-done | bytes 8224 | tf_op jit(solution)/shard_map/ppermute | solution.py:704
  60.3 2.4 %collective-permute-start.10 = (f32[16,128]{1,0:T(8,128)S(1)}, f32[16,128]{1,0:T(8,128)S(1)}, u32[]{:S(2)}, u32[]{:S(2)}) collective-permute-start(f32[16,128]{1,0:T(8,128)S(1)} %add.26), channel_id=1, source_target_pairs={{0,28},{1,29},{2,30},{3,31},{4,8},{5,9},{6,10},{7,11},{8,4},{9,5},... | collective-permute-start | bytes 24584 | tf_op jit(solution)/shard_map/ppermute | solution.py:704
  62.8 2.5 %collective-permute-done.10 = f32[16,128]{1,0:T(8,128)S(1)} collective-permute-done((f32[16,128]{1,0:T(8,128)S(1)}, f32[16,128]{1,0:T(8,128)S(1)}, u32[]{:S(2)}, u32[]{:S(2)}) %collective-permute-start.10) | collective-permute-done | bytes 8224 | tf_op jit(solution)/shard_map/ppermute | solution.py:704
  65.2 2.3 %collective-permute-start.11 = (f32[16,128]{1,0:T(8,128)S(1)}, f32[16,128]{1,0:T(8,128)S(1)}, u32[]{:S(2)}, u32[]{:S(2)}) collective-permute-start(f32[16,128]{1,0:T(8,128)S(1)} %add.27.refs_0_), channel_id=1, source_target_pairs={{0,12},{1,13},{2,14},{3,15},{4,24},{5,25},{6,26},{7,27},{8,20},{9,... | collective-permute-start | bytes 24584 | tf_op jit(solution)/shard_map/ppermute | solution.py:705
  67.5 3.2 %collective-permute-done.11.refs_1_ = f32[16,128]{1,0:T(8,128)S(1)} collective-permute-done((f32[16,128]{1,0:T(8,128)S(1)}, f32[16,128]{1,0:T(8,128)S(1)}, u32[]{:S(2)}, u32[]{:S(2)}) %collective-permute-start.11) | collective-permute-done | bytes 8224 | tf_op jit(solution)/shard_map/ppermute | solution.py:705
  70.7 0.7 final_kernel.1
  (13 shorter events, 0.0 us)
Async XLA Ops:
  2.5 8.3 %collective-permute-start = (f32[8,128]{1,0:T(8,128)S(1)}, f32[8,128]{1,0:T(8,128)S(1)}, u32[]{:S(2)}, u32[]{:S(2)}) collective-permute-start(f32[8,128]{1,0:T(8,128)S(1)} %get-tuple-element.44), channel_id=1, source_target_pairs={{0,1},{1,2},{2,3},{3,4},{4,5},{5,6},{6,7},{7,8},{8,9},{9,10},{10,1... | collective-permute-start | bytes 12296 | tf_op jit(solution)/shard_map/ppermute | solution.py:653
  2.6 8.2 %collective-permute-start.1 = (f32[8,128]{1,0:T(8,128)S(1)}, f32[8,128]{1,0:T(8,128)S(1)}, u32[]{:S(2)}, u32[]{:S(2)}) collective-permute-start(f32[8,128]{1,0:T(8,128)S(1)} %get-tuple-element.45), channel_id=1, source_target_pairs={{1,0},{2,1},{3,2},{4,3},{5,4},{6,5},{7,6},{8,7},{9,8},{10,9},{11,1... | collective-permute-start | bytes 12296 | tf_op jit(solution)/shard_map/ppermute | solution.py:654
  10.9 9.3 %collective-permute-start.2 = (f32[8,640]{1,0:T(8,128)S(1)}, f32[8,640]{1,0:T(8,128)S(1)}, u32[]{:S(2)}, u32[]{:S(2)}) collective-permute-start(f32[8,640]{1,0:T(8,128)S(1)} %get-tuple-element.47), channel_id=1, source_target_pairs={{0,32},{32,64},{64,96},{96,128},{128,160},{160,192},{192,224},{1,3... | collective-permute-start | bytes 61448 | tf_op jit(solution)/shard_map/ppermute | solution.py:669
  15.7 9.3 %collective-permute-start.3 = (f32[8,640]{1,0:T(8,128)S(1)}, f32[8,640]{1,0:T(8,128)S(1)}, u32[]{:S(2)}, u32[]{:S(2)}) collective-permute-start(f32[8,640]{1,0:T(8,128)S(1)} %get-tuple-element.48), channel_id=1, source_target_pairs={{32,0},{64,32},{96,64},{128,96},{160,128},{192,160},{224,192},{33,... | collective-permute-start | bytes 61448 | tf_op jit(solution)/shard_map/ppermute | solution.py:670
  38.4 1.3 %collective-permute-start.4 = (f32[16,128]{1,0:T(8,128)S(1)}, f32[16,128]{1,0:T(8,128)S(1)}, u32[]{:S(2)}, u32[]{:S(2)}) collective-permute-start(f32[16,128]{1,0:T(8,128)S(1)} %get-tuple-element.69), channel_id=1, source_target_pairs={{0,1},{1,0},{2,3},{3,2},{4,5},{5,4},{6,7},{7,6},{8,9},{9,8},{10,11... | collective-permute-start | bytes 24584 | tf_op jit(solution)/shard_map/ppermute | solution.py:704
  39.6 3.7 %collective-permute-start.5 = (f32[16,128]{1,0:T(8,128)S(1)}, f32[16,128]{1,0:T(8,128)S(1)}, u32[]{:S(2)}, u32[]{:S(2)}) collective-permute-start(f32[16,128]{1,0:T(8,128)S(1)} %add.21), channel_id=1, source_target_pairs={{0,32},{1,33},{2,34},{3,35},{4,36},{5,37},{6,38},{7,39},{8,40},{9,... | collective-permute-start | bytes 24584 | tf_op jit(solution)/shard_map/ppermute | solution.py:704
  43.3 4.9 %collective-permute-start.6 = (f32[16,128]{1,0:T(8,128)S(1)}, f32[16,128]{1,0:T(8,128)S(1)}, u32[]{:S(2)}, u32[]{:S(2)}) collective-permute-start(f32[16,128]{1,0:T(8,128)S(1)} %add.22), channel_id=1, source_target_pairs={{0,96},{1,97},{2,98},{3,99},{4,100},{5,101},{6,102},{7,103},{8,104... | collective-permute-start | bytes 24584 | tf_op jit(solution)/shard_map/ppermute | solution.py:704
  48.2 3.7 %collective-permute-start.7 = (f32[16,128]{1,0:T(8,128)S(1)}, f32[16,128]{1,0:T(8,128)S(1)}, u32[]{:S(2)}, u32[]{:S(2)}) collective-permute-start(f32[16,128]{1,0:T(8,128)S(1)} %add.23), channel_id=1, source_target_pairs={{0,2},{1,3},{2,0},{3,1},{4,6},{5,7},{6,4},{7,5},{8,10},{9,11},{10,... | collective-permute-start | bytes 24584 | tf_op jit(solution)/shard_map/ppermute | solution.py:704
  51.8 4.9 %collective-permute-start.8 = (f32[16,128]{1,0:T(8,128)S(1)}, f32[16,128]{1,0:T(8,128)S(1)}, u32[]{:S(2)}, u32[]{:S(2)}) collective-permute-start(f32[16,128]{1,0:T(8,128)S(1)} %add.24), channel_id=1, source_target_pairs={{0,130},{1,131},{2,128},{3,129},{4,134},{5,135},{6,132},{7,133},{8... | collective-permute-start | bytes 24584 | tf_op jit(solution)/shard_map/ppermute | solution.py:704
  56.7 3.7 %collective-permute-start.9 = (f32[16,128]{1,0:T(8,128)S(1)}, f32[16,128]{1,0:T(8,128)S(1)}, u32[]{:S(2)}, u32[]{:S(2)}) collective-permute-start(f32[16,128]{1,0:T(8,128)S(1)} %add.25), channel_id=1, source_target_pairs={{0,4},{1,5},{2,6},{3,7},{4,0},{5,1},{6,2},{7,3},{8,12},{9,13},{10,... | collective-permute-start | bytes 24584 | tf_op jit(solution)/shard_map/ppermute | solution.py:704
  60.3 4.9 %collective-permute-start.10 = (f32[16,128]{1,0:T(8,128)S(1)}, f32[16,128]{1,0:T(8,128)S(1)}, u32[]{:S(2)}, u32[]{:S(2)}) collective-permute-start(f32[16,128]{1,0:T(8,128)S(1)} %add.26), channel_id=1, source_target_pairs={{0,28},{1,29},{2,30},{3,31},{4,8},{5,9},{6,10},{7,11},{8,4},{9,5},... | collective-permute-start | bytes 24584 | tf_op jit(solution)/shard_map/ppermute | solution.py:704
  65.2 5.4 %collective-permute-start.11 = (f32[16,128]{1,0:T(8,128)S(1)}, f32[16,128]{1,0:T(8,128)S(1)}, u32[]{:S(2)}, u32[]{:S(2)}) collective-permute-start(f32[16,128]{1,0:T(8,128)S(1)} %add.27.refs_0_), channel_id=1, source_target_pairs={{0,12},{1,13},{2,14},{3,15},{4,24},{5,25},{6,26},{7,27},{8,20},{9,... | collective-permute-start | bytes 24584 | tf_op jit(solution)/shard_map/ppermute | solution.py:705

commit v4 on v3

--- a/solution.py
+++ b/solution.py
@@ -7,6 +7,7 @@
 from jax.experimental import pallas as pl
 from jax.experimental.pallas import tpu as pltpu
 from jax.sharding import PartitionSpec as P
+
 
 F32, BF16, I32 = jnp.float32, jnp.bfloat16, jnp.int32
 STEPS = (
@@ -110,9 +111,32 @@
     return jnp.where(lane >= 128 - h, pltpu.roll(left, (128 - h - at) % 128, 1), tile)
 
 
+def hat(level, fine, coarse):
+    place = (fine + 0.5) * (1.0 / (1 << level)) - 0.5
+    return jnp.maximum(1.0 - jnp.abs(place - coarse), 0.0).astype(BF16)
+
+
 def sides_kernel(copies, seed, *refs):
-    lats, (to_right, to_left), fields = refs[:6], refs[6:8], refs[8:]
-    settle(copies)
+    lats, (near, far), fields, scales = refs[:6], refs[6:8], refs[8:14], refs[14:]
+    row_scales, col_scales = scales[:5], scales[5:]
+    for level in range(1, LEVELS):
+        count = UPROWS[level]
+        shape = (72, 3 * count)
+        fine = lax.broadcasted_iota(I32, shape, 0) - 4
+        at = lax.broadcasted_iota(I32, shape, 1)
+        at = jnp.where(at >= 2 * count, at - 2 * count, jnp.where(at >= count, at - count, at))
+        row_scales[level - 1][...] = hat(level, fine.astype(F32), (at + (8 - TOP)).astype(F32))
+        own, wide, h = COLS[level], WIDE[level], HALO[level]
+        for first in range(0, wide, 128):
+            shape = (128, LANES)
+            fine = lax.broadcasted_iota(I32, shape, 1)
+            fine = jnp.where(fine < W + 4, fine, jnp.where(fine >= LANES - 4, fine - LANES, -99999))
+            at = lax.broadcasted_iota(I32, shape, 0) + first
+            at = jnp.where(at < own + h, at, jnp.where(at >= wide - h, at - wide, 99999))
+            col_scales[level - 1][first : first + 128, :] = hat(
+                level, fine.astype(F32), at.astype(F32)
+            )
+    settle(copies[:6])
     place_own(lats, seed[0, 0], fields)
     lane = lax.broadcasted_iota(I32, (8, 128), 1)
     right = jnp.zeros((8, 128), F32)
@@ -128,12 +152,20 @@
             first = fields[level][rows, 0:128]
             right = jnp.where(here, pltpu.roll(last, (at - (c - h - base)) % 128, 1), right)
             left = jnp.where(here, pltpu.roll(first, at % 128, 1), left)
-    to_right[...] = right
-    to_left[...] = left
+    odd = (lax.axis_index("lon") & 1) == 1
+    near[...] = jnp.where(odd, left, right)
+    far[...] = jnp.where(odd, right, left)
+    settle(copies[6:])
+
+
+def ordered(axis, near, far):
+    odd = (lax.axis_index(axis) & 1) == 1
+    return jnp.where(odd, near[...], far[...]), jnp.where(odd, far[...], near[...])
 
 
 def ends_kernel(copies, *refs):
-    fields, (left, right), (_, up, down) = refs[:6], refs[6:8], refs[8:]
+    fields, sides, (_, near_out, far_out, up, down) = refs[:6], refs[6:8], refs[8:]
+    left, right = ordered("lon", *sides)
     up[...] = jnp.zeros(up.shape, F32)
     down[...] = jnp.zeros(down.shape, F32)
     for level in range(LEVELS):
@@ -141,7 +173,7 @@
         count = max(1, ROWS[level] // 8)
         base = (own // 128) * 128
         for dst, g, skip in ((up, 0, 0), (down, count - 1, min(8, ROWS[level]) - h)):
-            tile = side_tile(left[...], right[...], level, g)
+            tile = side_tile(left, right, level, g)
             at = TOP + 8 * g + skip
             if base:
                 dst[r : r + h, c : c + base] = fields[level][at : at + h, 0:base]
@@ -150,6 +182,9 @@
                 dst[r : r + h, c : c + 128] = (
                     fields[level][at : at + h, :] + tile[skip : skip + h]
                 )
+    odd = (lax.axis_index("lat") & 1) == 1
+    near_out[...] = jnp.where(odd, up[...], down[...])
+    far_out[...] = jnp.where(odd, down[...], up[...])
 
 
 def slab_row(d, c):
@@ -210,34 +245,9 @@
     return hi, mid, (rest - mid.astype(F32)).astype(BF16)
 
 
-def hat(shape, level, fine, coarse):
-    place = (fine + 0.5) * (1.0 / (1 << level)) - 0.5
-    return jnp.maximum(1.0 - jnp.abs(place - coarse), 0.0).astype(BF16)
-
-
 def conv_weights_kernel(
-    copies, cf, cs, co, spread, place, tap, tap_out, wc1, wc2, wout, *scales
+    copies, cf, cs, co, spread, place, tap, tap_out, wc1, wc2, wout
 ):
-    row_scales, col_scales = scales[:5], scales[5:]
-    for level in range(1, LEVELS):
-        count = UPROWS[level]
-        shape = (72, 3 * count)
-        fine = lax.broadcasted_iota(I32, shape, 0) - 4
-        at = lax.broadcasted_iota(I32, shape, 1)
-        at = jnp.where(at >= 2 * count, at - 2 * count, jnp.where(at >= count, at - count, at))
-        row_scales[level - 1][...] = hat(
-            shape, level, fine.astype(F32), (at + (8 - TOP)).astype(F32)
-        )
-        own, wide, h = COLS[level], WIDE[level], HALO[level]
-        for first in range(0, wide, 128):
-            shape = (128, LANES)
-            fine = lax.broadcasted_iota(I32, shape, 1)
-            fine = jnp.where(fine < W + 4, fine, jnp.where(fine >= LANES - 4, fine - LANES, -99999))
-            at = lax.broadcasted_iota(I32, shape, 0) + first
-            at = jnp.where(at < own + h, at, jnp.where(at >= wide - h, at - wide, 99999))
-            col_scales[level - 1][first : first + 128, :] = hat(
-                shape, level, fine.astype(F32), at.astype(F32)
-            )
     settle(copies)
     grow = spread[0:HALF, :]
     short = place[:, 0:SHORT]
@@ -317,7 +327,7 @@
 
 
 def main_kernel(
-    copies, parity, scale, q0, q1, q2, q3, q4, q5, left, right, above, below, target,
+    copies, parity, scale, q0, q1, q2, q3, q4, q5, side_near, side_far, end_near, end_far, target,
     wm1, wm2, wc1, wc2, wout, a1, a2, a3, r1, r2, r3, r4, r5, u1, u2, u3, u4, u5,
     recon_out, bits_out, part,
     recon, bits, sems, f0, f1, f2, f3, f4, f5, up, second, third, taps, hidden1, hidden2, own, anchors, moved, sq,
@@ -326,8 +336,8 @@
     fields = (f0, f1, f2, f3, f4, f5)
     for src, dst in zip((q0, q1, q2, q3, q4, q5), fields):
         dst[...] = src[...]
-    place_sides(left[...], right[...], fields)
-    place_ends(above, below, fields)
+    place_sides(*ordered("lon", side_near, side_far), fields)
+    place_ends(*ordered("lat", end_near, end_far), fields)
 
     for n in range(BLOCKS):
         up[48 * n : 48 * n + 8, :] = f0[8 + 8 * n : 16 + 8 * n, :]
@@ -428,20 +438,37 @@
         buf[0, rows, :] = pltpu.roll(value, 1, 1)
         buf[2, rows, :] = pltpu.roll(value, LANES - 1, 1)
 
-    def conv(src, w, n, part):
-        slab = pl.ds(BLOCK * n + HALF * part, SHORT)
-        rows = pl.ds(EDGE + BLOCK * n + HALF * part, HALF)
-        c = dot(w[...], jnp.concatenate([src[b, slab, :] for b in range(3)], axis=0))
-        return rows, (src[1, rows, :].astype(F32) + jnp.maximum(c, 0.0)).astype(BF16)
+    def conv(src, w, n):
+        taps_of = []
+        for part in range(2):
+            at = BLOCK * n + HALF * part
+            taps_of.append([src[b, at : at + SHORT, :] for b in range(3)])
+        main = [dot(w[...], jnp.concatenate([t[:, 0:W] for t in taps], axis=0)) for taps in taps_of]
+        edge = dot(
+            w[...],
+            jnp.concatenate(
+                [
+                    jnp.concatenate([taps_of[0][b][:, W:], taps_of[1][b][:, W:]], axis=1)
+                    for b in range(3)
+                ],
+                axis=0,
+            ),
+        )
+        out = []
+        for part in range(2):
+            at = EDGE + BLOCK * n + HALF * part
+            rows = pl.ds(at, HALF)
+            tail = edge[:, (LANES - W) * part : (LANES - W) * (part + 1)]
+            c = jnp.concatenate([main[part], tail], axis=1)
+            out.append((rows, (src[1, rows, :].astype(F32) + jnp.maximum(c, 0.0)).astype(BF16)))
+        return out
 
     def conv_one(n):
-        for part in range(2):
-            rows, value = conv(second, wc1, n, part)
+        for rows, value in conv(second, wc1, n):
             put(third, rows, value)
 
     def conv_two(n):
-        for part in range(2):
-            rows, value = conv(third, wc2, n, part)
+        for rows, value in conv(third, wc2, n):
             second[1, rows, :] = value
 
     def middle(u):
@@ -470,7 +497,7 @@
         own[u] = laplace(own[u], centre, jnp.where(anchor, plain, 0.1 + soft))
 
     def run(synth, entropy):
-        def body(t, _):
+        def body(t):
             for k in range(4):
                 if k < 3:
                     synth(3 * t + k)
@@ -479,7 +506,7 @@
             return 0
 
         for t in range(3):
-            body(t, 0)
+            body(t)
 
     run(mix, lambda u: layer(taps, hidden1, a1, u, 80))
     clear(second)
@@ -601,28 +628,34 @@
     return steps
 
 
-def call(kernel, outs, scratch, specs, mib, *args, out_specs=None):
+def call(kernel, outs, scratch, specs, mib, *args, out_specs=None, forward=()):
+    own = len(args)
+    args = args + tuple(forward)
+    specs = specs + [HBM] * len(forward)
+    outs = outs + tuple(jax.ShapeDtypeStruct(a.shape, a.dtype) for a in forward)
     held = [i for i, spec in enumerate(specs) if spec is HBM or spec is SCALARS]
     many = len(jax.tree.leaves(outs))
 
     def body(*refs):
         args_in, rest = list(refs[: len(specs)]), refs[len(specs) :]
         outs_in, work = rest[:many], rest[many:]
-        bufs, sems, work = work[: len(held)], work[len(held)], work[len(held) + 1 :]
+        bufs, sems, work = work[: inner], work[inner], work[inner + 1 :]
+        bufs = list(bufs) + list(outs_in[many - len(forward) :])
         copies = []
         for k, i in enumerate(held):
             copy = pltpu.make_async_copy(args_in[i], bufs[k], sems.at[k])
             copy.start()
             copies.append(copy)
             args_in[i] = bufs[k]
-        kernel(copies, *args_in, *outs_in, *work)
+        kernel(copies, *args_in[:own], *outs_in[: many - len(forward)], *work)
 
     args = [
         pltpu.with_memory_space_constraint(a, pltpu.HBM) if spec is HBM or spec is SCALARS else a
         for a, spec in zip(args, specs)
     ]
     space = {i: pltpu.SMEM if specs[i] is SCALARS else pltpu.VMEM for i in held}
-    buffers = [space[i](args[i].shape, args[i].dtype) for i in held]
+    buffers = [space[i](args[i].shape, args[i].dtype) for i in held if i < own]
+    inner = len(buffers)
     return pl.pallas_call(
         body,
         out_shape=outs,
@@ -630,7 +663,6 @@
         out_specs=out_specs or jax.tree.map(lambda _: VMEM, outs),
         scratch_shapes=buffers + [pltpu.SemaphoreType.DMA((max(1, len(held)),))] + list(scratch),
         compiler_params=pltpu.CompilerParams(vmem_limit_bytes=mib * 1024 * 1024),
-        name=getattr(kernel, "func", kernel).__name__,
     )(*args)
 
 
@@ -645,38 +677,49 @@
     sds = jax.ShapeDtypeStruct
     packs = (sds((8, LANES), F32),) * 2
     whole = tuple(sds((TALL[l], WIDE[l]), F32) for l in range(LEVELS))
-    to_right, to_left, *quantized = call(
-        sides_kernel, (sds((8, 128), F32),) * 2 + whole, [], [SMEM] + [HBM] * 6, 4,
-        tile_seeds, *lats,
+    first = ("spread", "gather", "same", "same_out", "levels", "rowof", "ctx")
+    second = ("spread", "place", "tap", "tap_out")
+    names = first + second[1:]
+    side_near, side_far, *made = call(
+        sides_kernel,
+        (sds((8, 128), F32),) * 2
+        + whole
+        + tuple(sds((72, 3 * UPROWS[l]), BF16) for l in range(1, LEVELS))
+        + tuple(sds((WIDE[l], LANES), BF16) for l in range(1, LEVELS)),
+        [], [SMEM] + [HBM] * 6, 8, tile_seeds, *lats,
+        forward=(
+            mix_levels.T, mix_hidden, context_in.T, context_mid, context_out,
+            conv_first.transpose(2, 3, 0, 1), conv_second.transpose(2, 3, 0, 1),
+            conv_output.transpose(0, 2, 3, 1),
+        )
+        + tuple(table(n) for n in names),
     )
-    east = [(i, (i + 1) % lon) for i in range(lon)]
-    left = lax.ppermute(to_right, "lon", east)
-    right = lax.ppermute(to_left, "lon", [(j, i) for i, j in east])
-    names = ("spread", "gather", "same", "same_out", "levels", "rowof", "ctx")
+    quantized, scales, params = made[:6], made[6:16], made[16:24]
+    held = dict(zip(names, made[24:]))
+    pair = [(i, i ^ 1) for i in range(lon)]
+    other = [(i, (i + 1) % lon if i & 1 else (i - 1) % lon) for i in range(lon)]
+    side_far = lax.ppermute(side_far, "lon", other)
+    side_near = lax.ppermute(side_near, "lon", pair)
     token, wm1, wm2, a1, a2, a3 = call(
         mix_weights_kernel,
         (
             sds((8, 128), F32), sds((BLOCK, 48), BF16), sds((BLOCK, BLOCK), BF16),
             sds((BLOCK, 240), BF16), sds((PAIR, 3 * PAIR), BF16), sds((16, 3 * BLOCK), BF16),
         ),
-        [], [HBM] * (5 + len(names)), 8,
-        mix_levels.T, mix_hidden, context_in.T, context_mid, context_out, *[table(n) for n in names],
+        [], [VMEM] * (5 + len(first)), 4, *params[:5], *[held[n] for n in first],
     )
-    up, down = call(
-        ends_kernel, packs, [], [VMEM] * 9, 4, *quantized, left, right, token,
+    end_near, end_far = call(
+        ends_kernel, packs, [pltpu.VMEM((8, LANES), F32)] * 2, [VMEM] * 9, 4,
+        *quantized, side_near, side_far, token,
     )
-    south = [(i, i + 1) for i in range(lat - 1)]
-    above = lax.ppermute(down, "lat", south)
-    below = lax.ppermute(up, "lat", [(j, i) for i, j in south])
-    names = ("spread", "place", "tap", "tap_out")
-    wc1, wc2, wout, *scales = call(
+    pair = [(i, i ^ 1) for i in range(lat)]
+    other = [(i, i + 1 if i & 1 else i - 1) for i in range(1, lat - 1)]
+    end_far = lax.ppermute(end_far, "lat", other)
+    end_near = lax.ppermute(end_near, "lat", pair)
+    wc1, wc2, wout = call(
         conv_weights_kernel,
-        (sds((HALF, 3 * SHORT), BF16), sds((HALF, 3 * SHORT), BF16), sds((72, SLAB), F32))
-        + tuple(sds((72, 3 * UPROWS[l]), BF16) for l in range(1, LEVELS))
-        + tuple(sds((WIDE[l], LANES), BF16) for l in range(1, LEVELS)),
-        [], [HBM] * (3 + len(names)), 8,
-        conv_first.transpose(2, 3, 0, 1), conv_second.transpose(2, 3, 0, 1),
-        conv_output.transpose(0, 2, 3, 1), *[table(n) for n in names],
+        (sds((HALF, 3 * SHORT), BF16), sds((HALF, 3 * SHORT), BF16), sds((72, SLAB), F32)),
+        [], [VMEM] * (3 + len(second)), 4, *params[5:], *[held[n] for n in second],
     )
 
     pixels = float(3 * H * W * lat * lon)
@@ -694,7 +737,7 @@
         + [pltpu.VMEM((8, 80, LANES), BF16), pltpu.VMEM((8, W), F32)],
         [SCALARS] * 2 + [VMEM] * 10 + [HBM] + [VMEM] * 18,
         40,
-        anchor_parity, anchor_scale, *quantized, left, right, above, below, target,
+        anchor_parity, anchor_scale, *quantized, side_near, side_far, end_near, end_far, target,
         wm1, wm2, wc1, wc2, wout, a1, a2, a3,
         *scales,
         out_specs=(HBM, HBM, VMEM),

time: 71.8 us -> 68 us (0.947)
  Pallas kernels: 19.9 us -> 17.7 us
  starting transfers between devices: 17.9 us -> 16.5 us
    pallas_call x6, Pallas kernels: 19.9 us -> 17.7 us  [call(): pl.pallas_call(body, out_shape=outs, in_specs=specs, out_specs=out_specs...]
    ppermute x4, waiting for transfers between devices: 4.73 us -> 2.94 us  [the longest x1 2.33 us: local(): end_far = lax.ppermute(end_far, 'lat', other)]
    ppermute x7, starting transfers between devices: 2.52 us -> 1.66 us  [local(): part = part + lax.ppermute(part, ('lat', 'lon'), step)]
    ppermute x7, waiting for transfers between devices: 24.3 us -> 25.1 us  [local(): part = part + lax.ppermute(part, ('lat', 'lon'), step)]
    ppermute x1, starting transfers between devices: 2.29 us -> 1.44 us  [local(): other = lax.ppermute(part, ('lat', 'lon'), steps[-1])]
    ppermute x1, waiting for transfers between devices: 3.16 us -> 4.01 us  [local(): other = lax.ppermute(part, ('lat', 'lon'), steps[-1])]
  transfers between devices with their start and end apart: 12 -> 12, of which waited for: 9 -> 10; matrix products, arithmetic and copies ran while one was open for 0% -> 0% of each run, Pallas kernels for 6% -> 3%
where the time goes in v4:
time: 68 us; the launch traced here: 67.8 us
  waiting for transfers between devices  32.1 us (47%)
  Pallas kernels  17.7 us (26%)
  starting transfers between devices  16.5 us (24%)
  between operations  1.54 us (2%)
    ppermute x7, waiting for transfers between devices, local(): part = part + lax.ppermute(part, ('lat', 'lon'), step)  25.1 us
    pallas_call x6, Pallas kernels, call(): pl.pallas_call(body, out_shape=outs, in_specs=specs, out_specs=out_specs...  17.7 us
    ppermute x1, starting transfers between devices, local(): side_far = lax.ppermute(side_far, 'lon', other)  6.97 us
    ppermute x1, starting transfers between devices, local(): end_far = lax.ppermute(end_far, 'lat', other)  5.37 us
    ppermute x1, waiting for transfers between devices, local(): other = lax.ppermute(part, ('lat', 'lon'), steps[-1])  4.01 us
    ppermute x1, waiting for transfers between devices, local(): end_far = lax.ppermute(end_far, 'lat', other)  2.33 us
    ppermute x7, starting transfers between devices, local(): part = part + lax.ppermute(part, ('lat', 'lon'), step)  1.66 us
    ppermute x1, starting transfers between devices, local(): other = lax.ppermute(part, ('lat', 'lon'), steps[-1])  1.44 us
  transfers between devices with their start and end apart: 12, of which 10 were waited for; matrix products, arithmetic and copies ran while one was open for 0% of the time, Pallas kernels for 3%

profile of v4, /device:TPU:6, one launch (start us, length us, event | category | flops | bytes accessed | tf_op | source)
XLA Modules:
  0.0 67.8 jit_solution(16449598859781548486)
XLA Ops:
  1.3 1.5 %shard_map.291 = (f32[8,128]{1,0:T(8,128)S(1)}, f32[8,128]{1,0:T(8,128)S(1)}, f32[80,640]{1,0:T(8,128)S(1)}, f32[56,384]{1,0:T(8,128)S(1)}, f32[40,256]{1,0:T(8,...) custom-call(s32[1,1]{1,0:T(1,128)S(6)} %copy.32.refs_0_, ...), custom_call_target="tpu_custom_call" | custom-call | tf_op jit(solution)/shard_map/pallas_call | solution.py:659
  2.8 0.1 collective-permute-start
  2.9 7.0 %collective-permute-start.1 = (f32[8,128]{1,0:T(8,128)S(1)}, f32[8,128]{1,0:T(8,128)S(1)}, u32[]{:S(2)}, u32[]{:S(2)}) collective-permute-start(f32[8,128]{1,0:T(8,128)S(1)} %get-tuple-element.63), channel_id=1, source_target_pairs={{0,31},{1,2},{2,1},{3,4},{4,3},{5,6},{6,5},{7,8},{8,7},{9,10},{10,... | collective-permute-start | bytes 12296 | tf_op jit(solution)/shard_map/ppermute | solution.py:701
  9.9 0.7 %shard_map.292 = (f32[8,128]{1,0:T(8,128)S(1)}, bf16[192,48]{1,0:T(8,128)(2,1)S(1)}, bf16[192,192]{1,0:T(8,128)(2,1)S(1)}, bf16[192,240]{1,0:T(8,128)(2,1)S(1)},...) custom-call(bf16[6,24]{1,0:T(8,128)(2,1)S(1)} %get-tuple-element.64.refs_0_, ...), custom_call_target="tpu_custom_call" | custom-call | tf_op jit(solution)/shard_map/pallas_call | solution.py:659
  10.6 0.6 collective-permute-done.1.refs_7_.refs_9_
  11.2 0.1 shard_map.293
  11.3 0.9 %collective-permute-start.2 = (f32[8,640]{1,0:T(8,128)S(1)}, f32[8,640]{1,0:T(8,128)S(1)}, u32[]{:S(2)}, u32[]{:S(2)}) collective-permute-start(f32[8,640]{1,0:T(8,128)S(1)} %get-tuple-element.77), channel_id=1, source_target_pairs={{0,32},{32,0},{64,96},{96,64},{128,160},{160,128},{192,224},{224,1... | collective-permute-start | bytes 61448 | tf_op jit(solution)/shard_map/ppermute | solution.py:718
  12.3 5.4 %collective-permute-start.3 = (f32[8,640]{1,0:T(8,128)S(1)}, f32[8,640]{1,0:T(8,128)S(1)}, u32[]{:S(2)}, u32[]{:S(2)}) collective-permute-start(f32[8,640]{1,0:T(8,128)S(1)} %get-tuple-element.78), channel_id=1, source_target_pairs={{32,64},{64,32},{96,128},{128,96},{160,192},{192,160},{33,65},{65,... | collective-permute-start | bytes 61448 | tf_op jit(solution)/shard_map/ppermute | solution.py:717
  17.6 1.5 %shard_map.294 = (bf16[96,480]{1,0:T(8,128)(2,1)S(1)}, bf16[96,480]{1,0:T(8,128)(2,1)S(1)}, f32[72,256]{1,0:T(8,128)S(1)}) custom-call(bf16[3,3,24,24]{3,2,1,0:T(8,128)(2,1)S(1)} %get-tuple-element.81.refs_0_, bf16[3,3,24,24]{3,2,1,0:T(8,128)(2,1)S(1)} %get-tuple-element.82.refs_1_, bf16[3,3,3,24]{3,2,1,0:T(4,128)(2,1)S(1)} %get-tuple-element.83.refs_2_, ...), custom_call_target="tpu_custom_call" | custom-call | tf_op jit(solution)/shard_map/pallas_call | solution.py:659
  19.2 0.0 collective-permute-done.2.refs_10_
  19.2 2.3 %collective-permute-done.3.refs_11_ = f32[8,640]{1,0:T(8,128)S(1)} collective-permute-done((f32[8,640]{1,0:T(8,128)S(1)}, f32[8,640]{1,0:T(8,128)S(1)}, u32[]{:S(2)}, u32[]{:S(2)}) %collective-permute-start.3) | collective-permute-done | bytes 20512 | tf_op jit(solution)/shard_map/ppermute | solution.py:717
  21.5 13.1 %shard_map.295 = (f32[3,64,512]{2,1,0:T(8,128)}, f32[64,512]{1,0:T(8,128)}, f32[16,128]{1,0:T(8,128)S(1)}) custom-call(s32[6]{0:T(128)} %refs_0_.2, f32[6]{0:T(128)} %refs_1_.3, f32[80,640]{1,0:T(8,128)S(1)} %get-tuple-element.56.refs_0_.refs_2_, f32[56,384]{1,0:T(8,128)S(1)} %get-tuple-element.57.refs_1_.refs_3_, ...), custom_call_target="tpu_custom_call" | custom-call | tf_op jit(solution)/shard_map/pallas_call | solution.py:659
  34.7 0.1 collective-permute-start.4
  34.8 1.2 %collective-permute-done.4 = f32[16,128]{1,0:T(8,128)S(1)} collective-permute-done((f32[16,128]{1,0:T(8,128)S(1)}, f32[16,128]{1,0:T(8,128)S(1)}, u32[]{:S(2)}, u32[]{:S(2)}) %collective-permute-start.4) | collective-permute-done | bytes 8224 | tf_op jit(solution)/shard_map/ppermute | solution.py:747
  36.0 3.6 %collective-permute-done.5 = f32[16,128]{1,0:T(8,128)S(1)} collective-permute-done((f32[16,128]{1,0:T(8,128)S(1)}, f32[16,128]{1,0:T(8,128)S(1)}, u32[]{:S(2)}, u32[]{:S(2)}) %collective-permute-start.5) | collective-permute-done | bytes 8224 | tf_op jit(solution)/shard_map/ppermute | solution.py:747
  39.6 4.9 %collective-permute-done.6 = f32[16,128]{1,0:T(8,128)S(1)} collective-permute-done((f32[16,128]{1,0:T(8,128)S(1)}, f32[16,128]{1,0:T(8,128)S(1)}, u32[]{:S(2)}, u32[]{:S(2)}) %collective-permute-start.6) | collective-permute-done | bytes 8224 | tf_op jit(solution)/shard_map/ppermute | solution.py:747
  44.5 3.6 %collective-permute-done.7 = f32[16,128]{1,0:T(8,128)S(1)} collective-permute-done((f32[16,128]{1,0:T(8,128)S(1)}, f32[16,128]{1,0:T(8,128)S(1)}, u32[]{:S(2)}, u32[]{:S(2)}) %collective-permute-start.7) | collective-permute-done | bytes 8224 | tf_op jit(solution)/shard_map/ppermute | solution.py:747
  48.1 4.9 %collective-permute-done.8 = f32[16,128]{1,0:T(8,128)S(1)} collective-permute-done((f32[16,128]{1,0:T(8,128)S(1)}, f32[16,128]{1,0:T(8,128)S(1)}, u32[]{:S(2)}, u32[]{:S(2)}) %collective-permute-start.8) | collective-permute-done | bytes 8224 | tf_op jit(solution)/shard_map/ppermute | solution.py:747
  53.0 3.6 %collective-permute-done.9 = f32[16,128]{1,0:T(8,128)S(1)} collective-permute-done((f32[16,128]{1,0:T(8,128)S(1)}, f32[16,128]{1,0:T(8,128)S(1)}, u32[]{:S(2)}, u32[]{:S(2)}) %collective-permute-start.9) | collective-permute-done | bytes 8224 | tf_op jit(solution)/shard_map/ppermute | solution.py:747
  56.7 1.6 %collective-permute-start.10 = (f32[16,128]{1,0:T(8,128)S(1)}, f32[16,128]{1,0:T(8,128)S(1)}, u32[]{:S(2)}, u32[]{:S(2)}) collective-permute-start(f32[16,128]{1,0:T(8,128)S(1)} %add.26), channel_id=1, source_target_pairs={{0,28},{1,29},{2,30},{3,31},{4,8},{5,9},{6,10},{7,11},{8,4},{9,5},... | collective-permute-start | bytes 24584 | tf_op jit(solution)/shard_map/ppermute | solution.py:747
  58.2 3.3 %collective-permute-done.10 = f32[16,128]{1,0:T(8,128)S(1)} collective-permute-done((f32[16,128]{1,0:T(8,128)S(1)}, f32[16,128]{1,0:T(8,128)S(1)}, u32[]{:S(2)}, u32[]{:S(2)}) %collective-permute-start.10) | collective-permute-done | bytes 8224 | tf_op jit(solution)/shard_map/ppermute | solution.py:747
  61.5 1.4 %collective-permute-start.11 = (f32[16,128]{1,0:T(8,128)S(1)}, f32[16,128]{1,0:T(8,128)S(1)}, u32[]{:S(2)}, u32[]{:S(2)}) collective-permute-start(f32[16,128]{1,0:T(8,128)S(1)} %add.27.refs_0_), channel_id=1, source_target_pairs={{0,12},{1,13},{2,14},{3,15},{4,24},{5,25},{6,26},{7,27},{8,20},{9,... | collective-permute-start | bytes 24584 | tf_op jit(solution)/shard_map/ppermute | solution.py:748
  63.0 4.0 %collective-permute-done.11.refs_1_ = f32[16,128]{1,0:T(8,128)S(1)} collective-permute-done((f32[16,128]{1,0:T(8,128)S(1)}, f32[16,128]{1,0:T(8,128)S(1)}, u32[]{:S(2)}, u32[]{:S(2)}) %collective-permute-start.11) | collective-permute-done | bytes 8224 | tf_op jit(solution)/shard_map/ppermute | solution.py:748
  67.0 0.7 %shard_map.296 = (f32[1,7]{1,0:T(1,128)}, f32[3,3,3,24]{3,2,1,0:T(4,128)}) custom-call(f32[16,128]{1,0:T(8,128)S(1)} %add.27.refs_0_, f32[16,128]{1,0:T(8,128)S(1)} %collective-permute-done.11.refs_1_), custom_call_target="tpu_custom_call" | custom-call | tf_op jit(solution)/shard_map/pallas_call | solution.py:659
  (13 shorter events, 0.0 us)
Async XLA Ops:
  2.8 7.8 %collective-permute-start = (f32[8,128]{1,0:T(8,128)S(1)}, f32[8,128]{1,0:T(8,128)S(1)}, u32[]{:S(2)}, u32[]{:S(2)}) collective-permute-start(f32[8,128]{1,0:T(8,128)S(1)} %get-tuple-element.62), channel_id=1, source_target_pairs={{0,1},{1,0},{2,3},{3,2},{4,5},{5,4},{6,7},{7,6},{8,9},{9,8},{10,11... | collective-permute-start | bytes 12296 | tf_op jit(solution)/shard_map/ppermute | solution.py:702
  2.9 8.3 %collective-permute-start.1 = (f32[8,128]{1,0:T(8,128)S(1)}, f32[8,128]{1,0:T(8,128)S(1)}, u32[]{:S(2)}, u32[]{:S(2)}) collective-permute-start(f32[8,128]{1,0:T(8,128)S(1)} %get-tuple-element.63), channel_id=1, source_target_pairs={{0,31},{1,2},{2,1},{3,4},{4,3},{5,6},{6,5},{7,8},{8,7},{9,10},{10,... | collective-permute-start | bytes 12296 | tf_op jit(solution)/shard_map/ppermute | solution.py:701
  11.3 7.9 %collective-permute-start.2 = (f32[8,640]{1,0:T(8,128)S(1)}, f32[8,640]{1,0:T(8,128)S(1)}, u32[]{:S(2)}, u32[]{:S(2)}) collective-permute-start(f32[8,640]{1,0:T(8,128)S(1)} %get-tuple-element.77), channel_id=1, source_target_pairs={{0,32},{32,0},{64,96},{96,64},{128,160},{160,128},{192,224},{224,1... | collective-permute-start | bytes 61448 | tf_op jit(solution)/shard_map/ppermute | solution.py:718
  12.3 9.3 %collective-permute-start.3 = (f32[8,640]{1,0:T(8,128)S(1)}, f32[8,640]{1,0:T(8,128)S(1)}, u32[]{:S(2)}, u32[]{:S(2)}) collective-permute-start(f32[8,640]{1,0:T(8,128)S(1)} %get-tuple-element.78), channel_id=1, source_target_pairs={{32,64},{64,32},{96,128},{128,96},{160,192},{192,160},{33,65},{65,... | collective-permute-start | bytes 61448 | tf_op jit(solution)/shard_map/ppermute | solution.py:717
  34.7 1.3 %collective-permute-start.4 = (f32[16,128]{1,0:T(8,128)S(1)}, f32[16,128]{1,0:T(8,128)S(1)}, u32[]{:S(2)}, u32[]{:S(2)}) collective-permute-start(f32[16,128]{1,0:T(8,128)S(1)} %get-tuple-element.105), channel_id=1, source_target_pairs={{0,1},{1,0},{2,3},{3,2},{4,5},{5,4},{6,7},{7,6},{8,9},{9,8},{10,11... | collective-permute-start | bytes 24584 | tf_op jit(solution)/shard_map/ppermute | solution.py:747
  36.0 3.7 %collective-permute-start.5 = (f32[16,128]{1,0:T(8,128)S(1)}, f32[16,128]{1,0:T(8,128)S(1)}, u32[]{:S(2)}, u32[]{:S(2)}) collective-permute-start(f32[16,128]{1,0:T(8,128)S(1)} %add.21), channel_id=1, source_target_pairs={{0,32},{1,33},{2,34},{3,35},{4,36},{5,37},{6,38},{7,39},{8,40},{9,... | collective-permute-start | bytes 24584 | tf_op jit(solution)/shard_map/ppermute | solution.py:747
  39.6 4.9 %collective-permute-start.6 = (f32[16,128]{1,0:T(8,128)S(1)}, f32[16,128]{1,0:T(8,128)S(1)}, u32[]{:S(2)}, u32[]{:S(2)}) collective-permute-start(f32[16,128]{1,0:T(8,128)S(1)} %add.22), channel_id=1, source_target_pairs={{0,96},{1,97},{2,98},{3,99},{4,100},{5,101},{6,102},{7,103},{8,104... | collective-permute-start | bytes 24584 | tf_op jit(solution)/shard_map/ppermute | solution.py:747
  44.5 3.7 %collective-permute-start.7 = (f32[16,128]{1,0:T(8,128)S(1)}, f32[16,128]{1,0:T(8,128)S(1)}, u32[]{:S(2)}, u32[]{:S(2)}) collective-permute-start(f32[16,128]{1,0:T(8,128)S(1)} %add.23), channel_id=1, source_target_pairs={{0,2},{1,3},{2,0},{3,1},{4,6},{5,7},{6,4},{7,5},{8,10},{9,11},{10,... | collective-permute-start | bytes 24584 | tf_op jit(solution)/shard_map/ppermute | solution.py:747
  48.1 4.9 %collective-permute-start.8 = (f32[16,128]{1,0:T(8,128)S(1)}, f32[16,128]{1,0:T(8,128)S(1)}, u32[]{:S(2)}, u32[]{:S(2)}) collective-permute-start(f32[16,128]{1,0:T(8,128)S(1)} %add.24), channel_id=1, source_target_pairs={{0,130},{1,131},{2,128},{3,129},{4,134},{5,135},{6,132},{7,133},{8... | collective-permute-start | bytes 24584 | tf_op jit(solution)/shard_map/ppermute | solution.py:747
  53.0 3.7 %collective-permute-start.9 = (f32[16,128]{1,0:T(8,128)S(1)}, f32[16,128]{1,0:T(8,128)S(1)}, u32[]{:S(2)}, u32[]{:S(2)}) collective-permute-start(f32[16,128]{1,0:T(8,128)S(1)} %add.25), channel_id=1, source_target_pairs={{0,4},{1,5},{2,6},{3,7},{4,0},{5,1},{6,2},{7,3},{8,12},{9,13},{10,... | collective-permute-start | bytes 24584 | tf_op jit(solution)/shard_map/ppermute | solution.py:747
  56.7 4.9 %collective-permute-start.10 = (f32[16,128]{1,0:T(8,128)S(1)}, f32[16,128]{1,0:T(8,128)S(1)}, u32[]{:S(2)}, u32[]{:S(2)}) collective-permute-start(f32[16,128]{1,0:T(8,128)S(1)} %add.26), channel_id=1, source_target_pairs={{0,28},{1,29},{2,30},{3,31},{4,8},{5,9},{6,10},{7,11},{8,4},{9,5},... | collective-permute-start | bytes 24584 | tf_op jit(solution)/shard_map/ppermute | solution.py:747
  61.5 5.4 %collective-permute-start.11 = (f32[16,128]{1,0:T(8,128)S(1)}, f32[16,128]{1,0:T(8,128)S(1)}, u32[]{:S(2)}, u32[]{:S(2)}) collective-permute-start(f32[16,128]{1,0:T(8,128)S(1)} %add.27.refs_0_), channel_id=1, source_target_pairs={{0,12},{1,13},{2,14},{3,15},{4,24},{5,25},{6,26},{7,27},{8,20},{9,... | collective-permute-start | bytes 24584 | tf_op jit(solution)/shard_map/ppermute | solution.py:748

commit v5 on v4

--- a/solution.py
+++ b/solution.py
@@ -32,6 +32,8 @@
 PAIR = 2 * CH
 SHORT = 160
 UNITS = 11
+EARLY = range(1, 6)
+LATE = [u for u in range(UNITS) if u not in EARLY]
 LAST = [(3, 0), (4, 64), (5, 96)]
 EDGE = 32
 PLACE = [(0, 0), (3, 0), (3, 384), (5, 0), (5, 128), (5, 256)]
@@ -245,10 +247,72 @@
     return hi, mid, (rest - mid.astype(F32)).astype(BF16)
 
 
+def laplace(x, centre, spread):
+    y = 1.0 / spread
+    off = x - centre
+    mag = jnp.abs(off)
+    inside = jnp.clip(off, -0.5, 0.5)
+    e1 = jnp.exp((inside - 0.5) * y)
+    e2 = jnp.exp((-0.5 - inside) * y)
+    poly = y * (1 - y * (1 / 2 - y * (1 / 6 - y * (1 / 24 - y * (1 / 120)))))
+    tail = jnp.where(y < 0.05, poly, 1.0 - e1 * e2)
+    beyond = mag >= 0.5
+    arg = jnp.where(beyond, 0.5 * tail, 1.0 - 0.5 * (e1 + e2))
+    extra = jnp.where(beyond, (mag - 0.5) * y, 0.0)
+    return (extra - jnp.log(arg)) * (1.0 / 0.6931471805599453)
+
+
+def price(raw, own, plain):
+    sigma = raw[8:16]
+    soft = jnp.maximum(sigma, 0.0) + jnp.log(1.0 + jnp.exp(-jnp.abs(sigma)))
+    anchor = plain > 0.0
+    centre = jnp.where(anchor, 0.0, raw[0:8])
+    return laplace(own, centre, jnp.where(anchor, plain, 0.1 + soft))
+
+
+def early_units(field, parity, scale, a1, a2, a3, out):
+    lane = lax.broadcasted_iota(I32, (8, W), 1)
+    row = lax.broadcasted_iota(I32, (8, W), 0)
+    plain = jnp.where(((row + lane + parity) & 1) == 0, scale, 0.0)
+    rows = field[...]
+    turned = [pltpu.roll(rows, (-j) % LANES, 1) if j else rows for j in range(-2, 3)]
+
+    def both(value):
+        hi, lo = split2(value)
+        return hi, lo
+
+    hidden = {}
+    for stage in range(len(EARLY) + 2):
+        if stage >= 2:
+            u = EARLY[stage - 2]
+            hi = jnp.concatenate([h for h, _ in hidden[u]], axis=0)
+            lo = jnp.concatenate([l for _, l in hidden[u]], axis=0)
+            raw = dot(a3[...], jnp.concatenate([hi, lo, hi], axis=0))
+            out[u - EARLY[0]] = price(raw, rows[8 * u + 12 : 8 * u + 20, 0:W], plain)
+        if 1 <= stage <= len(EARLY):
+            u = EARLY[stage - 1]
+            hi, lo = hidden[u]
+            hidden[u] = []
+            for k in range(4):
+                part = slice(PAIR * k, PAIR * k + PAIR)
+                deep = jnp.concatenate([hi[part], lo[part], hi[part]], axis=0)
+                hidden[u].append(both(jnp.maximum(dot(a2[...], deep), 0.0)))
+        if stage < len(EARLY):
+            u = EARLY[stage]
+            shifted = [t[8 * u + 8 : 8 * u + 24, 0:W] for t in turned]
+            hi, lo = split2(jnp.concatenate(shifted, axis=0))
+            inner = dot(a1[...], jnp.concatenate([hi, lo, hi], axis=0))
+            hidden[u] = both(jnp.maximum(inner, 0.0))
+
+
 def conv_weights_kernel(
-    copies, cf, cs, co, spread, place, tap, tap_out, wc1, wc2, wout
+    copies, parity, scale, q0, side_near, side_far, a1, a2, a3, cf, cs, co, spread, place, tap,
+    tap_out, wc1, wc2, wout, early, field,
 ):
-    settle(copies)
+    field[...] = q0[...]
+    left, right = ordered("lon", side_near, side_far)
+    for g in range(H // 8):
+        field[TOP + 8 * g : TOP + 8 * g + 8, W:] = side_tile(left, right, 0, g)
     grow = spread[0:HALF, :]
     short = place[:, 0:SHORT]
     taps = tap[0:HALF, 0:SHORT].astype(F32)
@@ -269,6 +333,8 @@
                 total = jnp.where(taps3 == float(a), line, total)
             at = 24 * b + 8 * o
             wout[at : at + 8, :] = total
+    settle(copies)
+    early_units(field, parity[0], scale[0], a1, a2, a3, early)
 
 
 def mix_weights_kernel(
@@ -311,24 +377,9 @@
     a3[...] = jnp.concatenate([h, h, l], axis=1)
 
 
-def laplace(x, centre, spread):
-    y = 1.0 / spread
-    off = x - centre
-    mag = jnp.abs(off)
-    inside = jnp.clip(off, -0.5, 0.5)
-    e1 = jnp.exp((inside - 0.5) * y)
-    e2 = jnp.exp((-0.5 - inside) * y)
-    poly = y * (1 - y * (1 / 2 - y * (1 / 6 - y * (1 / 24 - y * (1 / 120)))))
-    tail = jnp.where(y < 0.05, poly, 1.0 - e1 * e2)
-    beyond = mag >= 0.5
-    arg = jnp.where(beyond, 0.5 * tail, 1.0 - 0.5 * (e1 + e2))
-    extra = jnp.where(beyond, (mag - 0.5) * y, 0.0)
-    return (extra - jnp.log(arg)) * (1.0 / 0.6931471805599453)
-
-
 def main_kernel(
     copies, parity, scale, q0, q1, q2, q3, q4, q5, side_near, side_far, end_near, end_far, target,
-    wm1, wm2, wc1, wc2, wout, a1, a2, a3, r1, r2, r3, r4, r5, u1, u2, u3, u4, u5,
+    wm1, wm2, wc1, wc2, wout, a1, a2, a3, early, r1, r2, r3, r4, r5, u1, u2, u3, u4, u5,
     recon_out, bits_out, part,
     recon, bits, sems, f0, f1, f2, f3, f4, f5, up, second, third, taps, hidden1, hidden2, own, anchors, moved, sq,
     *, pixels, lat,
@@ -378,7 +429,8 @@
         own[u] = shifted[2][4:12]
 
     for n in range(8):
-        unit(n, [turn(0, n, j) for j in range(-2, 3)])
+        if n not in EARLY:
+            unit(n, [turn(0, n, j) for j in range(-2, 3)])
     for n in range(2):
         unit(8 + n, [
             jnp.concatenate([turn(1, 2 * n, j), turn(1, 2 * n + 1, j)], axis=1)
@@ -489,24 +541,16 @@
     def cost(u):
         hi, lo = hidden2[u, 0:BLOCK, :], hidden2[u, BLOCK : 2 * BLOCK, :]
         raw = dot(a3[...], jnp.concatenate([hi, lo, hi], axis=0))
-        sigma = raw[8:16]
-        soft = jnp.maximum(sigma, 0.0) + jnp.log(1.0 + jnp.exp(-jnp.abs(sigma)))
-        plain = anchors[u]
-        anchor = plain > 0.0
-        centre = jnp.where(anchor, 0.0, raw[0:8])
-        own[u] = laplace(own[u], centre, jnp.where(anchor, plain, 0.1 + soft))
+        own[u] = price(raw, own[u], anchors[u])
 
     def run(synth, entropy):
-        def body(t):
-            for k in range(4):
-                if k < 3:
-                    synth(3 * t + k)
-                if 4 * t + k < UNITS:
-                    entropy(4 * t + k)
-            return 0
-
-        for t in range(3):
-            body(t)
+        done = 0
+        for n in range(BLOCKS):
+            synth(n)
+            until = (n + 1) * len(LATE) // BLOCKS
+            for u in LATE[done:until]:
+                entropy(u)
+            done = until
 
     run(mix, lambda u: layer(taps, hidden1, a1, u, 80))
     clear(second)
@@ -515,8 +559,11 @@
     run(conv_two, cost)
     clear(second)
 
+    finest = jnp.zeros((8, W), F32)
     for n in range(8):
-        bits[8 * n : 8 * n + 8, :] = own[n]
+        value = early[n - EARLY[0]] if n in EARLY else own[n]
+        bits[8 * n : 8 * n + 8, :] = value
+        finest = finest + value
 
     def output(n):
         slab = second[1, BLOCK * n + 96 : BLOCK * n + 96 + SLAB, :]
@@ -551,8 +598,7 @@
     send_recon = pltpu.make_async_copy(recon, recon_out, sems.at[1])
     send_recon.start()
     sums = [jnp.zeros((8, W), F32)] * 2
-    for n in range(8):
-        sums[0] = sums[0] + own[n]
+    sums[0] = finest
     sums[1] = own[8] + own[9]
     sums.append(own[10, :, 0:128] + own[10, :, 128:256])
     for level, at in LAST:
@@ -562,14 +608,24 @@
     total = jnp.zeros((72, SLAB), F32)
     for r in range(8):
         total = total + jnp.where(row == r, pltpu.roll(g, (-CH * r) % SLAB, 1), 0.0)
-    part[...] = jnp.zeros(part.shape, F32)
-    for k in range(9):
-        part[k : k + 1, :] = jnp.sum(total[8 * k : 8 * k + 8, 0:128], axis=0, keepdims=True)
+    lane = lax.broadcasted_iota(I32, (1, 128), 1)
+    rows = [
+        jnp.where(
+            (lane >= 8) & (lane < 8 + 3 * CH),
+            jnp.sum(total[8 * k : 8 * k + 8, 0:128], axis=0, keepdims=True),
+            0.0,
+        )
+        for k in range(9)
+    ]
     lane = lax.broadcasted_iota(I32, (1, 128), 1)
     line = jnp.where(lane == 0, jnp.sum(sq[...]), 0.0)
     for level in range(LEVELS):
         line = jnp.where(lane == 1 + level, jnp.sum(sums[level]), line)
-    part[9:10, :] = line
+    rows[0] = rows[0] + jnp.where(lane >= 80, pltpu.roll(rows[8], 72, 1), 0.0)
+    rows[1] = rows[1] + jnp.where((lane >= 80) & (lane < 104), pltpu.roll(rows[8], 24, 1), 0.0)
+    rows[2] = rows[2] + jnp.where(lane >= 80, pltpu.roll(line, 80, 1), 0.0)
+    for k in range(8):
+        part[k : k + 1, :] = rows[k]
     send_bits.wait()
     send_recon.wait()
 
@@ -580,7 +636,12 @@
     size = jnp.full((1, 7), sizes[0], F32)
     for k in range(1, 7):
         size = jnp.where(lane == k, sizes[k], size)
-    loss[...] = total[9:10, 0:7] / size
+    loss[...] = pltpu.roll(total, 128 - 80, 1)[2:3, 0:7] / size
+    wide = lax.broadcasted_iota(I32, (1, 128), 1)
+    ninth = jnp.where(
+        wide < 56, pltpu.roll(total, 128 - 72, 1)[0:1], pltpu.roll(total, 128 - 24, 1)[1:2]
+    )
+    total = jnp.concatenate([total, jnp.broadcast_to(ninth, (8, 128))], axis=0)
     for a in range(3):
         turned = pltpu.roll(total, 128 - 8 - CH * a, 1)
         for b in range(3):
@@ -716,10 +777,15 @@
     other = [(i, i + 1 if i & 1 else i - 1) for i in range(1, lat - 1)]
     end_far = lax.ppermute(end_far, "lat", other)
     end_near = lax.ppermute(end_near, "lat", pair)
-    wc1, wc2, wout = call(
+    wc1, wc2, wout, early = call(
         conv_weights_kernel,
-        (sds((HALF, 3 * SHORT), BF16), sds((HALF, 3 * SHORT), BF16), sds((72, SLAB), F32)),
-        [], [VMEM] * (3 + len(second)), 4, *params[5:], *[held[n] for n in second],
+        (
+            sds((HALF, 3 * SHORT), BF16), sds((HALF, 3 * SHORT), BF16), sds((72, SLAB), F32),
+            sds((len(EARLY), 8, W), F32),
+        ),
+        [pltpu.VMEM((TALL[0], LANES), F32)],
+        [SCALARS] * 2 + [VMEM] * (9 + len(second)), 16, anchor_parity, anchor_scale, quantized[0],
+        side_near, side_far, a1, a2, a3, *params[5:], *[held[n] for n in second],
     )
 
     pixels = float(3 * H * W * lat * lon)
@@ -729,16 +795,16 @@
     fields = [pltpu.VMEM((TALL[l], WIDE[l]), F32) for l in range(LEVELS)]
     recon, bits, part = call(
         functools.partial(main_kernel, pixels=pixels, lat=lat),
-        (sds((3, H, W), F32), sds((H, W), F32), sds((16, 128), F32)),
+        (sds((3, H, W), F32), sds((H, W), F32), sds((8, 128), F32)),
         [pltpu.VMEM((3, H, W), F32), pltpu.VMEM((H, W), F32), pltpu.SemaphoreType.DMA((2,))]
         + fields
         + [pltpu.VMEM((48 * BLOCKS, LANES), F32), feature, feature]
         + [pltpu.VMEM((UNITS + 1, 160, W), BF16), hidden, hidden, plain, plain]
         + [pltpu.VMEM((8, 80, LANES), BF16), pltpu.VMEM((8, W), F32)],
-        [SCALARS] * 2 + [VMEM] * 10 + [HBM] + [VMEM] * 18,
+        [SCALARS] * 2 + [VMEM] * 10 + [HBM] + [VMEM] * 19,
         40,
         anchor_parity, anchor_scale, *quantized, side_near, side_far, end_near, end_far, target,
-        wm1, wm2, wc1, wc2, wout, a1, a2, a3,
+        wm1, wm2, wc1, wc2, wout, a1, a2, a3, early,
         *scales,
         out_specs=(HBM, HBM, VMEM),
     )

time: 68 us -> 66.8 us (0.982)
  waiting for transfers between devices: 32.1 us -> 28.8 us
  Pallas kernels: 17.7 us -> 19.2 us
    ppermute x1, waiting for transfers between devices: 2.33 us -> 0.01 us  [local(): end_far = lax.ppermute(end_far, 'lat', other)]
    pallas_call x6, Pallas kernels: 17.7 us -> 19.2 us  [call(): pl.pallas_call(body, out_shape=outs, in_specs=specs, out_specs=out_specs...]
  transfers between devices with their start and end apart: 12 -> 12, of which waited for: 10 -> 9; matrix products, arithmetic and copies ran while one was open for 0% -> 0% of each run, Pallas kernels for 3% -> 7%
where the time goes in v5:
time: 66.8 us; the launch traced here: 66.7 us
  waiting for transfers between devices  28.8 us (43%)
  Pallas kernels  19.2 us (29%)
  starting transfers between devices  17.1 us (26%)
  between operations  1.54 us (2%)
    ppermute x7, waiting for transfers between devices, local(): part = part + lax.ppermute(part, ('lat', 'lon'), step)  24.5 us
    pallas_call x6, Pallas kernels, call(): pl.pallas_call(body, out_shape=outs, in_specs=specs, out_specs=out_specs...  19.2 us
    ppermute x1, starting transfers between devices, local(): side_far = lax.ppermute(side_far, 'lon', other)  6.97 us
    ppermute x1, starting transfers between devices, local(): end_far = lax.ppermute(end_far, 'lat', other)  5.37 us
    ppermute x1, waiting for transfers between devices, local(): other = lax.ppermute(part, ('lat', 'lon'), steps[-1])  3.65 us
    ppermute x7, starting transfers between devices, local(): part = part + lax.ppermute(part, ('lat', 'lon'), step)  2 us
    ppermute x1, starting transfers between devices, local(): other = lax.ppermute(part, ('lat', 'lon'), steps[-1])  1.75 us
  transfers between devices with their start and end apart: 12, of which 9 were waited for; matrix products, arithmetic and copies ran while one was open for 0% of the time, Pallas kernels for 7%

profile of v5, /device:TPU:6, one launch (start us, length us, event | category | flops | bytes accessed | tf_op | source)
XLA Modules:
  0.0 66.7 jit_solution(1233732424451962136)
XLA Ops:
  1.3 1.5 %shard_map.291 = (f32[8,128]{1,0:T(8,128)S(1)}, f32[8,128]{1,0:T(8,128)S(1)}, f32[80,640]{1,0:T(8,128)S(1)}, f32[56,384]{1,0:T(8,128)S(1)}, f32[40,256]{1,0:T(8,...) custom-call(s32[1,1]{1,0:T(1,128)S(6)} %copy.32.refs_0_, ...), custom_call_target="tpu_custom_call" | custom-call | tf_op jit(solution)/shard_map/pallas_call | solution.py:720
  2.8 0.1 collective-permute-start
  2.9 7.0 %collective-permute-start.1 = (f32[8,128]{1,0:T(8,128)S(1)}, f32[8,128]{1,0:T(8,128)S(1)}, u32[]{:S(2)}, u32[]{:S(2)}) collective-permute-start(f32[8,128]{1,0:T(8,128)S(1)} %get-tuple-element.64), channel_id=1, source_target_pairs={{0,31},{1,2},{2,1},{3,4},{4,3},{5,6},{6,5},{7,8},{8,7},{9,10},{10,... | collective-permute-start | bytes 12296 | tf_op jit(solution)/shard_map/ppermute | solution.py:762
  9.9 0.7 %shard_map.292 = (f32[8,128]{1,0:T(8,128)S(1)}, bf16[192,48]{1,0:T(8,128)(2,1)S(1)}, bf16[192,192]{1,0:T(8,128)(2,1)S(1)}, bf16[192,240]{1,0:T(8,128)(2,1)S(1)},...) custom-call(bf16[6,24]{1,0:T(8,128)(2,1)S(1)} %get-tuple-element.65.refs_0_, ...), custom_call_target="tpu_custom_call" | custom-call | tf_op jit(solution)/shard_map/pallas_call | solution.py:720
  10.6 0.6 collective-permute-done.1.refs_7_.refs_4_.refs_9_
  11.2 0.1 shard_map.293
  11.3 0.9 %collective-permute-start.2 = (f32[8,640]{1,0:T(8,128)S(1)}, f32[8,640]{1,0:T(8,128)S(1)}, u32[]{:S(2)}, u32[]{:S(2)}) collective-permute-start(f32[8,640]{1,0:T(8,128)S(1)} %get-tuple-element.78), channel_id=1, source_target_pairs={{0,32},{32,0},{64,96},{96,64},{128,160},{160,128},{192,224},{224,1... | collective-permute-start | bytes 61448 | tf_op jit(solution)/shard_map/ppermute | solution.py:779
  12.3 5.4 %collective-permute-start.3 = (f32[8,640]{1,0:T(8,128)S(1)}, f32[8,640]{1,0:T(8,128)S(1)}, u32[]{:S(2)}, u32[]{:S(2)}) collective-permute-start(f32[8,640]{1,0:T(8,128)S(1)} %get-tuple-element.79), channel_id=1, source_target_pairs={{32,64},{64,32},{96,128},{128,96},{160,192},{192,160},{33,65},{65,... | collective-permute-start | bytes 61448 | tf_op jit(solution)/shard_map/ppermute | solution.py:778
  17.6 4.1 %shard_map.294 = (bf16[96,480]{1,0:T(8,128)(2,1)S(1)}, bf16[96,480]{1,0:T(8,128)(2,1)S(1)}, f32[72,256]{1,0:T(8,128)S(1)}, f32[5,8,512]{2,1,0:T(8,128)S(1)}) custom-call(s32[6]{0:T(128)} %refs_0_.4, f32[6]{0:T(128)} %refs_1_.5, f32[80,640]{1,0:T(8,128)S(1)} %get-tuple-element.57.refs_0_.refs_2_, f32[8,128]{1,0:T(8,128)S(1)} %collective-permute-done.refs_6_.refs_3_.refs_8_, ...), custom_call_target="tpu_custom_call" | custom-call | tf_op jit(solution)/shard_map/pallas_call | solution.py:720
  21.8 0.0 collective-permute-done.2.refs_10_
  21.8 0.0 collective-permute-done.3.refs_11_
  21.8 12.0 %shard_map.295 = (f32[3,64,512]{2,1,0:T(8,128)}, f32[64,512]{1,0:T(8,128)}, f32[8,128]{1,0:T(8,128)S(1)}) custom-call(s32[6]{0:T(128)} %refs_0_.4, f32[6]{0:T(128)} %refs_1_.5, f32[80,640]{1,0:T(8,128)S(1)} %get-tuple-element.57.refs_0_.refs_2_, f32[56,384]{1,0:T(8,128)S(1)} %get-tuple-element.58.refs_1_.refs_3_, ...), custom_call_target="tpu_custom_call" | custom-call | tf_op jit(solution)/shard_map/pallas_call | solution.py:720
  33.8 0.1 collective-permute-start.4
  33.9 1.2 %collective-permute-done.4 = f32[8,128]{1,0:T(8,128)S(1)} collective-permute-done((f32[8,128]{1,0:T(8,128)S(1)}, f32[8,128]{1,0:T(8,128)S(1)}, u32[]{:S(2)}, u32[]{:S(2)}) %collective-permute-start.4) | collective-permute-done | bytes 4128 | tf_op jit(solution)/shard_map/ppermute | solution.py:813
  35.1 3.6 %collective-permute-done.5 = f32[8,128]{1,0:T(8,128)S(1)} collective-permute-done((f32[8,128]{1,0:T(8,128)S(1)}, f32[8,128]{1,0:T(8,128)S(1)}, u32[]{:S(2)}, u32[]{:S(2)}) %collective-permute-start.5) | collective-permute-done | bytes 4128 | tf_op jit(solution)/shard_map/ppermute | solution.py:813
  38.7 4.8 %collective-permute-done.6 = f32[8,128]{1,0:T(8,128)S(1)} collective-permute-done((f32[8,128]{1,0:T(8,128)S(1)}, f32[8,128]{1,0:T(8,128)S(1)}, u32[]{:S(2)}, u32[]{:S(2)}) %collective-permute-start.6) | collective-permute-done | bytes 4128 | tf_op jit(solution)/shard_map/ppermute | solution.py:813
  43.5 3.6 %collective-permute-done.7 = f32[8,128]{1,0:T(8,128)S(1)} collective-permute-done((f32[8,128]{1,0:T(8,128)S(1)}, f32[8,128]{1,0:T(8,128)S(1)}, u32[]{:S(2)}, u32[]{:S(2)}) %collective-permute-start.7) | collective-permute-done | bytes 4128 | tf_op jit(solution)/shard_map/ppermute | solution.py:813
  47.1 4.8 %collective-permute-done.8 = f32[8,128]{1,0:T(8,128)S(1)} collective-permute-done((f32[8,128]{1,0:T(8,128)S(1)}, f32[8,128]{1,0:T(8,128)S(1)}, u32[]{:S(2)}, u32[]{:S(2)}) %collective-permute-start.8) | collective-permute-done | bytes 4128 | tf_op jit(solution)/shard_map/ppermute | solution.py:813
  51.9 3.6 %collective-permute-done.9 = f32[8,128]{1,0:T(8,128)S(1)} collective-permute-done((f32[8,128]{1,0:T(8,128)S(1)}, f32[8,128]{1,0:T(8,128)S(1)}, u32[]{:S(2)}, u32[]{:S(2)}) %collective-permute-start.9) | collective-permute-done | bytes 4128 | tf_op jit(solution)/shard_map/ppermute | solution.py:813
  55.5 1.9 %collective-permute-start.10 = (f32[8,128]{1,0:T(8,128)S(1)}, f32[8,128]{1,0:T(8,128)S(1)}, u32[]{:S(2)}, u32[]{:S(2)}) collective-permute-start(f32[8,128]{1,0:T(8,128)S(1)} %add.26), channel_id=1, source_target_pairs={{0,28},{1,29},{2,30},{3,31},{4,8},{5,9},{6,10},{7,11},{8,4},{9,5},... | collective-permute-start | bytes 12296 | tf_op jit(solution)/shard_map/ppermute | solution.py:813
  57.4 2.9 %collective-permute-done.10 = f32[8,128]{1,0:T(8,128)S(1)} collective-permute-done((f32[8,128]{1,0:T(8,128)S(1)}, f32[8,128]{1,0:T(8,128)S(1)}, u32[]{:S(2)}, u32[]{:S(2)}) %collective-permute-start.10) | collective-permute-done | bytes 4128 | tf_op jit(solution)/shard_map/ppermute | solution.py:813
  60.4 1.8 %collective-permute-start.11 = (f32[8,128]{1,0:T(8,128)S(1)}, f32[8,128]{1,0:T(8,128)S(1)}, u32[]{:S(2)}, u32[]{:S(2)}) collective-permute-start(f32[8,128]{1,0:T(8,128)S(1)} %add.27.refs_0_), channel_id=1, source_target_pairs={{0,12},{1,13},{2,14},{3,15},{4,24},{5,25},{6,26},{7,27},{8,20},{9,... | collective-permute-start | bytes 12296 | tf_op jit(solution)/shard_map/ppermute | solution.py:814
  62.1 3.6 %collective-permute-done.11.refs_1_ = f32[8,128]{1,0:T(8,128)S(1)} collective-permute-done((f32[8,128]{1,0:T(8,128)S(1)}, f32[8,128]{1,0:T(8,128)S(1)}, u32[]{:S(2)}, u32[]{:S(2)}) %collective-permute-start.11) | collective-permute-done | bytes 4128 | tf_op jit(solution)/shard_map/ppermute | solution.py:814
  65.8 0.8 %shard_map.296 = (f32[1,7]{1,0:T(1,128)}, f32[3,3,3,24]{3,2,1,0:T(4,128)}) custom-call(f32[8,128]{1,0:T(8,128)S(1)} %add.27.refs_0_, f32[8,128]{1,0:T(8,128)S(1)} %collective-permute-done.11.refs_1_), custom_call_target="tpu_custom_call" | custom-call | tf_op jit(solution)/shard_map/pallas_call | solution.py:720
  (13 shorter events, 0.0 us)
Async XLA Ops:
  2.8 7.8 %collective-permute-start = (f32[8,128]{1,0:T(8,128)S(1)}, f32[8,128]{1,0:T(8,128)S(1)}, u32[]{:S(2)}, u32[]{:S(2)}) collective-permute-start(f32[8,128]{1,0:T(8,128)S(1)} %get-tuple-element.63), channel_id=1, source_target_pairs={{0,1},{1,0},{2,3},{3,2},{4,5},{5,4},{6,7},{7,6},{8,9},{9,8},{10,11... | collective-permute-start | bytes 12296 | tf_op jit(solution)/shard_map/ppermute | solution.py:763
  2.9 8.3 %collective-permute-start.1 = (f32[8,128]{1,0:T(8,128)S(1)}, f32[8,128]{1,0:T(8,128)S(1)}, u32[]{:S(2)}, u32[]{:S(2)}) collective-permute-start(f32[8,128]{1,0:T(8,128)S(1)} %get-tuple-element.64), channel_id=1, source_target_pairs={{0,31},{1,2},{2,1},{3,4},{4,3},{5,6},{6,5},{7,8},{8,7},{9,10},{10,... | collective-permute-start | bytes 12296 | tf_op jit(solution)/shard_map/ppermute | solution.py:762
  11.3 10.4 %collective-permute-start.2 = (f32[8,640]{1,0:T(8,128)S(1)}, f32[8,640]{1,0:T(8,128)S(1)}, u32[]{:S(2)}, u32[]{:S(2)}) collective-permute-start(f32[8,640]{1,0:T(8,128)S(1)} %get-tuple-element.78), channel_id=1, source_target_pairs={{0,32},{32,0},{64,96},{96,64},{128,160},{160,128},{192,224},{224,1... | collective-permute-start | bytes 61448 | tf_op jit(solution)/shard_map/ppermute | solution.py:779
  12.3 9.5 %collective-permute-start.3 = (f32[8,640]{1,0:T(8,128)S(1)}, f32[8,640]{1,0:T(8,128)S(1)}, u32[]{:S(2)}, u32[]{:S(2)}) collective-permute-start(f32[8,640]{1,0:T(8,128)S(1)} %get-tuple-element.79), channel_id=1, source_target_pairs={{32,64},{64,32},{96,128},{128,96},{160,192},{192,160},{33,65},{65,... | collective-permute-start | bytes 61448 | tf_op jit(solution)/shard_map/ppermute | solution.py:778
  33.8 1.3 %collective-permute-start.4 = (f32[8,128]{1,0:T(8,128)S(1)}, f32[8,128]{1,0:T(8,128)S(1)}, u32[]{:S(2)}, u32[]{:S(2)}) collective-permute-start(f32[8,128]{1,0:T(8,128)S(1)} %get-tuple-element.107), channel_id=1, source_target_pairs={{0,1},{1,0},{2,3},{3,2},{4,5},{5,4},{6,7},{7,6},{8,9},{9,8},{10,11... | collective-permute-start | bytes 12296 | tf_op jit(solution)/shard_map/ppermute | solution.py:813
  35.1 3.6 %collective-permute-start.5 = (f32[8,128]{1,0:T(8,128)S(1)}, f32[8,128]{1,0:T(8,128)S(1)}, u32[]{:S(2)}, u32[]{:S(2)}) collective-permute-start(f32[8,128]{1,0:T(8,128)S(1)} %add.21), channel_id=1, source_target_pairs={{0,32},{1,33},{2,34},{3,35},{4,36},{5,37},{6,38},{7,39},{8,40},{9,... | collective-permute-start | bytes 12296 | tf_op jit(solution)/shard_map/ppermute | solution.py:813
  38.7 4.8 %collective-permute-start.6 = (f32[8,128]{1,0:T(8,128)S(1)}, f32[8,128]{1,0:T(8,128)S(1)}, u32[]{:S(2)}, u32[]{:S(2)}) collective-permute-start(f32[8,128]{1,0:T(8,128)S(1)} %add.22), channel_id=1, source_target_pairs={{0,96},{1,97},{2,98},{3,99},{4,100},{5,101},{6,102},{7,103},{8,104... | collective-permute-start | bytes 12296 | tf_op jit(solution)/shard_map/ppermute | solution.py:813
  43.5 3.6 %collective-permute-start.7 = (f32[8,128]{1,0:T(8,128)S(1)}, f32[8,128]{1,0:T(8,128)S(1)}, u32[]{:S(2)}, u32[]{:S(2)}) collective-permute-start(f32[8,128]{1,0:T(8,128)S(1)} %add.23), channel_id=1, source_target_pairs={{0,2},{1,3},{2,0},{3,1},{4,6},{5,7},{6,4},{7,5},{8,10},{9,11},{10,... | collective-permute-start | bytes 12296 | tf_op jit(solution)/shard_map/ppermute | solution.py:813
  47.1 4.8 %collective-permute-start.8 = (f32[8,128]{1,0:T(8,128)S(1)}, f32[8,128]{1,0:T(8,128)S(1)}, u32[]{:S(2)}, u32[]{:S(2)}) collective-permute-start(f32[8,128]{1,0:T(8,128)S(1)} %add.24), channel_id=1, source_target_pairs={{0,130},{1,131},{2,128},{3,129},{4,134},{5,135},{6,132},{7,133},{8... | collective-permute-start | bytes 12296 | tf_op jit(solution)/shard_map/ppermute | solution.py:813
  51.9 3.6 %collective-permute-start.9 = (f32[8,128]{1,0:T(8,128)S(1)}, f32[8,128]{1,0:T(8,128)S(1)}, u32[]{:S(2)}, u32[]{:S(2)}) collective-permute-start(f32[8,128]{1,0:T(8,128)S(1)} %add.25), channel_id=1, source_target_pairs={{0,4},{1,5},{2,6},{3,7},{4,0},{5,1},{6,2},{7,3},{8,12},{9,13},{10,... | collective-permute-start | bytes 12296 | tf_op jit(solution)/shard_map/ppermute | solution.py:813
  55.5 4.8 %collective-permute-start.10 = (f32[8,128]{1,0:T(8,128)S(1)}, f32[8,128]{1,0:T(8,128)S(1)}, u32[]{:S(2)}, u32[]{:S(2)}) collective-permute-start(f32[8,128]{1,0:T(8,128)S(1)} %add.26), channel_id=1, source_target_pairs={{0,28},{1,29},{2,30},{3,31},{4,8},{5,9},{6,10},{7,11},{8,4},{9,5},... | collective-permute-start | bytes 12296 | tf_op jit(solution)/shard_map/ppermute | solution.py:813
  60.4 5.4 %collective-permute-start.11 = (f32[8,128]{1,0:T(8,128)S(1)}, f32[8,128]{1,0:T(8,128)S(1)}, u32[]{:S(2)}, u32[]{:S(2)}) collective-permute-start(f32[8,128]{1,0:T(8,128)S(1)} %add.27.refs_0_), channel_id=1, source_target_pairs={{0,12},{1,13},{2,14},{3,15},{4,24},{5,25},{6,26},{7,27},{8,20},{9,... | collective-permute-start | bytes 12296 | tf_op jit(solution)/shard_map/ppermute | solution.py:814
